TPU v7x, 256 devices: a whole 4x4x8 slice. The times are simulated.
256 devices in a mesh: grp: 8 (over z_hi, y), sp: 32 (over z_lo, x, core).
Axes of the slice: x: 4, y: 4, z: 8 (z_hi: 2, z_lo: 4; z = z_hi * 4 + z_lo), core: 2. Of those that a mesh axis runs over, the one named last changes fastest.
Arguments:
- alpha: float32 [80, 32, 4096], P('grp', None, 'sp'), may hold values from -6 to 6
- ensemble: bfloat16 [80, 3, 32, 4096], P('grp', None, None, 'sp'), may hold values from -6 to 6
- static_std: float32 [3, 32, 4096], P(None, 'grp', 'sp'), may hold values from 0.2 to 1
- control: float32 [3, 32, 4096], P(None, 'grp', 'sp'), may hold values from -6 to 6
- loc_spectrum: float32 [1024], replicated, may hold values from 0.00024414062 to 0.001953125
- obs_cell: int32 [262144], P(('grp', 'sp')), may hold values from 0 to 131071, as said below
- obs_step: int32 [262144], P(('grp', 'sp')), may hold values from 0 to 2
- innovation: float32 [262144], P(('grp', 'sp')), may hold values from -6 to 6
- obs_weight: float32 [262144], P(('grp', 'sp')), may hold values from 0.5 to 4
Outputs:
- grad_alpha: float32 [80, 32, 4096], P('grp', None, 'sp')
- grad_control: float32 [3, 32, 4096], P(None, 'grp', 'sp')
Inputs may be any that keep to these rules, and one draw needn't show every extreme that they name: `obs_cell`: an entry is row * 4096 + column. Entries 1024 * b to 1024 * (b + 1) - 1 lie in the tile of 4 rows from row 4 * (b // 32) and 128 columns from column 128 * (b % 32).
All inputs are finite; a program needn't handle non-finite values.
Results may differ from a plain program's by a relative error of at most 0.0075.
Values may be sent and summed in bfloat16 or wider, within the bound.
No kernel may reach another device: no remote copies, remote signals or barrier semaphores. Data moves between devices by JAX's collectives and lax.ppermute only.
A program may use at most 128 MiB of HBM per device.

v0:
```python
import math

import jax
import jax.numpy as jnp
from jax import lax
from jax.sharding import Mesh
from jax.sharding import PartitionSpec as P

NX = 4096
GRP_SP = ("grp", "sp_0", "sp_1", "sp_2")
SP = ("sp_0", "sp_1", "sp_2")


courant = 0.4


def extended(block, sides, width):
    for axis, dim in sides:
        count = lax.axis_size(axis)
        forward = [(i, i + 1) for i in range(count - 1)]
        forward.append((count - 1, 0))
        backward = [(target, source) for source, target in forward]
        low = lax.ppermute(
            lax.slice_in_dim(block, block.shape[dim] - width, None, axis=dim), axis, forward
        )
        high = lax.ppermute(lax.slice_in_dim(block, 0, width, axis=dim), axis, backward)
        block = jnp.concatenate([low, block, high], axis=dim)
    return block


def in_blocks(x, dim, length):
    shape = x.shape
    tiles = x.reshape(*shape[:dim], length, shape[dim] // length, *shape[dim + 1 :])
    return jnp.moveaxis(tiles, dim, 0)


def sum_at_owner(x, axis, dim):
    tiles = in_blocks(x, dim, lax.axis_size(axis))
    arrived = lax.all_to_all(tiles, axis, split_axis=0, concat_axis=0, tiled=True)
    return arrived.sum(axis=0)


def in_order(tiles, dim):
    tiles = jnp.moveaxis(tiles, 0, dim)
    shape = tiles.shape
    return tiles.reshape(*shape[:dim], shape[dim] * shape[dim + 1], *shape[dim + 2 :])


def copy_for_each(x, axis):
    copies = jnp.broadcast_to(x, (lax.axis_size(axis), *x.shape))
    return lax.all_to_all(copies, axis, split_axis=0, concat_axis=0, tiled=True)


def gathered_copies(x, axis, dim):
    return in_order(copy_for_each(x, axis), dim)


def moved_by_axis(tiles, axes, turns):
    shape = [lax.axis_size(a) for a in axes]
    tiles = tiles.reshape(*shape, *tiles.shape[1:])
    for k in turns:
        tiles = lax.all_to_all(tiles, axes[k], split_axis=k, concat_axis=k, tiled=True)
    return tiles.reshape(-1, *tiles.shape[len(axes) :])


def core_and_chips(x, groups, turns, split_dim, concat_dim):
    length = lax.axis_size(groups[0]) * lax.axis_size(groups[1])
    tiles = in_blocks(x, split_dim, length)
    return in_order(moved_by_axis(tiles, groups, turns), concat_dim)


def spectral_filter(rows_data, loc_spectrum):
    length_x = rows_data.shape[1]
    kept_waves = loc_spectrum.shape[0]
    freq_block = math.gcd(kept_waves, 256)
    positions = jnp.arange(length_x, dtype=jnp.int32)
    filtered = jnp.zeros(rows_data.shape, jnp.float32)
    for start_wave in range(0, kept_waves, freq_block):
        waves = start_wave + jnp.arange(freq_block, dtype=jnp.int32)
        phases = positions[:, None] * waves[None, :] % length_x
        radians = 2.0 * math.pi / length_x * phases.astype(jnp.float32)
        fourier_basis = jnp.concatenate([jnp.cos(radians), jnp.sin(radians)], axis=1)
        weights = loc_spectrum[start_wave : start_wave + freq_block]
        weights = jnp.concatenate([weights, weights])
        coeffs = jnp.dot(
            rows_data,
            fourier_basis,
            precision=lax.Precision.HIGHEST,
            preferred_element_type=jnp.float32,
        )
        filtered = filtered + jnp.dot(
            coeffs * weights[None, :],
            fourier_basis.T,
            precision=lax.Precision.HIGHEST,
            preferred_element_type=jnp.float32,
        )
    return filtered


def inner(field):
    return field[..., 1:-1, 1:-1]


def diff_x(field):
    return 0.5 * (field[..., 1:-1, 2:] - field[..., 1:-1, :-2])


def diff_y(field):
    return 0.5 * (field[..., 2:, 1:-1] - field[..., :-2, 1:-1])


def clip_rows(stack, margin, first_row, total_rows):
    rows_index = first_row - margin + jnp.arange(stack.shape[1], dtype=jnp.int32)
    valid = jnp.logical_and(rows_index >= 0, rows_index < total_rows).astype(jnp.float32)
    return stack * valid[None, :, None]


def coriolis_rows(first_row, margin, count, total_rows):
    rows_index = first_row - margin + jnp.arange(count, dtype=jnp.int32)
    return (0.1 + 0.2 * (rows_index.astype(jnp.float32) + 0.5) / total_rows)[:, None]


def forward_a(stack, margin, first_row, total_rows):
    height, eastward, northward = (stack[0], stack[1], stack[2])
    new_height = inner(height) - courant * (diff_x(eastward) + diff_y(northward))
    result = jnp.stack([new_height, inner(eastward), inner(northward)])
    return clip_rows(result, margin - 1, first_row, total_rows)


def forward_b(stack, margin, first_row, total_rows):
    height, eastward, northward = (stack[0], stack[1], stack[2])
    rotation = coriolis_rows(first_row, margin - 1, stack.shape[1] - 2, total_rows)
    new_east = inner(eastward) - courant * diff_x(height) + rotation * inner(northward)
    new_north = inner(northward) - courant * diff_y(height) - rotation * inner(eastward)
    result = jnp.stack([inner(height), new_east, new_north])
    return clip_rows(result, margin - 1, first_row, total_rows)


def backward_a(stack, margin, first_row, total_rows):
    back_h, back_u, back_w = (stack[0], stack[1], stack[2])
    adj_height = inner(back_h) + courant * (diff_x(back_u) + diff_y(back_w))
    result = jnp.stack([adj_height, inner(back_u), inner(back_w)])
    return clip_rows(result, margin - 1, first_row, total_rows)


def backward_b(stack, margin, first_row, total_rows):
    adj_height, back_u, back_w = (stack[0], stack[1], stack[2])
    rotation = coriolis_rows(first_row, margin - 1, stack.shape[1] - 2, total_rows)
    adj_east = inner(back_u) - rotation * inner(back_w) + courant * diff_x(adj_height)
    adj_north = inner(back_w) + rotation * inner(back_u) + courant * diff_y(adj_height)
    result = jnp.stack([inner(adj_height), adj_east, adj_north])
    return clip_rows(result, margin - 1, first_row, total_rows)


def deep_rim(stack):
    return extended(stack, (("grp", 1), (SP, 2)), 4)


def per_device(
    alpha, ensemble, static_std, control, loc_spectrum, obs_cell, obs_step, innovation, obs_weight
):
    members_local = alpha.shape[0]
    groups = lax.axis_size("grp")
    spread = 1.0 / math.sqrt(members_local * groups - 1)
    tile_rows, tile_cols = (control.shape[1], control.shape[2])
    total_rows = tile_rows * groups
    first_row = lax.axis_index("grp") * tile_rows
    first_col = lax.axis_index(SP) * tile_cols

    def localize_items(items):
        dims = items.shape
        flat = items.reshape(dims[0] * dims[1], dims[2])
        return spectral_filter(flat, loc_spectrum).reshape(dims)

    def to_rows(columns):
        return localize_items(lax.all_to_all(columns, SP, split_axis=1, concat_axis=2, tiled=True))

    localized = lax.all_to_all(
        to_rows(alpha).astype(jnp.bfloat16), SP, split_axis=2, concat_axis=1, tiled=True
    )
    partial_value = jnp.einsum(
        "mvyx,myx->vyx", ensemble, localized, preferred_element_type=jnp.float32
    )
    summed = sum_at_owner(partial_value, "grp", 1)
    increment = static_std * control + spread * summed
    padded = clip_rows(deep_rim(increment), 4, first_row, total_rows)
    middle = forward_b(forward_a(padded, 4, first_row, total_rows), 3, first_row, total_rows)
    first_state = middle[:, 2:-2, 2:-2]
    second_state = forward_b(forward_a(middle, 2, first_row, total_rows), 1, first_row, total_rows)
    states = (increment, first_state, second_state)
    local_index = (obs_cell // NX - first_row) * tile_cols + (obs_cell % NX - first_col)
    observed = jnp.zeros(innovation.shape, jnp.float32)
    for moment in range(3):
        values = states[moment][0].reshape(-1)[local_index]
        observed = jnp.where(obs_step == moment, values, observed)
    misfit = obs_weight * (observed - innovation)
    forcings = []
    for moment in range(3):
        spread_obs = jnp.where(obs_step == moment, misfit, jnp.zeros_like(misfit))
        height_force = (
            jnp.zeros((tile_rows * tile_cols,), jnp.float32).at[local_index].add(spread_obs)
        )
        forcings.append(height_force.reshape(tile_rows, tile_cols))
    zero_field = jnp.zeros((tile_rows, tile_cols), jnp.float32)
    last_adjoint = jnp.stack([forcings[2], zero_field, zero_field])
    padded = clip_rows(
        deep_rim(jnp.concatenate([last_adjoint, forcings[1][None]], axis=0)),
        4,
        first_row,
        total_rows,
    )
    middle = backward_b(backward_a(padded[:3], 4, first_row, total_rows), 3, first_row, total_rows)
    middle = middle.at[0].add(padded[3, 2:-2, 2:-2])
    adjoint = backward_b(backward_a(middle, 2, first_row, total_rows), 1, first_row, total_rows)
    adjoint = adjoint.at[0].add(forcings[0])
    grad_control = control + static_std * adjoint
    half = adjoint.astype(jnp.bfloat16)
    weighted = jnp.einsum(
        "mvyx,vyx->myx",
        ensemble,
        gathered_copies(half, "grp", 1),
        preferred_element_type=jnp.float32,
    )
    filtered = core_and_chips(to_rows(weighted), (("sp_0", "sp_1"), "sp_2"), (1, 0), 2, 1)
    grad_alpha = alpha + spread * filtered
    return (grad_alpha, grad_control)


def solution(mesh):
    torus = Mesh(mesh.devices.reshape(mesh.shape["grp"], 4, 4, 2), ("grp", "sp_0", "sp_1", "sp_2"))
    placed = (
        P("grp", None, SP),
        P("grp", None, None, SP),
        P(None, "grp", SP),
        P(None, "grp", SP),
        P(),
        P(GRP_SP),
        P(GRP_SP),
        P(GRP_SP),
        P(GRP_SP),
    )
    return jax.shard_map(
        per_device,
        mesh=torus,
        in_specs=placed,
        out_specs=(P("grp", None, SP), P(None, "grp", SP)),
        check_vma=False,
    )
```

profile of v0, /device:TPU:1, one launch (start us, length us, event | category | flops | bytes accessed | tf_op | source)
XLA Modules:
  0.0 377.0 jit_solution(4057525190884514991)
XLA Ops:
  0.6 1.7 copy.25
  2.4 10.0 %all-to-all-start = ((f32[10,32,128]{2,0,1:T(8,128)}), f32[10,32,128]{2,0,1:T(8,128)S(1)}, u32[]{:S(2)}, u32[]{:S(2)}) async-start(f32[10,32,128]{2,0,1:T(8,128)} %copy.25), calls=%async_computation | async-start | bytes 524288 | tf_op jit(solution)/shard_map/all_to_all | solution.py:176
  12.4 17.6 %fusion.36 = (f32[4096,256]{1,0:T(8,128)}, f32[4096,256]{1,0:T(8,128)}) fusion(), kind=kLoop, calls=%fused_computation.64 | loop fusion | flops 14680064 | bytes 8388608 | tf_op jit(solution)/shard_map/sin | solution.py:82
  30.1 17.9 %fusion.43 = (f32[4096,256]{1,0:T(8,128)}, f32[4096,256]{1,0:T(8,128)}) fusion(s32[256]{0:T(256)S(1)} %iota_add_fusion.2), kind=kLoop, calls=%fused_computation.71 | loop fusion | flops 14680064 | bytes 8389632 | tf_op jit(solution)/shard_map/cos | solution.py:82
  47.9 17.9 %fusion.41 = (f32[4096,256]{1,0:T(8,128)}, f32[4096,256]{1,0:T(8,128)}) fusion(s32[256]{0:T(256)S(1)} %iota_add_fusion.1), kind=kLoop, calls=%fused_computation.69 | loop fusion | flops 14680064 | bytes 8389632 | tf_op jit(solution)/shard_map/cos | solution.py:82
  65.8 17.9 %fusion.39 = (f32[4096,256]{1,0:T(8,128)}, f32[4096,256]{1,0:T(8,128)}) fusion(s32[256]{0:T(256)S(1)} %iota_add_fusion), kind=kLoop, calls=%fused_computation.67 | loop fusion | flops 14680064 | bytes 8389632 | tf_op jit(solution)/shard_map/cos | solution.py:82
  83.9 0.2 copy.53
  84.1 7.5 %fusion.44 = f32[512,10]{0,1:T(8,128)S(1)} fusion(f32[10,4096]{1,0:T(8,128)S(1)} %bitcast.186, f32[4096,256]{1,0:T(8,128)} %get-tuple-element.102, f32[4096,256]{1,0:T(8,128)} %get-tuple-element.103, f32[512]{0:T(512)S(1)} %get-tuple-element.98), kind=kOutput, calls=%fused_computation.72 | convolution fusion | flops 253760512 | bytes 8574976 | tf_op jit(solution)/shard_map/dot_general | solution.py:85
  91.6 7.0 %fusion.34 = f32[10,4096]{1,0:T(8,128)S(1)} fusion(f32[512,10]{0,1:T(8,128)S(1)} %fusion.44, f32[4096,256]{1,0:T(8,128)S(1)} %copy-done, f32[4096,256]{1,0:T(8,128)S(1)} %copy-done.2), kind=kOutput, calls=%fused_computation.62 | convolution fusion | flops 253755392 | bytes 8572928 | tf_op jit(solution)/shard_map/dot_general | solution.py:91
  98.6 4.5 %fusion.46 = f32[512,10]{0,1:T(8,128)S(1)} fusion(f32[10,4096]{1,0:T(8,128)S(1)} %bitcast.187, f32[4096,256]{1,0:T(8,128)S(1)} %copy-done.14, f32[4096,256]{1,0:T(8,128)S(1)} %copy-done.12, f32[512]{0:T(512)S(1)} %get-tuple-element.99), kind=kOutput, calls=%fused_computation.74 | convolution fusion | flops 253760512 | bytes 8574976 | tf_op jit(solution)/shard_map/dot_general | solution.py:85
  103.1 7.2 %convolution_add_fusion.5 = f32[10,4096]{1,0:T(8,128)S(1)} fusion(f32[10,4096]{1,0:T(8,128)S(1)} %fusion.34, f32[512,10]{0,1:T(8,128)S(1)} %fusion.46, f32[4096,256]{1,0:T(8,128)S(1)} %copy-done.14, f32[4096,256]{1,0:T(8,128)S(1)} %copy-done.12), kind=kOutput, calls=%fused_computation.27 | convolution fusion | flops 253796352 | bytes 8736768 | tf_op jit(solution)/shard_map/dot_general | solution.py:91
  110.3 4.5 %fusion.48 = f32[512,10]{0,1:T(8,128)S(1)} fusion(f32[10,4096]{1,0:T(8,128)S(1)} %bitcast.188, f32[4096,256]{1,0:T(8,128)S(1)} %copy-done.10, f32[4096,256]{1,0:T(8,128)S(1)} %copy-done.8, f32[512]{0:T(512)S(1)} %get-tuple-element.100), kind=kOutput, calls=%fused_computation.76 | convolution fusion | flops 253760512 | bytes 8574976 | tf_op jit(solution)/shard_map/dot_general | solution.py:85
  114.9 7.2 %convolution_add_fusion.4 = f32[10,4096]{1,0:T(8,128)S(1)} fusion(f32[10,4096]{1,0:T(8,128)S(1)} %convolution_add_fusion.5, f32[512,10]{0,1:T(8,128)S(1)} %fusion.48, f32[4096,256]{1,0:T(8,128)S(1)} %copy-done.10, f32[4096,256]{1,0:T(8,128)S(1)} %copy-done.8), kind=kOutput, calls=%fused_computation.26 | convolution fusion | flops 253796352 | bytes 8736768 | tf_op jit(solution)/shard_map/dot_general | solution.py:91
  122.1 4.5 %fusion.50 = f32[512,10]{0,1:T(8,128)S(1)} fusion(f32[10,4096]{1,0:T(8,128)S(1)} %bitcast.189, f32[4096,256]{1,0:T(8,128)S(1)} %copy-done.6, f32[4096,256]{1,0:T(8,128)S(1)} %copy-done.4, f32[512]{0:T(512)S(1)} %get-tuple-element.101), kind=kOutput, calls=%fused_computation.78 | convolution fusion | flops 253760512 | bytes 8574976 | tf_op jit(solution)/shard_map/dot_general | solution.py:85
  126.6 7.4 %fusion.1 = bf16[10,1,4096]{2,0,1:T(8,128)(2,1)S(1)} fusion(f32[10,4096]{1,0:T(8,128)S(1)} %convolution_add_fusion.4, f32[512,10]{0,1:T(8,128)S(1)} %fusion.50, f32[4096,256]{1,0:T(8,128)S(1)} %copy-done.6, f32[4096,256]{1,0:T(8,128)S(1)} %copy-done.4), kind=kOutput, calls=%fused_computation.29 | convolution fusion | flops 253837312 | bytes 8654848 | tf_op jit(solution)/shard_map/dot_general | solution.py:91
  134.0 2.8 copy.27
  136.8 0.5 broadcast.396
  137.3 22.5 %reduce.8 = bf16[4096,10]{1,0:T(8,128)(2,1)S(1)} reduce(bf16[4096,1,10]{2,1,0:T(2,128)(2,1)S(1)} %bitcast.171, bf16[]{:T(256)} %broadcast.396), dimensions={1}, to_apply=%bitcast.152.reduce_sub_computation | reduce | bytes 163842
  159.8 2.5 reshape.241
  162.2 7.7 %all-to-all-start.1 = ((bf16[32,2,640]{2,1,0:T(2,128)(2,1)}), bf16[32,2,640]{2,1,0:T(2,128)(2,1)S(1)}, u32[]{:S(2)}, u32[]{:S(2)}) async-start(bf16[32,2,640]{2,1,0:T(2,128)(2,1)} %reshape.241), calls=%async_computation.1 | async-start | bytes 163840 | tf_op jit(solution)/shard_map/all_to_all | solution.py:178
  170.0 7.9 %all-to-all-done.1 = bf16[32,2,640]{2,1,0:T(2,128)(2,1)S(1)} async-done(((bf16[32,2,640]{2,1,0:T(2,128)(2,1)}), bf16[32,2,640]{2,1,0:T(2,128)(2,1)S(1)}, u32[]{:S(2)}, u32[]{:S(2)}) %all-to-all-start.1) | async-done | bytes 81952 | tf_op jit(solution)/shard_map/all_to_all | solution.py:178
  177.9 2.2 reshape.242
  180.1 2.1 copy.28
  182.4 0.6 copy.29
  183.0 8.1 %all-to-all-start.2 = ((f32[8,3,4,128]{3,2,1,0:T(4,128)}), f32[8,3,4,128]{3,2,1,0:T(4,128)S(1)}, u32[]{:S(2)}, u32[]{:S(2)}) async-start(f32[8,3,4,128]{3,2,1,0:T(4,128)} %copy.29), calls=%async_computation.2 | async-start | bytes 98304 | tf_op jit(solution)/shard_map/all_to_all | solution.py:39
  191.2 9.1 %all-to-all-done.2 = f32[8,3,4,128]{3,2,1,0:T(4,128)S(1)} async-done(((f32[8,3,4,128]{3,2,1,0:T(4,128)}), f32[8,3,4,128]{3,2,1,0:T(4,128)S(1)}, u32[]{:S(2)}, u32[]{:S(2)}) %all-to-all-start.2) | async-done | bytes 49184 | tf_op jit(solution)/shard_map/all_to_all | solution.py:39
  200.3 0.4 collective-permute-start
  200.6 7.2 %collective-permute-start.1 = (f32[3,4,128]{2,1,0:T(4,128)S(1)}, f32[3,4,128]{2,1,0:T(4,128)S(1)}, u32[]{:S(2)}, u32[]{:S(2)}) collective-permute-start(f32[3,4,128]{2,1,0:T(4,128)S(1)} %multiply_add_fusion.1), channel_id=1, source_target_pairs={{32,0},{64,32},{96,64},{128,96},{160,128},{192,160},{224,192},{0,2... | collective-permute-start | bytes 18440 | tf_op jit(solution)/shard_map/ppermute | solution.py:26
  207.8 1.0 collective-permute-done
  208.9 3.1 collective-permute-start.2
  212.1 0.2 collective-permute-start.3
  212.3 6.9 %gather_fusion.2 = f32[1024]{0:T(1024)S(1)} fusion(f32[512]{0:T(512)S(1)} %slice_bitcast_fusion.36, s32[1024]{0:T(1024)S(1)} %get-tuple-element.30), kind=kCustom, calls=%fused_computation.2 | custom fusion | bytes 12288 | tf_op jit(solution)/shard_map/gather | solution.py:194
  219.2 0.1 maximum_multiply_fusion.1
  219.3 0.1 fusion.60
  220.0 6.9 %gather_fusion = f32[1024]{0:T(1024)S(1)} fusion(f32[512]{0:T(512)S(1)} %fusion.100, s32[1024]{0:T(1024)S(1)} %get-tuple-element.30), kind=kCustom, calls=%fused_computation | custom fusion | bytes 12288 | tf_op jit(solution)/shard_map/gather | solution.py:194
  226.9 6.9 %gather_fusion.1 = f32[1024]{0:T(1024)S(1)} fusion(f32[512]{0:T(512)S(1)} %slice_bitcast_fusion.37, s32[1024]{0:T(1024)S(1)} %get-tuple-element.30), kind=kCustom, calls=%fused_computation.1 | custom fusion | bytes 12288 | tf_op jit(solution)/shard_map/gather | solution.py:194
  233.8 7.6 %scatter_custom_fusion = f32[512]{0:T(512)S(1)} fusion(s32[1024]{0:T(1024)S(1)} %get-tuple-element.31, f32[1024]{0:T(1024)S(1)} %get-tuple-element.86, f32[]{:T(128)} %constant.182.clone.1), kind=kCustom, calls=%fused_computation.245 | custom fusion | flops 1024 | bytes 2052 | tf_op jit(solution)/shard_map/scatter-add | solution.py:201
  241.4 7.6 %scatter_custom_fusion.1 = f32[512]{0:T(512)S(1)} fusion(s32[1024]{0:T(1024)S(1)} %get-tuple-element.31, f32[1024]{0:T(1024)S(1)} %get-tuple-element.87, f32[]{:T(128)} %constant.182.clone.1), kind=kCustom, calls=%fused_computation.243 | custom fusion | flops 1024 | bytes 2052 | tf_op jit(solution)/shard_map/scatter-add | solution.py:201
  249.1 0.1 collective-permute-start.4
  249.2 7.8 %collective-permute-start.5 = (f32[4,4,128]{2,1,0:T(4,128)S(1)}, f32[4,4,128]{2,1,0:T(4,128)S(1)}, u32[]{:S(2)}, u32[]{:S(2)}) collective-permute-start(f32[4,4,128]{2,1,0:T(4,128)S(1)} %pad_maximum_fusion.38), channel_id=1, source_target_pairs={{32,0},{64,32},{96,64},{128,96},{160,128},{192,160},{224,192},{0,2... | collective-permute-start | bytes 24584 | tf_op jit(solution)/shard_map/ppermute | solution.py:26
  257.0 0.9 collective-permute-done.4
  258.1 2.6 collective-permute-start.6
  260.7 3.8 %collective-permute-start.7 = (f32[4,12,4]{2,1,0:T(8,128)S(1)}, f32[4,12,4]{2,1,0:T(8,128)S(1)}, u32[]{:S(2)}, u32[]{:S(2)}) collective-permute-start(f32[4,12,4]{2,1,0:T(8,128)S(1)} %get-tuple-element.49), channel_id=1, source_target_pairs={{1,0},{2,1},{3,2},{4,3},{5,4},{6,5},{7,6},{8,7},{9,8},{10,9},{11,1... | collective-permute-start | bytes 2312 | tf_op jit(solution)/shard_map/ppermute | solution.py:26
  264.5 7.6 %scatter_custom_fusion.2 = f32[512]{0:T(512)S(1)} fusion(s32[1024]{0:T(1024)S(1)} %get-tuple-element.31, f32[1024]{0:T(1024)S(1)} %get-tuple-element.26, f32[]{:T(128)} %constant.182.clone.1), kind=kCustom, calls=%fused_computation.241 | custom fusion | flops 1024 | bytes 2052 | tf_op jit(solution)/shard_map/scatter-add | solution.py:201
  272.1 0.1 maximum_multiply_fusion
  272.3 0.1 fusion.56
  273.0 0.6 multiply_add_fusion
  273.6 17.9 %all_to_all.50 = bf16[8,3,4,128]{3,2,1,0:T(4,128)(2,1)S(1)} all-to-all(bf16[8,3,4,128]{3,2,1,0:T(4,128)(2,1)S(1)} %broadcast_in_dim.5), channel_id=1, replica_groups=mesh['grp'=8,'sp_0'=4,'sp_1'=4,'sp_2'=2] {'grp'}, dimensions={0} | all-to-all | bytes 49152 | tf_op jit(solution)/shard_map/all_to_all | solution.py:51
  291.6 0.1 copy.59
  291.8 20.8 %all_to_all.51 = f32[10,32,128]{2,0,1:T(8,128)S(1)} all-to-all(f32[10,32,128]{2,0,1:T(8,128)S(1)} %bitcast.180), channel_id=1, replica_groups=mesh['grp'=8,'sp_0'=4,'sp_1'=4,'sp_2'=2] {'sp_0','sp_1','sp_2'}, dimensions={1} | all-to-all | bytes 327680 | tf_op jit(solution)/shard_map/all_to_all | solution.py:176
  312.7 0.2 copy.55
  312.9 6.8 %fusion.51 = f32[10,512]{1,0:T(8,128)S(1)} fusion(f32[10,4096]{1,0:T(8,128)S(1)} %bitcast.173, f32[4096,256]{1,0:T(8,128)} %get-tuple-element.93, f32[4096,256]{1,0:T(8,128)} %get-tuple-element.92, f32[512]{0:T(512)S(1)} %get-tuple-element.101), kind=kOutput, calls=%fused_computation.79 | convolution fusion | flops 253760512 | bytes 8574976 | tf_op jit(solution)/shard_map/dot_general | solution.py:85
  319.7 4.1 %fusion.49 = f32[10,512]{1,0:T(8,128)S(1)} fusion(f32[10,4096]{1,0:T(8,128)S(1)} %bitcast.174, f32[4096,256]{1,0:T(8,128)S(1)} %copy-done.11, f32[4096,256]{1,0:T(8,128)S(1)} %copy-done.9, f32[512]{0:T(512)S(1)} %get-tuple-element.100), kind=kOutput, calls=%fused_computation.77 | convolution fusion | flops 253760512 | bytes 8574976 | tf_op jit(solution)/shard_map/dot_general | solution.py:85
  323.9 4.1 %fusion.47 = f32[10,512]{1,0:T(8,128)S(1)} fusion(f32[10,4096]{1,0:T(8,128)S(1)} %bitcast.175, f32[4096,256]{1,0:T(8,128)S(1)} %copy-done.15, f32[4096,256]{1,0:T(8,128)S(1)} %copy-done.13, f32[512]{0:T(512)S(1)} %get-tuple-element.99), kind=kOutput, calls=%fused_computation.75 | convolution fusion | flops 253760512 | bytes 8574976 | tf_op jit(solution)/shard_map/dot_general | solution.py:85
  327.9 4.5 %fusion.45 = f32[10,512]{1,0:T(8,128)S(1)} fusion(f32[10,4096]{1,0:T(8,128)S(1)} %bitcast.176, f32[4096,256]{1,0:T(8,128)S(1)} %copy-done.1, f32[4096,256]{1,0:T(8,128)S(1)} %copy-done.3, f32[512]{0:T(512)S(1)} %get-tuple-element.98), kind=kOutput, calls=%fused_computation.73 | convolution fusion | flops 253760512 | bytes 8574976 | tf_op jit(solution)/shard_map/dot_general | solution.py:85
  332.5 7.0 %fusion.32 = f32[10,4096]{1,0:T(8,128)S(1)} fusion(f32[10,512]{1,0:T(8,128)S(1)} %fusion.45, f32[4096,256]{1,0:T(8,128)S(1)} %copy-done.1, f32[4096,256]{1,0:T(8,128)S(1)} %copy-done.3), kind=kOutput, calls=%fused_computation.60 | convolution fusion | flops 253755392 | bytes 8572928 | tf_op jit(solution)/shard_map/dot_general | solution.py:91
  339.5 7.2 %convolution_add_fusion.2 = f32[10,4096]{1,0:T(8,128)S(1)} fusion(f32[10,4096]{1,0:T(8,128)S(1)} %fusion.32, f32[10,512]{1,0:T(8,128)S(1)} %fusion.47, f32[4096,256]{1,0:T(8,128)S(1)} %copy-done.15, f32[4096,256]{1,0:T(8,128)S(1)} %copy-done.13), kind=kOutput, calls=%fused_computation.24 | convolution fusion | flops 253796352 | bytes 8736768 | tf_op jit(solution)/shard_map/dot_general | solution.py:91
  346.7 7.0 %convolution_add_fusion.1 = f32[10,4096]{1,0:T(8,128)S(1)} fusion(f32[10,4096]{1,0:T(8,128)S(1)} %convolution_add_fusion.2, f32[10,512]{1,0:T(8,128)S(1)} %fusion.49, f32[4096,256]{1,0:T(8,128)S(1)} %copy-done.11, f32[4096,256]{1,0:T(8,128)S(1)} %copy-done.9), kind=kOutput, calls=%fused_computation.23 | convolution fusion | flops 253796352 | bytes 8736768 | tf_op jit(solution)/shard_map/dot_general | solution.py:91
  353.7 7.0 %convolution_add_fusion = f32[10,4096]{1,0:T(8,128)S(1)} fusion(f32[10,4096]{1,0:T(8,128)S(1)} %convolution_add_fusion.1, f32[10,512]{1,0:T(8,128)S(1)} %fusion.51, f32[4096,256]{1,0:T(8,128)S(1)} %copy-done.7, f32[4096,256]{1,0:T(8,128)S(1)} %copy-done.5), kind=kOutput, calls=%fused_computation.22 | convolution fusion | flops 253796352 | bytes 8736768 | tf_op jit(solution)/shard_map/dot_general | solution.py:91
  360.8 3.7 all_to_all.52
  364.5 0.1 copy.33
  364.7 11.2 %all_to_all.53 = f32[16,2,10,1,128]{4,1,2,3,0:T(2,128)S(1)} all-to-all(f32[16,2,10,1,128]{4,1,2,3,0:T(2,128)S(1)} %copy.33), channel_id=1, replica_groups=mesh['grp'=8,'sp_0'=4,'sp_1'=4,'sp_2'=2] {'sp_0','sp_1'}, dimensions={0} | all-to-all | bytes 327680 | tf_op jit(solution)/shard_map/all_to_all | solution.py:62
  375.9 0.1 copy.35
  376.1 0.7 add.330
  (121 shorter events, 2.2 us)
Async XLA Ops:
  2.4 81.4 %all-to-all-start = ((f32[10,32,128]{2,0,1:T(8,128)}), f32[10,32,128]{2,0,1:T(8,128)S(1)}, u32[]{:S(2)}, u32[]{:S(2)}) async-start(f32[10,32,128]{2,0,1:T(8,128)} %copy.25), calls=%async_computation | async-start | bytes 524288 | tf_op jit(solution)/shard_map/all_to_all | solution.py:176
  12.4 17.7 %copy-start.23 = (f32[1024]{0:T(1024)S(1)}, f32[1024]{0:T(1024)}, u32[]{:S(2)}) copy-start(f32[1024]{0:T(1024)} %param.17) | copy-start | bytes 12292
  65.8 17.9 %copy-start.24 = (s32[1024]{0:T(1024)S(1)}, s32[1024]{0:T(1024)}, u32[]{:S(2)}) copy-start(s32[1024]{0:T(1024)} %param.18) | copy-start | bytes 12292
  84.1 7.5 %copy-start = (f32[4096,256]{1,0:T(8,128)S(1)}, f32[4096,256]{1,0:T(8,128)}, u32[]{:S(2)}) copy-start(f32[4096,256]{1,0:T(8,128)} %get-tuple-element.102) | copy-start | bytes 12582916
  84.1 7.5 %copy-start.2 = (f32[4096,256]{1,0:T(8,128)S(1)}, f32[4096,256]{1,0:T(8,128)}, u32[]{:S(2)}) copy-start(f32[4096,256]{1,0:T(8,128)} %get-tuple-element.103) | copy-start | bytes 12582916
  91.6 7.0 %copy-start.12 = (f32[4096,256]{1,0:T(8,128)S(1)}, f32[4096,256]{1,0:T(8,128)}, u32[]{:S(2)}) copy-start(f32[4096,256]{1,0:T(8,128)} %get-tuple-element.96) | copy-start | bytes 12582916
  91.6 7.0 %copy-start.14 = (f32[4096,256]{1,0:T(8,128)S(1)}, f32[4096,256]{1,0:T(8,128)}, u32[]{:S(2)}) copy-start(f32[4096,256]{1,0:T(8,128)} %get-tuple-element.97) | copy-start | bytes 12582916
  103.1 7.2 %copy-start.8 = (f32[4096,256]{1,0:T(8,128)S(1)}, f32[4096,256]{1,0:T(8,128)}, u32[]{:S(2)}) copy-start(f32[4096,256]{1,0:T(8,128)} %get-tuple-element.94) | copy-start | bytes 12582916
  103.1 7.2 %copy-start.10 = (f32[4096,256]{1,0:T(8,128)S(1)}, f32[4096,256]{1,0:T(8,128)}, u32[]{:S(2)}) copy-start(f32[4096,256]{1,0:T(8,128)} %get-tuple-element.95) | copy-start | bytes 12582916
  114.8 7.2 %copy-start.4 = (f32[4096,256]{1,0:T(8,128)S(1)}, f32[4096,256]{1,0:T(8,128)}, u32[]{:S(2)}) copy-start(f32[4096,256]{1,0:T(8,128)} %get-tuple-element.92) | copy-start | bytes 12582916
  114.8 7.2 %copy-start.6 = (f32[4096,256]{1,0:T(8,128)S(1)}, f32[4096,256]{1,0:T(8,128)}, u32[]{:S(2)}) copy-start(f32[4096,256]{1,0:T(8,128)} %get-tuple-element.93) | copy-start | bytes 12582916
  137.3 45.0 %copy-start.16 = (bf16[10,3,32,128]{3,2,1,0:T(8,128)(2,1)S(1)}, bf16[10,3,32,128]{3,2,1,0:T(8,128)(2,1)}, u32[]{:S(2)}) copy-start(bf16[10,3,32,128]{3,2,1,0:T(8,128)(2,1)} %param.14) | copy-start | bytes 737284
  159.8 40.5 %copy-start.18 = (f32[3,4,128]{2,1,0:T(4,128)S(1)}, f32[3,4,128]{2,1,0:T(4,128)}, u32[]{:S(2)}) copy-start(f32[3,4,128]{2,1,0:T(4,128)} %param.16) | copy-start | bytes 18436
  159.8 40.5 %copy-start.19 = (f32[3,4,128]{2,1,0:T(4,128)S(1)}, f32[3,4,128]{2,1,0:T(4,128)}, u32[]{:S(2)}) copy-start(f32[3,4,128]{2,1,0:T(4,128)} %param.15) | copy-start | bytes 18436
  162.2 15.6 %all-to-all-start.1 = ((bf16[32,2,640]{2,1,0:T(2,128)(2,1)}), bf16[32,2,640]{2,1,0:T(2,128)(2,1)S(1)}, u32[]{:S(2)}, u32[]{:S(2)}) async-start(bf16[32,2,640]{2,1,0:T(2,128)(2,1)} %reshape.241), calls=%async_computation.1 | async-start | bytes 163840 | tf_op jit(solution)/shard_map/all_to_all | solution.py:178
  183.0 17.2 %all-to-all-start.2 = ((f32[8,3,4,128]{3,2,1,0:T(4,128)}), f32[8,3,4,128]{3,2,1,0:T(4,128)S(1)}, u32[]{:S(2)}, u32[]{:S(2)}) async-start(f32[8,3,4,128]{3,2,1,0:T(4,128)} %copy.29), calls=%async_computation.2 | async-start | bytes 98304 | tf_op jit(solution)/shard_map/all_to_all | solution.py:39
  200.3 8.6 %collective-permute-start = (f32[3,4,128]{2,1,0:T(4,128)S(1)}, f32[3,4,128]{2,1,0:T(4,128)S(1)}, u32[]{:S(2)}, u32[]{:S(2)}) collective-permute-start(f32[3,4,128]{2,1,0:T(4,128)S(1)} %multiply_add_fusion.1), channel_id=1, source_target_pairs={{0,32},{32,64},{64,96},{96,128},{128,160},{160,192},{192,224},{224... | collective-permute-start | bytes 18440 | tf_op jit(solution)/shard_map/ppermute | solution.py:23
  200.6 8.2 %collective-permute-start.1 = (f32[3,4,128]{2,1,0:T(4,128)S(1)}, f32[3,4,128]{2,1,0:T(4,128)S(1)}, u32[]{:S(2)}, u32[]{:S(2)}) collective-permute-start(f32[3,4,128]{2,1,0:T(4,128)S(1)} %multiply_add_fusion.1), channel_id=1, source_target_pairs={{32,0},{64,32},{96,64},{128,96},{160,128},{192,160},{224,192},{0,2... | collective-permute-start | bytes 18440 | tf_op jit(solution)/shard_map/ppermute | solution.py:26
  208.9 10.2 %collective-permute-start.2 = (f32[3,12,4]{2,1,0:T(8,128)S(1)}, f32[3,12,4]{2,1,0:T(8,128)S(1)}, u32[]{:S(2)}, u32[]{:S(2)}) collective-permute-start(f32[3,12,4]{2,1,0:T(8,128)S(1)} %get-tuple-element.66), channel_id=1, source_target_pairs={{0,1},{1,2},{2,3},{3,4},{4,5},{5,6},{6,7},{7,8},{8,9},{9,10},{10,1... | collective-permute-start | bytes 1736 | tf_op jit(solution)/shard_map/ppermute | solution.py:23
  212.1 7.1 %collective-permute-start.3 = (f32[3,12,4]{2,1,0:T(8,128)S(1)}, f32[3,12,4]{2,1,0:T(8,128)S(1)}, u32[]{:S(2)}, u32[]{:S(2)}) collective-permute-start(f32[3,12,4]{2,1,0:T(8,128)S(1)} %get-tuple-element.67), channel_id=1, source_target_pairs={{1,0},{2,1},{3,2},{4,3},{5,4},{6,5},{7,6},{8,7},{9,8},{10,9},{11,1... | collective-permute-start | bytes 1736 | tf_op jit(solution)/shard_map/ppermute | solution.py:26
  220.0 13.8 %copy-start.20 = (f32[1024]{0:T(1024)S(1)}, f32[1024]{0:T(1024)}, u32[]{:S(2)}) copy-start(f32[1024]{0:T(1024)} %param.21) | copy-start | bytes 12292
  220.0 13.8 %copy-start.21 = (f32[1024]{0:T(1024)S(1)}, f32[1024]{0:T(1024)}, u32[]{:S(2)}) copy-start(f32[1024]{0:T(1024)} %param.20) | copy-start | bytes 12292
  220.0 13.8 %copy-start.22 = (s32[1024]{0:T(1024)S(1)}, s32[1024]{0:T(1024)}, u32[]{:S(2)}) copy-start(s32[1024]{0:T(1024)} %param.19) | copy-start | bytes 12292
  249.1 8.9 %collective-permute-start.4 = (f32[4,4,128]{2,1,0:T(4,128)S(1)}, f32[4,4,128]{2,1,0:T(4,128)S(1)}, u32[]{:S(2)}, u32[]{:S(2)}) collective-permute-start(f32[4,4,128]{2,1,0:T(4,128)S(1)} %pad_maximum_fusion.38), channel_id=1, source_target_pairs={{0,32},{32,64},{64,96},{96,128},{128,160},{160,192},{192,224},{224... | collective-permute-start | bytes 24584 | tf_op jit(solution)/shard_map/ppermute | solution.py:23
  249.2 8.8 %collective-permute-start.5 = (f32[4,4,128]{2,1,0:T(4,128)S(1)}, f32[4,4,128]{2,1,0:T(4,128)S(1)}, u32[]{:S(2)}, u32[]{:S(2)}) collective-permute-start(f32[4,4,128]{2,1,0:T(4,128)S(1)} %pad_maximum_fusion.38), channel_id=1, source_target_pairs={{32,0},{64,32},{96,64},{128,96},{160,128},{192,160},{224,192},{0,2... | collective-permute-start | bytes 24584 | tf_op jit(solution)/shard_map/ppermute | solution.py:26
  258.1 14.1 %collective-permute-start.6 = (f32[4,12,4]{2,1,0:T(8,128)S(1)}, f32[4,12,4]{2,1,0:T(8,128)S(1)}, u32[]{:S(2)}, u32[]{:S(2)}) collective-permute-start(f32[4,12,4]{2,1,0:T(8,128)S(1)} %get-tuple-element.48), channel_id=1, source_target_pairs={{0,1},{1,2},{2,3},{3,4},{4,5},{5,6},{6,7},{7,8},{8,9},{9,10},{10,1... | collective-permute-start | bytes 2312 | tf_op jit(solution)/shard_map/ppermute | solution.py:23
  260.7 11.5 %collective-permute-start.7 = (f32[4,12,4]{2,1,0:T(8,128)S(1)}, f32[4,12,4]{2,1,0:T(8,128)S(1)}, u32[]{:S(2)}, u32[]{:S(2)}) collective-permute-start(f32[4,12,4]{2,1,0:T(8,128)S(1)} %get-tuple-element.49), channel_id=1, source_target_pairs={{1,0},{2,1},{3,2},{4,3},{5,4},{6,5},{7,6},{8,7},{9,8},{10,9},{11,1... | collective-permute-start | bytes 2312 | tf_op jit(solution)/shard_map/ppermute | solution.py:26
  312.8 6.9 %copy-start.9 = (f32[4096,256]{1,0:T(8,128)S(1)}, f32[4096,256]{1,0:T(8,128)}, u32[]{:S(2)}) copy-start(f32[4096,256]{1,0:T(8,128)} %get-tuple-element.94) | copy-start | bytes 12582916
  312.9 6.9 %copy-start.11 = (f32[4096,256]{1,0:T(8,128)S(1)}, f32[4096,256]{1,0:T(8,128)}, u32[]{:S(2)}) copy-start(f32[4096,256]{1,0:T(8,128)} %get-tuple-element.95) | copy-start | bytes 12582916
  319.7 4.1 %copy-start.13 = (f32[4096,256]{1,0:T(8,128)S(1)}, f32[4096,256]{1,0:T(8,128)}, u32[]{:S(2)}) copy-start(f32[4096,256]{1,0:T(8,128)} %get-tuple-element.96) | copy-start | bytes 12582916
  319.7 4.1 %copy-start.15 = (f32[4096,256]{1,0:T(8,128)S(1)}, f32[4096,256]{1,0:T(8,128)}, u32[]{:S(2)}) copy-start(f32[4096,256]{1,0:T(8,128)} %get-tuple-element.97) | copy-start | bytes 12582916
  323.8 4.1 %copy-start.1 = (f32[4096,256]{1,0:T(8,128)S(1)}, f32[4096,256]{1,0:T(8,128)}, u32[]{:S(2)}) copy-start(f32[4096,256]{1,0:T(8,128)} %get-tuple-element.102) | copy-start | bytes 12582916
  323.8 4.1 %copy-start.3 = (f32[4096,256]{1,0:T(8,128)S(1)}, f32[4096,256]{1,0:T(8,128)}, u32[]{:S(2)}) copy-start(f32[4096,256]{1,0:T(8,128)} %get-tuple-element.103) | copy-start | bytes 12582916
  346.6 7.0 %copy-start.5 = (f32[4096,256]{1,0:T(8,128)S(1)}, f32[4096,256]{1,0:T(8,128)}, u32[]{:S(2)}) copy-start(f32[4096,256]{1,0:T(8,128)} %get-tuple-element.92) | copy-start | bytes 12582916
  346.7 7.0 %copy-start.7 = (f32[4096,256]{1,0:T(8,128)S(1)}, f32[4096,256]{1,0:T(8,128)}, u32[]{:S(2)}) copy-start(f32[4096,256]{1,0:T(8,128)} %get-tuple-element.93) | copy-start | bytes 12582916
  353.7 22.4 %copy-start.17 = (f32[10,32,128]{2,1,0:T(8,128)S(1)}, f32[10,32,128]{2,1,0:T(8,128)}, u32[]{:S(2)}) copy-start(f32[10,32,128]{2,1,0:T(8,128)} %param.13) | copy-start | bytes 491524
where the time goes:
time: 383 us; the launch traced here: 377 us
  other arithmetic  120 us (31%)
  matrix products  97.4 us (25%)
  blocking collectives  53.7 us (14%)
  starting transfers between devices  51.1 us (13%)
  local copies, waits for them, and re-layouts  34.5 us (9%)
  waiting for transfers between devices  18.9 us (5%)
    dot_general x8, matrix products, spectral_filter(): jnp.dot(coeffs * weights[None, :], fourier_basis.T, precision=lax.Precisi...  56.9 us
    cos x3, other arithmetic, spectral_filter(): jnp.cos(radians)  53.6 us
    dot_general x8, matrix products, spectral_filter(): jnp.dot(rows_data, fourier_basis, precision=lax.Precision.HIGHEST, prefer...  40.5 us
    scatter-add x3, other arithmetic, per_device(): jnp.zeros((tile_rows * tile_cols,), jnp.float32).at[local_index]  22.8 us
    unnamed x4, other arithmetic  22.5 us
    all_to_all x1, blocking collectives, to_rows(): lax.all_to_all(columns, SP, split_axis=1, concat_axis=2, tiled=True)  20.8 us
    gather x3, local copies, waits for them, and re-layouts, per_device(): values = states[moment][0].reshape(-1)[local_index]  20.6 us
    ppermute x4, starting transfers between devices, extended(): lax.ppermute(lax.slice_in_dim(block, 0, width, axis=dim), axis, backward)  19 us
  transfers between devices with their start and end apart: 11, of which 4 were waited for; matrix products, arithmetic and copies ran while one was open for 23% of the time, Pallas kernels for 0%

commit v1 on v0

v1 whole, which is shorter than its diff:
```python
import math

import jax
import jax.numpy as jnp
import numpy as np
from jax import lax
from jax.experimental import pallas as pl
from jax.experimental.pallas import tpu as pltpu
from jax.sharding import Mesh
from jax.sharding import PartitionSpec as P

GRP_SP = ("grp", "sp_0", "sp_1", "sp_2")
SP = ("sp_0", "sp_1", "sp_2")

MEM = 10
SLOTS = 16
ROWS = 32
COLS = 128
BLOCKS = 32
GROUPS = 8
TILE_ROWS = 4
NX = BLOCKS * COLS
KEEP = 1024
ALPHAS = 2 * KEEP // BLOCKS
FIELDS = 9
COURANT = 0.4

F32 = jnp.float32
BF16 = jnp.bfloat16
VMEM = pltpu.VMEM


def call(body, out_shape, scratch=(), n_in=1):
    single = not isinstance(out_shape, (list, tuple))
    spec = pl.BlockSpec(memory_space=VMEM)
    return pl.pallas_call(
        body,
        out_shape=out_shape,
        in_specs=[spec] * n_in,
        out_specs=spec if single else [spec] * len(out_shape),
        scratch_shapes=list(scratch),
        compiler_params=pltpu.CompilerParams(vmem_limit_bytes=32 << 20),
    )


def split(table):
    high = table.astype(jnp.bfloat16)
    low = (table - np.asarray(high).astype(np.float64)).astype(jnp.bfloat16)
    return np.asarray(high), np.asarray(low)


def tables():
    j = np.arange(COLS)
    wave = np.concatenate([np.arange(ALPHAS // 2), -1 - np.arange(ALPHAS // 2)])
    angle = 2.0 * np.pi * ((j[:, None] * wave[None, :]) % COLS) / COLS
    c, s = np.cos(angle), np.sin(angle)
    basis = np.concatenate(
        [np.concatenate([c, -s], axis=1), np.concatenate([s, c], axis=1)], axis=0
    )
    turn = 2.0 * np.pi * np.arange(BLOCKS)[:, None] * j[None, :] / NX
    twiddle = np.stack([np.cos(turn), np.sin(turn)]).astype(np.float32)
    high, low = split(basis)
    return high, low, np.ascontiguousarray(high.T), np.ascontiguousarray(low.T), twiddle


def fft(load, start, step, n, sign):
    if n == 1:
        return [load(start)]
    even = fft(load, start, 2 * step, n // 2, sign)
    odd = fft(load, start + step, 2 * step, n // 2, sign)
    low, high = [], []
    for k in range(n // 2):
        er, ei = even[k]
        xr, xi = odd[k]
        if k == 0:
            tr, ti = xr, xi
        elif 4 * k == n:
            tr, ti = (-xi, xr) if sign > 0 else (xi, -xr)
        elif 8 * k == n:
            r = math.sqrt(0.5)
            tr, ti = ((xr - xi) * r, (xr + xi) * r) if sign > 0 else ((xr + xi) * r, (xi - xr) * r)
        elif 8 * k == 3 * n:
            r = math.sqrt(0.5)
            tr, ti = (-(xr + xi) * r, (xr - xi) * r) if sign > 0 else ((xi - xr) * r, -(xr + xi) * r)
        else:
            c = math.cos(2.0 * math.pi * k / n)
            s = sign * math.sin(2.0 * math.pi * k / n)
            tr, ti = xr * c - xi * s, xr * s + xi * c
        low.append((er + tr, ei + ti))
        high.append((er - tr, ei - ti))
    return low + high


def product(x, high, low):
    xh = x.astype(BF16)
    xl = (x - xh.astype(F32)).astype(BF16)
    h = high[...]
    total = jnp.dot(xl, h, preferred_element_type=F32)
    total = total + jnp.dot(xh, low[...], preferred_element_type=F32)
    return total + jnp.dot(xh, h, preferred_element_type=F32)


def filter_rows(rows, high, low, high_t, low_t, twiddle, weights, out, wide, spec):
    def load(p):
        x = rows[p].astype(F32)
        return x[:8], x[8:]

    for b, (ur, ui) in enumerate(fft(load, 0, 1, BLOCKS, -1)):
        c, s = twiddle[0, b : b + 1, :], twiddle[1, b : b + 1, :]
        wide[8 * b : 8 * b + 8, :COLS] = ur * c + ui * s
        wide[8 * b : 8 * b + 8, COLS:] = ui * c - ur * s
    spec[...] = product(wide[...], high, low)
    for b in range(BLOCKS):
        spec[8 * b : 8 * b + 8, :] = spec[8 * b : 8 * b + 8, :] * weights[b : b + 1, :]
    wide[...] = product(spec[...], high_t, low_t)

    def load_back(b):
        c, s = twiddle[0, b : b + 1, :], twiddle[1, b : b + 1, :]
        yr, yi = wide[8 * b : 8 * b + 8, :COLS], wide[8 * b : 8 * b + 8, COLS:]
        return yr * c - yi * s, yr * s + yi * c

    for p, (yr, yi) in enumerate(fft(load_back, 0, 1, BLOCKS, 1)):
        out[p] = jnp.concatenate([yr, yi], axis=0).astype(BF16)


def localize(rows, weights):
    return call(
        filter_rows,
        jax.ShapeDtypeStruct((BLOCKS, SLOTS, COLS), BF16),
        [VMEM((8 * BLOCKS, 2 * COLS), F32), VMEM((8 * BLOCKS, COLS), F32)],
        7,
    )(rows, *tables(), weights)


def by_row(flat, out):
    for y in range(ROWS):
        x = flat[pl.ds(y, MEM, stride=ROWS), :]
        x = jnp.concatenate([x, jnp.zeros((SLOTS - MEM, COLS), F32)], axis=0)
        out[y] = x.astype(BF16)


def to_send(alpha):
    return call(by_row, jax.ShapeDtypeStruct((ROWS, SLOTS, COLS), BF16))(
        alpha.reshape(MEM * ROWS, COLS)
    )


def contract(ensemble, arrived, out, flat):
    flat[...] = arrived[...].astype(F32).reshape(ROWS * SLOTS, COLS)
    totals = [jnp.zeros((ROWS, COLS), F32)] * 3
    for m in range(MEM):
        field = flat[pl.ds(m, ROWS, stride=SLOTS), :]
        for v in range(3):
            totals[v] = totals[v] + ensemble[m, v].astype(F32) * field
    for v in range(3):
        part = totals[v].astype(BF16)
        for g in range(GROUPS):
            out[g, ROWS * v : ROWS * v + ROWS, :] = part


def partial_sums(ensemble, arrived):
    return call(
        contract,
        jax.ShapeDtypeStruct((GROUPS, 3 * ROWS, COLS), BF16),
        [VMEM((ROWS * SLOTS, COLS), F32)],
        2,
    )(ensemble, arrived)


def observe(cell, step, innovation, weight, std, control, out):
    where_row = jnp.right_shift(cell[...], 12) & (TILE_ROWS - 1)
    key = step[...] * TILE_ROWS + where_row
    column = cell[...] & (COLS - 1)
    w = weight[...]
    wd = w * innovation[...]
    n = 3 * TILE_ROWS
    count = w.shape[1]
    mine = lax.broadcasted_iota(jnp.int32, (n, count), 0) == key
    values = jnp.concatenate([jnp.where(mine, w, 0.0), jnp.where(mine, wd, 0.0)], axis=0)
    high = values.astype(BF16)
    rest = values - high.astype(F32)
    mid = rest.astype(BF16)
    low = (rest - mid.astype(F32)).astype(BF16)
    hot = (lax.broadcasted_iota(jnp.int32, (COLS, count), 0) == column).astype(F32).astype(BF16)
    total = jnp.zeros((2 * n, COLS), F32)
    for piece in (low, mid, high):
        total = total + lax.dot_general(
            piece, hot, (((1,), (1,)), ((), ())), preferred_element_type=F32
        )
    for g in range(GROUPS):
        out[g, : 2 * n, :] = total
        for v in range(3):
            out[g, 2 * n + 4 * v : 2 * n + 4 * v + 4, :] = std[v] * control[v]
        out[g, 36:40, :] = jnp.zeros((4, COLS), F32)


def tile_fields(cell, step, innovation, weight, std, control):
    flat = [a.reshape(1, -1) for a in (cell, step, innovation, weight)]
    return call(observe, jax.ShapeDtypeStruct((GROUPS, 40, COLS), F32), (), 6)(
        *flat, std, control
    )


def stack_rows(arrived, out):
    for f in range(FIELDS):
        for g in range(GROUPS):
            out[f, TILE_ROWS * g : TILE_ROWS * g + TILE_ROWS, :] = arrived[
                g, TILE_ROWS * f : TILE_ROWS * f + TILE_ROWS, :
            ]


def all_rows(arrived):
    return call(stack_rows, jax.ShapeDtypeStruct((FIELDS, ROWS, COLS), F32))(arrived)


def add_groups(arrived, fields, out):
    spread = 1.0 / math.sqrt(MEM * GROUPS - 1)
    for v in range(3):
        total = arrived[0, ROWS * v : ROWS * v + ROWS, :].astype(F32)
        for g in range(1, GROUPS):
            total = total + arrived[g, ROWS * v : ROWS * v + ROWS, :].astype(F32)
        out[v] = spread * total + fields[6 + v]


def increments(arrived, fields):
    return call(add_groups, jax.ShapeDtypeStruct((3, ROWS, COLS), F32), (), 2)(arrived, fields)


def window(inc, inc_low, inc_high, fields, f_low, f_high, ensemble, sent, adj, flat):
    lane = lax.broadcasted_iota(jnp.int32, (ROWS, COLS), 1)

    def wide(main, low, high):
        rim = jnp.where(lane < 8, high, jnp.where(lane >= COLS - 8, low, 0.0))
        return jnp.concatenate([main, rim], axis=1)

    row = lax.broadcasted_iota(jnp.int32, (ROWS, 2 * COLS), 0)
    rotation = 0.1 + 0.2 * (row.astype(F32) + 0.5) / ROWS
    down = row < ROWS - 1
    up = row > 0
    half_c = 0.5 * COURANT

    def dx(q):
        return half_c * (pltpu.roll(q, 2 * COLS - 1, 1) - pltpu.roll(q, 1, 1))

    def dy(q):
        below = jnp.where(down, pltpu.roll(q, ROWS - 1, 0), 0.0)
        above = jnp.where(up, pltpu.roll(q, 1, 0), 0.0)
        return half_c * (below - above)

    def forward(h, u, w):
        h1 = h - (dx(u) + dy(w))
        return h1, u - dx(h1) + rotation * w, w - dy(h1) - rotation * u

    def backward(bh, bu, bw):
        a = bh + (dx(bu) + dy(bw))
        return a, bu - rotation * bw + dx(a), bw + rotation * bu + dy(a)

    state = tuple(wide(inc[v], inc_low[v], inc_high[v]) for v in range(3))
    forcing = []
    for t in range(3):
        w_t = wide(fields[t], f_low[t], f_high[t])
        v_t = wide(fields[3 + t], f_low[3 + t], f_high[3 + t])
        forcing.append(w_t * state[0] - v_t)
        if t < 2:
            state = forward(*state)
    zero = jnp.zeros((ROWS, 2 * COLS), F32)
    bh, bu, bw = backward(forcing[2], zero, zero)
    bh, bu, bw = backward(bh + forcing[1], bu, bw)
    bh = bh + forcing[0]
    fin = [x[:, :COLS] for x in (bh, bu, bw)]
    for v in range(3):
        adj[v] = fin[v]
    for m in range(MEM):
        total = ensemble[m, 0].astype(F32) * fin[0]
        for v in range(1, 3):
            total = total + ensemble[m, v].astype(F32) * fin[v]
        flat[ROWS * m : ROWS * m + ROWS, :] = total
    by_row(flat, sent)


def assimilate(inc, inc_low, inc_high, fields, f_low, f_high, ensemble):
    return call(
        window,
        [
            jax.ShapeDtypeStruct((ROWS, SLOTS, COLS), BF16),
            jax.ShapeDtypeStruct((3, ROWS, COLS), F32),
        ],
        [VMEM((MEM * ROWS, COLS), F32)],
        7,
    )(inc, inc_low, inc_high, fields, f_low, f_high, ensemble)


def add_alpha(alpha, arrived, out, flat):
    spread = 1.0 / math.sqrt(MEM * GROUPS - 1)
    flat[...] = arrived[...].astype(F32).reshape(ROWS * SLOTS, COLS)
    for m in range(MEM):
        out[m] = alpha[m] + spread * flat[pl.ds(m, ROWS, stride=SLOTS), :]


def finish(alpha, arrived):
    return call(
        add_alpha,
        jax.ShapeDtypeStruct((MEM, ROWS, COLS), F32),
        [VMEM((ROWS * SLOTS, COLS), F32)],
        2,
    )(alpha, arrived)


def wave_weights(loc_spectrum):
    side = KEEP // BLOCKS
    first = jnp.arange(KEEP) == 0
    up = jnp.where(first, loc_spectrum, 0.5 * loc_spectrum).reshape(side, BLOCKS)
    after = jnp.concatenate([0.5 * loc_spectrum[1:], jnp.zeros((1,), F32)])
    down = after.reshape(side, BLOCKS)[:, ::-1]
    both = jnp.concatenate([up, down], axis=0).T
    return jnp.concatenate([both, both], axis=1)


def swap(x, axis):
    return lax.all_to_all(x, axis, split_axis=0, concat_axis=0, tiled=True)


def neighbours(x):
    ahead = [(i, (i + 1) % BLOCKS) for i in range(BLOCKS)]
    back = [(t, s) for s, t in ahead]
    return lax.ppermute(x, SP, ahead), lax.ppermute(x, SP, back)


def per_device(
    alpha, ensemble, static_std, control, loc_spectrum, obs_cell, obs_step, innovation, obs_weight
):
    first_row = lax.axis_index("grp") * TILE_ROWS
    rows = swap(to_send(alpha), SP)
    tiles = tile_fields(obs_cell, obs_step, innovation, obs_weight, static_std, control)
    weights = wave_weights(loc_spectrum)
    localized = swap(localize(rows, weights), SP)
    fields = all_rows(swap(tiles, "grp"))
    f_low, f_high = neighbours(fields[:6])
    summed = swap(partial_sums(ensemble, localized), "grp")
    inc = increments(summed, fields)
    inc_low, inc_high = neighbours(inc)
    sent, adjoint = assimilate(inc, inc_low, inc_high, fields, f_low, f_high, ensemble)
    weighted = swap(sent, SP)
    mine = lax.dynamic_slice_in_dim(adjoint, first_row, TILE_ROWS, axis=1)
    grad_control = control + static_std * mine
    filtered = swap(localize(weighted, weights), SP)
    return finish(alpha, filtered), grad_control


def solution(mesh):
    torus = Mesh(mesh.devices.reshape(mesh.shape["grp"], 4, 4, 2), GRP_SP)
    placed = (
        P("grp", None, SP),
        P("grp", None, None, SP),
        P(None, "grp", SP),
        P(None, "grp", SP),
        P(),
        P(GRP_SP),
        P(GRP_SP),
        P(GRP_SP),
        P(GRP_SP),
    )
    return jax.shard_map(
        per_device,
        mesh=torus,
        in_specs=placed,
        out_specs=(P("grp", None, SP), P(None, "grp", SP)),
        check_vma=False,
    )
```

time: 383 us -> 108 us (0.28); the launches traced: 377 us -> 107 us
  other arithmetic: 120 us -> 0.91 us
  matrix products: 97.4 us -> 0 us
  blocking collectives: 53.7 us -> 19.2 us
  local copies, waits for them, and re-layouts: 34.5 us -> 1.91 us
  waiting for transfers between devices: 18.9 us -> 42.8 us
  starting transfers between devices: 51.1 us -> 34.8 us
  Pallas kernels: 0 us -> 6.81 us
    dot_general x16 -> x0, matrix products: 97.4 us -> none  [the longest x8 56.9 us: spectral_filter(): jnp.dot(coeffs * weights[None, :], fourier_basis.T, precision=lax.Precisi...]
    cos x3 -> x0, other arithmetic: 53.6 us -> none  [spectral_filter(): jnp.cos(radians)]
    all_to_all x4 -> x1, blocking collectives: 53.7 us -> 19.2 us  [swap(): return lax.all_to_all(x, axis, split_axis=0, concat_axis=0, tiled=True)]
    scatter-add x4 -> x0, other arithmetic: 22.8 us -> none  [the longest x3 22.8 us: per_device(): jnp.zeros((tile_rows * tile_cols,), jnp.float32).at[local_index]]
    unnamed x4 -> x0, other arithmetic: 22.5 us -> none
    all_to_all x3 -> x5, waiting for transfers between devices: 16.9 us -> 39.3 us  [swap(): return lax.all_to_all(x, axis, split_axis=0, concat_axis=0, tiled=True)]
    gather x3 -> x0, local copies, waits for them, and re-layouts: 20.6 us -> none  [per_device(): values = states[moment][0].reshape(-1)[local_index]]
    ppermute x8 -> x4, starting transfers between devices: 25.2 us -> 5.11 us  [neighbours(): return (lax.ppermute(x, SP, ahead), lax.ppermute(x, SP, back))]
  transfers between devices with their start and end apart: 11 -> 9, of which waited for: 4 -> 7; matrix products, arithmetic and copies ran while one was open for 23% -> 1% of each run, Pallas kernels for 0% -> 2%
where the time goes in v1:
time: 108 us; the launch traced here: 107 us
  waiting for transfers between devices  42.8 us (40%)
  starting transfers between devices  34.8 us (32%)
  blocking collectives  19.2 us (18%)
  Pallas kernels  6.81 us (6%)
  local copies, waits for them, and re-layouts  1.91 us (2%)
    all_to_all x5, waiting for transfers between devices, swap(): return lax.all_to_all(x, axis, split_axis=0, concat_axis=0, tiled=True)  39.3 us
    all_to_all x5, starting transfers between devices, swap(): return lax.all_to_all(x, axis, split_axis=0, concat_axis=0, tiled=True)  29.7 us
    all_to_all x1, blocking collectives, swap(): return lax.all_to_all(x, axis, split_axis=0, concat_axis=0, tiled=True)  19.2 us
    ppermute x4, starting transfers between devices, neighbours(): return (lax.ppermute(x, SP, ahead), lax.ppermute(x, SP, back))  5.11 us
    ppermute x4, waiting for transfers between devices, neighbours(): return (lax.ppermute(x, SP, ahead), lax.ppermute(x, SP, back))  3.51 us
    pallas_call x2, Pallas kernels, localize(): call(filter_rows, jax.ShapeDtypeStruct((BLOCKS, SLOTS, COLS), BF16), [VME...  2.74 us
  transfers between devices with their start and end apart: 9, of which 7 were waited for; matrix products, arithmetic and copies ran while one was open for 1% of the time, Pallas kernels for 2%

profile of v1, /device:TPU:1, one launch (start us, length us, event | category | flops | bytes accessed | tf_op | source)
XLA Modules:
  0.0 107.2 jit_solution(6464804588796129574)
XLA Ops:
  0.6 0.0 copy-start.1
  0.6 0.9 copy-done.1
  1.5 0.8 shard_map.194
  2.3 0.0 copy-start.14
  2.3 0.0 copy-start.6
  2.3 10.2 %all-to-all-start = ((bf16[32,16,128]{2,1,0:T(8,128)(2,1)}), bf16[32,16,128]{2,1,0:T(8,128)(2,1)S(1)}, u32[]{:S(2)}, u32[]{:S(2)}) async-start(bf16[32,16,128]{2,1,0:T(8,128)(2,1)} %shard_map.194), calls=%async_computation | async-start | bytes 262144 | tf_op jit(solution)/shard_map/all_to_all | solution.py:320
  12.5 0.0 copy-done.14
  12.5 0.1 slice_multiply_fusion
  12.6 0.0 copy-start.7
  12.6 0.1 pad_maximum_fusion.1
  12.6 0.1 reshape.27
  12.7 0.0 copy-start.5
  12.7 0.1 copy.21
  12.8 0.0 copy-start.3
  12.8 0.0 copy-start.4
  12.8 0.1 reshape.26
  12.9 0.1 copy.22
  13.0 0.1 maximum_bitcast_fusion
  13.0 0.1 pad_maximum_fusion.weights
  13.1 7.9 %all-to-all-done.rows = bf16[32,16,128]{2,1,0:T(8,128)(2,1)S(1)} async-done(((bf16[32,16,128]{2,1,0:T(8,128)(2,1)}), bf16[32,16,128]{2,1,0:T(8,128)(2,1)S(1)}, u32[]{:S(2)}, u32[]{:S(2)}) %all-to-all-start) | async-done | bytes 131104 | tf_op jit(solution)/shard_map/all_to_all | solution.py:320
  21.0 0.0 copy-done.6
  21.0 0.0 copy-done.7
  21.0 0.0 copy-done.5
  21.0 0.0 copy-done.3
  21.0 0.0 copy-done.4
  21.0 1.4 %shard_map.195 = bf16[32,16,128]{2,1,0:T(8,128)(2,1)} custom-call(bf16[32,16,128]{2,1,0:T(8,128)(2,1)S(1)} %all-to-all-done.rows, bf16[256,128]{1,0:T(8,128)(2,1)S(1)} %copy-done.3, bf16[256,128]{1,0:T(8,128)(2,1)S(1)} %copy-done.4, bf16[128,256]{1,0:T(8,128)(2,1)S(1)} %copy-done.5, bf16[128,256]{1,0:T(8,128)(2,1)S(1)} %copy-done.6, ...), custom_call_target="tpu_custom_call" | custom-call | tf_op jit(solution)/shard_map/pallas_call | solution.py:127
  22.4 0.0 copy-start.9
  22.4 0.0 copy-start.10
  22.4 0.0 copy-start.11
  22.4 0.0 copy-start.12
  22.4 0.0 copy-start.13
  22.4 4.0 %all-to-all-start.1 = ((bf16[32,16,128]{2,1,0:T(8,128)(2,1)}), bf16[32,16,128]{2,1,0:T(8,128)(2,1)S(1)}, u32[]{:S(2)}, u32[]{:S(2)}) async-start(bf16[32,16,128]{2,1,0:T(8,128)(2,1)} %shard_map.195), calls=%async_computation.1 | async-start | bytes 262144 | tf_op jit(solution)/shard_map/all_to_all | solution.py:320
  26.5 0.0 copy-start.8
  26.5 0.0 copy-done.9
  26.5 0.0 copy-done.10
  26.5 0.0 copy-done.11
  26.5 0.0 copy-done.12
  26.5 0.0 copy-done.13
  26.5 0.6 copy-done.8
  27.2 0.0 copy-start
  27.2 1.1 %shard_map.197 = f32[8,40,128]{2,1,0:T(8,128)} custom-call(s32[1,1024]{1,0:T(1,128)S(1)} %bitcast.8, s32[1,1024]{1,0:T(1,128)S(1)} %bitcast.9, f32[1,1024]{1,0:T(1,128)S(1)} %bitcast.10, f32[1,1024]{1,0:T(1,128)S(1)} %bitcast.11, f32[3,4,128]{2,1,0:T(4,128)S(1)} %copy-done.8, f32[3,4,128]{2,1,0:T(4,128)S(1)} %copy-done.9), custom_call_target="tpu_custom_call" | custom-call | tf_op jit(solution)/shard_map/pallas_call | solution.py:199
  28.3 6.9 %all-to-all-done.1.arrived = bf16[32,16,128]{2,1,0:T(8,128)(2,1)S(1)} async-done(((bf16[32,16,128]{2,1,0:T(8,128)(2,1)}), bf16[32,16,128]{2,1,0:T(8,128)(2,1)S(1)}, u32[]{:S(2)}, u32[]{:S(2)}) %all-to-all-start.1) | async-done | bytes 131104 | tf_op jit(solution)/shard_map/all_to_all | solution.py:320
  35.1 8.1 %all-to-all-start.3 = ((f32[8,40,128]{2,1,0:T(8,128)}), f32[8,40,128]{2,1,0:T(8,128)S(1)}, u32[]{:S(2)}, u32[]{:S(2)}) async-start(f32[8,40,128]{2,1,0:T(8,128)} %shard_map.197), calls=%async_computation.3 | async-start | bytes 327680 | tf_op jit(solution)/shard_map/all_to_all | solution.py:320
  43.3 0.0 copy-done
  43.3 0.8 shard_map.196
  44.0 8.8 %all-to-all-done.3.arrived = f32[8,40,128]{2,1,0:T(8,128)S(1)} async-done(((f32[8,40,128]{2,1,0:T(8,128)}), f32[8,40,128]{2,1,0:T(8,128)S(1)}, u32[]{:S(2)}, u32[]{:S(2)}) %all-to-all-start.3) | async-done | bytes 163872 | tf_op jit(solution)/shard_map/all_to_all | solution.py:320
  52.9 3.4 %all-to-all-start.2 = ((bf16[8,96,128]{2,1,0:T(8,128)(2,1)}), bf16[8,96,128]{2,1,0:T(8,128)(2,1)S(1)}, u32[]{:S(2)}, u32[]{:S(2)}) async-start(bf16[8,96,128]{2,1,0:T(8,128)(2,1)} %shard_map.196), calls=%async_computation.2 | async-start | bytes 393216 | tf_op jit(solution)/shard_map/all_to_all | solution.py:320
  56.3 2.0 %collective-permute-start.2 = (f32[6,32,128]{2,1,0:T(8,128)S(1)}, f32[6,32,128]{2,1,0:T(8,128)S(1)}, u32[]{:S(2)}, u32[]{:S(2)}) collective-permute-start(f32[6,32,128]{2,1,0:T(8,128)S(1)} %slice.8), channel_id=1, source_target_pairs={{0,1},{1,2},{2,3},{3,4},{4,5},{5,6},{6,7},{7,8},{8,9},{9,10},{10,1... | collective-permute-start | bytes 294920 | tf_op jit(solution)/shard_map/ppermute | solution.py:326
  58.3 0.0 collective-permute-start.3
  58.3 7.6 %all-to-all-done.2.arrived = bf16[8,96,128]{2,1,0:T(8,128)(2,1)S(1)} async-done(((bf16[8,96,128]{2,1,0:T(8,128)(2,1)}), bf16[8,96,128]{2,1,0:T(8,128)(2,1)S(1)}, u32[]{:S(2)}, u32[]{:S(2)}) %all-to-all-start.2) | async-done | bytes 196640 | tf_op jit(solution)/shard_map/all_to_all | solution.py:320
  65.9 3.1 %collective-permute-start = (f32[3,32,128]{2,1,0:T(8,128)S(1)}, f32[3,32,128]{2,1,0:T(8,128)S(1)}, u32[]{:S(2)}, u32[]{:S(2)}) collective-permute-start(f32[3,32,128]{2,1,0:T(8,128)S(1)} %shard_map.199.inc), channel_id=1, source_target_pairs={{0,1},{1,2},{2,3},{3,4},{4,5},{5,6},{6,7},{7,8},{8,9},{9,10},{10,1... | collective-permute-start | bytes 147464 | tf_op jit(solution)/shard_map/ppermute | solution.py:326
  69.1 0.0 collective-permute-start.1
  69.1 0.0 collective-permute-done.2.f_low
  69.1 0.0 collective-permute-done.3.f_high
  69.1 1.2 %collective-permute-done.inc_low = f32[3,32,128]{2,1,0:T(8,128)S(1)} collective-permute-done((f32[3,32,128]{2,1,0:T(8,128)S(1)}, f32[3,32,128]{2,1,0:T(8,128)S(1)}, u32[]{:S(2)}, u32[]{:S(2)}) %collective-permute-start) | collective-permute-done | bytes 49184 | tf_op jit(solution)/shard_map/ppermute | solution.py:326
  70.2 2.3 %collective-permute-done.1.inc_high = f32[3,32,128]{2,1,0:T(8,128)S(1)} collective-permute-done((f32[3,32,128]{2,1,0:T(8,128)S(1)}, f32[3,32,128]{2,1,0:T(8,128)S(1)}, u32[]{:S(2)}, u32[]{:S(2)}) %collective-permute-start.1) | collective-permute-done | bytes 49184 | tf_op jit(solution)/shard_map/ppermute | solution.py:326
  72.6 0.6 shard_map.200
  73.2 19.2 %all_to_all.30.rows = bf16[32,16,128]{2,1,0:T(8,128)(2,1)S(1)} all-to-all(bf16[32,16,128]{2,1,0:T(8,128)(2,1)S(1)} %get-tuple-element.4), channel_id=1, replica_groups=mesh['grp'=8,'sp_0'=4,'sp_1'=4,'sp_2'=2] {'sp_0','sp_1','sp_2'}, dimensions={0} | all-to-all | bytes 262144 | tf_op jit(solution)/shard_map/all_to_all | solution.py:320
  92.4 1.4 %shard_map.201 = bf16[32,16,128]{2,1,0:T(8,128)(2,1)} custom-call(bf16[32,16,128]{2,1,0:T(8,128)(2,1)S(1)} %all_to_all.30.rows, bf16[256,128]{1,0:T(8,128)(2,1)S(1)} %copy-done.3, bf16[256,128]{1,0:T(8,128)(2,1)S(1)} %copy-done.4, bf16[128,256]{1,0:T(8,128)(2,1)S(1)} %copy-done.5, bf16[128,256]{1,0:T(8,128)(2,1)S(1)} %copy-done.6, ...), custom_call_target="tpu_custom_call" | custom-call | tf_op jit(solution)/shard_map/pallas_call | solution.py:127
  93.8 4.0 %all-to-all-start.5 = ((bf16[32,16,128]{2,1,0:T(8,128)(2,1)}), bf16[32,16,128]{2,1,0:T(8,128)(2,1)S(1)}, u32[]{:S(2)}, u32[]{:S(2)}) async-start(bf16[32,16,128]{2,1,0:T(8,128)(2,1)} %shard_map.201), calls=%async_computation.5 | async-start | bytes 262144 | tf_op jit(solution)/shard_map/all_to_all | solution.py:320
  97.8 0.6 multiply_add_fusion
  98.4 8.0 %all-to-all-done.5.arrived = bf16[32,16,128]{2,1,0:T(8,128)(2,1)S(1)} async-done(((bf16[32,16,128]{2,1,0:T(8,128)(2,1)}), bf16[32,16,128]{2,1,0:T(8,128)(2,1)S(1)}, u32[]{:S(2)}, u32[]{:S(2)}) %all-to-all-start.5) | async-done | bytes 131104 | tf_op jit(solution)/shard_map/all_to_all | solution.py:320
  106.5 0.0 copy-done.2
  106.5 0.7 shard_map.202
  (6 shorter events, 0.1 us)
Async XLA Ops:
  0.6 0.9 copy-start.1
  2.3 10.2 %copy-start.14 = (f32[1024]{0:T(1024)S(1)}, f32[1024]{0:T(1024)}, u32[]{:S(2)}) copy-start(f32[1024]{0:T(1024)} %param.23) | copy-start | bytes 12292
  2.3 18.7 %copy-start.6 = (bf16[128,256]{1,0:T(8,128)(2,1)S(1)}, bf16[128,256]{1,0:T(8,128)(2,1)}, u32[]{:S(2)}) copy-start(bf16[128,256]{1,0:T(8,128)(2,1)} %constant.31.clone.low_t) | copy-start | bytes 196612
  2.3 18.7 %all-to-all-start = ((bf16[32,16,128]{2,1,0:T(8,128)(2,1)}), bf16[32,16,128]{2,1,0:T(8,128)(2,1)S(1)}, u32[]{:S(2)}, u32[]{:S(2)}) async-start(bf16[32,16,128]{2,1,0:T(8,128)(2,1)} %shard_map.194), calls=%async_computation | async-start | bytes 262144 | tf_op jit(solution)/shard_map/all_to_all | solution.py:320
  12.6 8.5 %copy-start.7 = (f32[2,32,128]{2,1,0:T(8,128)S(1)}, f32[2,32,128]{2,1,0:T(8,128)}, u32[]{:S(2)}) copy-start(f32[2,32,128]{2,1,0:T(8,128)} %constant.32.clone.twiddle) | copy-start | bytes 98308
  12.7 8.3 %copy-start.5 = (bf16[128,256]{1,0:T(8,128)(2,1)S(1)}, bf16[128,256]{1,0:T(8,128)(2,1)}, u32[]{:S(2)}) copy-start(bf16[128,256]{1,0:T(8,128)(2,1)} %constant.30.clone.high_t) | copy-start | bytes 196612
  12.8 8.2 %copy-start.3 = (bf16[256,128]{1,0:T(8,128)(2,1)S(1)}, bf16[256,128]{1,0:T(8,128)(2,1)}, u32[]{:S(2)}) copy-start(bf16[256,128]{1,0:T(8,128)(2,1)} %constant.28.clone.high) | copy-start | bytes 196612
  12.8 8.2 %copy-start.4 = (bf16[256,128]{1,0:T(8,128)(2,1)S(1)}, bf16[256,128]{1,0:T(8,128)(2,1)}, u32[]{:S(2)}) copy-start(bf16[256,128]{1,0:T(8,128)(2,1)} %constant.29.clone.low) | copy-start | bytes 196612
  22.4 4.1 %copy-start.9 = (f32[3,4,128]{2,1,0:T(4,128)S(1)}, f32[3,4,128]{2,1,0:T(4,128)}, u32[]{:S(2)}) copy-start(f32[3,4,128]{2,1,0:T(4,128)} %control.1) | copy-start | bytes 18436
  22.4 4.1 %copy-start.10 = (s32[1024]{0:T(1024)S(1)}, s32[1024]{0:T(1024)}, u32[]{:S(2)}) copy-start(s32[1024]{0:T(1024)} %param.24) | copy-start | bytes 12292
  22.4 4.1 %copy-start.11 = (s32[1024]{0:T(1024)S(1)}, s32[1024]{0:T(1024)}, u32[]{:S(2)}) copy-start(s32[1024]{0:T(1024)} %param.25) | copy-start | bytes 12292
  22.4 4.1 %copy-start.12 = (f32[1024]{0:T(1024)S(1)}, f32[1024]{0:T(1024)}, u32[]{:S(2)}) copy-start(f32[1024]{0:T(1024)} %param.26) | copy-start | bytes 12292
  22.4 4.1 %copy-start.13 = (f32[1024]{0:T(1024)S(1)}, f32[1024]{0:T(1024)}, u32[]{:S(2)}) copy-start(f32[1024]{0:T(1024)} %param.27) | copy-start | bytes 12292
  22.4 12.7 %all-to-all-start.1 = ((bf16[32,16,128]{2,1,0:T(8,128)(2,1)}), bf16[32,16,128]{2,1,0:T(8,128)(2,1)S(1)}, u32[]{:S(2)}, u32[]{:S(2)}) async-start(bf16[32,16,128]{2,1,0:T(8,128)(2,1)} %shard_map.195), calls=%async_computation.1 | async-start | bytes 262144 | tf_op jit(solution)/shard_map/all_to_all | solution.py:320
  26.5 0.7 copy-start.8
  27.2 16.1 %copy-start = (bf16[10,3,32,128]{3,2,1,0:T(8,128)(2,1)S(1)}, bf16[10,3,32,128]{3,2,1,0:T(8,128)(2,1)}, u32[]{:S(2)}) copy-start(bf16[10,3,32,128]{3,2,1,0:T(8,128)(2,1)} %ensemble.3) | copy-start | bytes 737284
  35.1 17.7 %all-to-all-start.3 = ((f32[8,40,128]{2,1,0:T(8,128)}), f32[8,40,128]{2,1,0:T(8,128)S(1)}, u32[]{:S(2)}, u32[]{:S(2)}) async-start(f32[8,40,128]{2,1,0:T(8,128)} %shard_map.197), calls=%async_computation.3 | async-start | bytes 327680 | tf_op jit(solution)/shard_map/all_to_all | solution.py:320
  52.9 13.0 %all-to-all-start.2 = ((bf16[8,96,128]{2,1,0:T(8,128)(2,1)}), bf16[8,96,128]{2,1,0:T(8,128)(2,1)S(1)}, u32[]{:S(2)}, u32[]{:S(2)}) async-start(bf16[8,96,128]{2,1,0:T(8,128)(2,1)} %shard_map.196), calls=%async_computation.2 | async-start | bytes 393216 | tf_op jit(solution)/shard_map/all_to_all | solution.py:320
  56.3 12.7 %collective-permute-start.2 = (f32[6,32,128]{2,1,0:T(8,128)S(1)}, f32[6,32,128]{2,1,0:T(8,128)S(1)}, u32[]{:S(2)}, u32[]{:S(2)}) collective-permute-start(f32[6,32,128]{2,1,0:T(8,128)S(1)} %slice.8), channel_id=1, source_target_pairs={{0,1},{1,2},{2,3},{3,4},{4,5},{5,6},{6,7},{7,8},{8,9},{9,10},{10,1... | collective-permute-start | bytes 294920 | tf_op jit(solution)/shard_map/ppermute | solution.py:326
  58.3 10.8 %collective-permute-start.3 = (f32[6,32,128]{2,1,0:T(8,128)S(1)}, f32[6,32,128]{2,1,0:T(8,128)S(1)}, u32[]{:S(2)}, u32[]{:S(2)}) collective-permute-start(f32[6,32,128]{2,1,0:T(8,128)S(1)} %slice.8), channel_id=1, source_target_pairs={{1,0},{2,1},{3,2},{4,3},{5,4},{6,5},{7,6},{8,7},{9,8},{10,9},{11,1... | collective-permute-start | bytes 294920 | tf_op jit(solution)/shard_map/ppermute | solution.py:326
  65.9 4.3 %collective-permute-start = (f32[3,32,128]{2,1,0:T(8,128)S(1)}, f32[3,32,128]{2,1,0:T(8,128)S(1)}, u32[]{:S(2)}, u32[]{:S(2)}) collective-permute-start(f32[3,32,128]{2,1,0:T(8,128)S(1)} %shard_map.199.inc), channel_id=1, source_target_pairs={{0,1},{1,2},{2,3},{3,4},{4,5},{5,6},{6,7},{7,8},{8,9},{9,10},{10,1... | collective-permute-start | bytes 147464 | tf_op jit(solution)/shard_map/ppermute | solution.py:326
  69.1 3.5 %collective-permute-start.1 = (f32[3,32,128]{2,1,0:T(8,128)S(1)}, f32[3,32,128]{2,1,0:T(8,128)S(1)}, u32[]{:S(2)}, u32[]{:S(2)}) collective-permute-start(f32[3,32,128]{2,1,0:T(8,128)S(1)} %shard_map.199.inc), channel_id=1, source_target_pairs={{1,0},{2,1},{3,2},{4,3},{5,4},{6,5},{7,6},{8,7},{9,8},{10,9},{11,1... | collective-permute-start | bytes 147464 | tf_op jit(solution)/shard_map/ppermute | solution.py:326
  93.8 12.7 %copy-start.2 = (f32[10,32,128]{2,1,0:T(8,128)S(1)}, f32[10,32,128]{2,1,0:T(8,128)}, u32[]{:S(2)}) copy-start(f32[10,32,128]{2,1,0:T(8,128)} %alpha.1) | copy-start | bytes 491524
  93.8 12.7 %all-to-all-start.5 = ((bf16[32,16,128]{2,1,0:T(8,128)(2,1)}), bf16[32,16,128]{2,1,0:T(8,128)(2,1)S(1)}, u32[]{:S(2)}, u32[]{:S(2)}) async-start(bf16[32,16,128]{2,1,0:T(8,128)(2,1)} %shard_map.201), calls=%async_computation.5 | async-start | bytes 262144 | tf_op jit(solution)/shard_map/all_to_all | solution.py:320

commit v2 on v1

--- a/solution.py
+++ b/solution.py
@@ -1,3 +1,4 @@
+import functools
 import math
 
 import jax
@@ -22,7 +23,9 @@
 NX = BLOCKS * COLS
 KEEP = 1024
 ALPHAS = 2 * KEEP // BLOCKS
-FIELDS = 9
+RIM = 8
+SLOT_COUNT = COLS // 16
+EXTRA = MEM - SLOT_COUNT
 COURANT = 0.4
 
 F32 = jnp.float32
@@ -100,7 +103,17 @@
     return total + jnp.dot(xh, h, preferred_element_type=F32)
 
 
-def filter_rows(rows, high, low, high_t, low_t, twiddle, weights, out, wide, spec):
+def slot_of(shape):
+    lane = lax.broadcasted_iota(jnp.int32, shape, 1)
+    return jnp.right_shift(lane + RIM, 4) & (SLOT_COUNT - 1)
+
+
+def turned(x, by):
+    by = by % COLS
+    return x if by == 0 else pltpu.roll(x, by, 1)
+
+
+def filter_body(rims, rows, high, low, high_t, low_t, twiddle, weights, out, wide, spec, flat):
     def load(p):
         x = rows[p].astype(F32)
         return x[:8], x[8:]
@@ -119,15 +132,45 @@
         yr, yi = wide[8 * b : 8 * b + 8, :COLS], wide[8 * b : 8 * b + 8, COLS:]
         return yr * c - yi * s, yr * s + yi * c
 
-    for p, (yr, yi) in enumerate(fft(load_back, 0, 1, BLOCKS, 1)):
-        out[p] = jnp.concatenate([yr, yi], axis=0).astype(BF16)
-
-
-def localize(rows, weights):
+    blocks = fft(load_back, 0, 1, BLOCKS, 1)
+    if not rims:
+        for p, (yr, yi) in enumerate(blocks):
+            out[p] = jnp.concatenate([yr, yi], axis=0).astype(BF16)
+        return
+    for p, (yr, yi) in enumerate(blocks):
+        for place in {p + 1, 0 if p == BLOCKS - 1 else p + 1, BLOCKS + 1 if p == 0 else p + 1}:
+            flat[SLOTS * place : SLOTS * place + 8, :] = yr
+            flat[SLOTS * place + 8 : SLOTS * place + 16, :] = yi
+    slot = slot_of((BLOCKS, COLS))
+    right = (lax.broadcasted_iota(jnp.int32, (BLOCKS, COLS), 1) & 15) < RIM
+    first = jnp.zeros((BLOCKS, COLS), F32)
+    second = jnp.zeros((BLOCKS, COLS), F32)
+    for m in range(MEM):
+        before = flat[pl.ds(m, BLOCKS, stride=SLOTS), :]
+        after = flat[pl.ds(m + 2 * SLOTS, BLOCKS, stride=SLOTS), :]
+        if m < SLOT_COUNT:
+            rim = jnp.where(right, turned(after, 16 * m), turned(before, 16 * m))
+            first = jnp.where(slot == m, rim, first)
+        else:
+            for v in range(3):
+                q = EXTRA * v + m - SLOT_COUNT
+                rim = jnp.where(right, turned(after, 16 * q), turned(before, 16 * q))
+                second = jnp.where(slot == q, rim, second)
+    flat[pl.ds(SLOTS + MEM, BLOCKS, stride=SLOTS), :] = first
+    flat[pl.ds(SLOTS + MEM + 1, BLOCKS, stride=SLOTS), :] = second
+    for p in range(BLOCKS):
+        out[p] = flat[SLOTS * (p + 1) : SLOTS * (p + 2), :].astype(BF16)
+
+
+def localize(rows, weights, rims):
     return call(
-        filter_rows,
+        functools.partial(filter_body, rims),
         jax.ShapeDtypeStruct((BLOCKS, SLOTS, COLS), BF16),
-        [VMEM((8 * BLOCKS, 2 * COLS), F32), VMEM((8 * BLOCKS, COLS), F32)],
+        [
+            VMEM((8 * BLOCKS, 2 * COLS), F32),
+            VMEM((8 * BLOCKS, COLS), F32),
+            VMEM((SLOTS * (BLOCKS + 2), COLS), F32),
+        ],
         7,
     )(rows, *tables(), weights)
 
@@ -145,29 +188,70 @@
     )
 
 
-def contract(ensemble, arrived, out, flat):
+def contract(ensemble, arrived, from_low, from_high, tiles, out, flat):
+    own = lax.axis_index("grp")
+    unspread = math.sqrt(MEM * GROUPS - 1)
     flat[...] = arrived[...].astype(F32).reshape(ROWS * SLOTS, COLS)
     totals = [jnp.zeros((ROWS, COLS), F32)] * 3
     for m in range(MEM):
         field = flat[pl.ds(m, ROWS, stride=SLOTS), :]
         for v in range(3):
             totals[v] = totals[v] + ensemble[m, v].astype(F32) * field
+    right = (lax.broadcasted_iota(jnp.int32, (16, COLS), 1) & 15) < RIM
+
+    def rim(at, count):
+        return jnp.concatenate(
+            [
+                jnp.where(
+                    right,
+                    from_high[at + i : at + i + 16, :].astype(F32),
+                    from_low[at + i : at + i + 16, :].astype(F32),
+                )
+                for i in range(0, count, 16)
+            ],
+            axis=0,
+        )
+
+    slot = slot_of((ROWS, COLS))
+    first = flat[pl.ds(MEM, ROWS, stride=SLOTS), :]
+    second = flat[pl.ds(MEM + 1, ROWS, stride=SLOTS), :]
+    extra = rim(3 * ROWS, ROWS) * second
+    side = jnp.zeros((ROWS, COLS), F32)
     for v in range(3):
-        part = totals[v].astype(BF16)
+        t = rim(ROWS * v, ROWS) * first
+        t = t + jnp.where(jnp.right_shift(slot, 1) == v, extra, 0.0)
+        for by in (64, 32, 16):
+            t = t + turned(t, by)
+        side = jnp.where(slot == v, t, side)
+    obs_rim = rim(4 * ROWS, 16)
+    mine = jnp.right_shift(lax.broadcasted_iota(jnp.int32, (ROWS, COLS), 0), 2) == own
+
+    def on_own_rows(tile):
+        return jnp.where(mine, unspread * jnp.concatenate([tile] * GROUPS, axis=0), 0.0)
+
+    parts = [
+        (totals[v] + on_own_rows(tiles[24 + 4 * v : 28 + 4 * v, :])).astype(BF16)
+        for v in range(3)
+    ]
+    parts.append((side + on_own_rows(obs_rim[4:8])).astype(BF16))
+    parts.append(
+        jnp.concatenate([tiles[:24, :], obs_rim[:4], jnp.zeros((4, COLS), F32)], axis=0).astype(BF16)
+    )
+    for i, part in enumerate(parts):
         for g in range(GROUPS):
-            out[g, ROWS * v : ROWS * v + ROWS, :] = part
-
-
-def partial_sums(ensemble, arrived):
+            out[g, ROWS * i : ROWS * i + ROWS, :] = part
+
+
+def partial_sums(ensemble, arrived, from_low, from_high, tiles):
     return call(
         contract,
-        jax.ShapeDtypeStruct((GROUPS, 3 * ROWS, COLS), BF16),
+        jax.ShapeDtypeStruct((GROUPS, 5 * ROWS, COLS), BF16),
         [VMEM((ROWS * SLOTS, COLS), F32)],
-        2,
-    )(ensemble, arrived)
-
-
-def observe(cell, step, innovation, weight, std, control, out):
+        5,
+    )(ensemble, arrived, from_low, from_high, tiles)
+
+
+def observe(cell, step, innovation, weight, std, control, ensemble, tiles, edges):
     where_row = jnp.right_shift(cell[...], 12) & (TILE_ROWS - 1)
     key = step[...] * TILE_ROWS + where_row
     column = cell[...] & (COLS - 1)
@@ -187,50 +271,62 @@
         total = total + lax.dot_general(
             piece, hot, (((1,), (1,)), ((), ())), preferred_element_type=F32
         )
+    static = [std[v] * control[v] for v in range(3)]
+    tiles[:24, :] = total
+    for v in range(3):
+        tiles[24 + 4 * v : 28 + 4 * v, :] = static[v]
+    slot = slot_of((ROWS, COLS))
+    extra = jnp.zeros((ROWS, COLS), F32)
+    for v in range(3):
+        packed = jnp.zeros((ROWS, COLS), F32)
+        for m in range(SLOT_COUNT):
+            packed = jnp.where(slot == m, turned(ensemble[m, v].astype(F32), 16 * m), packed)
+        edges[ROWS * v : ROWS * v + ROWS, :] = packed.astype(BF16)
+        for m in range(SLOT_COUNT, MEM):
+            q = EXTRA * v + m - SLOT_COUNT
+            extra = jnp.where(slot == q, turned(ensemble[m, v].astype(F32), 16 * q), extra)
+    edges[3 * ROWS : 4 * ROWS, :] = extra.astype(BF16)
+    slot = slot_of((TILE_ROWS, COLS))
+    sums = jnp.zeros((TILE_ROWS, COLS), F32)
+    for f in range(6):
+        sums = jnp.where(slot == f, turned(total[4 * f : 4 * f + 4], 16 * f), sums)
+    product_rim = jnp.zeros((TILE_ROWS, COLS), F32)
+    for v in range(3):
+        product_rim = jnp.where(slot == v, turned(static[v], 16 * v), product_rim)
+    pad = jnp.zeros((8, COLS), F32)
+    edges[4 * ROWS :, :] = jnp.concatenate([sums, product_rim, pad], axis=0).astype(BF16)
+
+
+def tile_fields(cell, step, innovation, weight, std, control, ensemble):
+    flat = [a.reshape(1, -1) for a in (cell, step, innovation, weight)]
+    return call(
+        observe,
+        [
+            jax.ShapeDtypeStruct((36, COLS), F32),
+            jax.ShapeDtypeStruct((4 * ROWS + 16, COLS), BF16),
+        ],
+        (),
+        7,
+    )(*flat, std, control, ensemble)
+
+
+def window(arrived, ensemble, sent, adj, flat, sums):
+    spread = 1.0 / math.sqrt(MEM * GROUPS - 1)
+    parts = []
+    for i in range(4):
+        total = arrived[0, ROWS * i : ROWS * i + ROWS, :].astype(F32)
+        for g in range(1, GROUPS):
+            total = total + arrived[g, ROWS * i : ROWS * i + ROWS, :].astype(F32)
+        parts.append(spread * total)
     for g in range(GROUPS):
-        out[g, : 2 * n, :] = total
-        for v in range(3):
-            out[g, 2 * n + 4 * v : 2 * n + 4 * v + 4, :] = std[v] * control[v]
-        out[g, 36:40, :] = jnp.zeros((4, COLS), F32)
-
-
-def tile_fields(cell, step, innovation, weight, std, control):
-    flat = [a.reshape(1, -1) for a in (cell, step, innovation, weight)]
-    return call(observe, jax.ShapeDtypeStruct((GROUPS, 40, COLS), F32), (), 6)(
-        *flat, std, control
-    )
-
-
-def stack_rows(arrived, out):
-    for f in range(FIELDS):
-        for g in range(GROUPS):
-            out[f, TILE_ROWS * g : TILE_ROWS * g + TILE_ROWS, :] = arrived[
-                g, TILE_ROWS * f : TILE_ROWS * f + TILE_ROWS, :
-            ]
-
-
-def all_rows(arrived):
-    return call(stack_rows, jax.ShapeDtypeStruct((FIELDS, ROWS, COLS), F32))(arrived)
-
-
-def add_groups(arrived, fields, out):
-    spread = 1.0 / math.sqrt(MEM * GROUPS - 1)
-    for v in range(3):
-        total = arrived[0, ROWS * v : ROWS * v + ROWS, :].astype(F32)
-        for g in range(1, GROUPS):
-            total = total + arrived[g, ROWS * v : ROWS * v + ROWS, :].astype(F32)
-        out[v] = spread * total + fields[6 + v]
-
-
-def increments(arrived, fields):
-    return call(add_groups, jax.ShapeDtypeStruct((3, ROWS, COLS), F32), (), 2)(arrived, fields)
-
-
-def window(inc, inc_low, inc_high, fields, f_low, f_high, ensemble, sent, adj, flat):
+        x = arrived[g, 4 * ROWS : 5 * ROWS, :].astype(F32)
+        for f in range(7):
+            sums[f, TILE_ROWS * g : TILE_ROWS * g + TILE_ROWS, :] = x[4 * f : 4 * f + 4]
     lane = lax.broadcasted_iota(jnp.int32, (ROWS, COLS), 1)
-
-    def wide(main, low, high):
-        rim = jnp.where(lane < 8, high, jnp.where(lane >= COLS - 8, low, 0.0))
+    used = jnp.logical_or(lane < RIM, lane >= COLS - RIM)
+
+    def wide(main, packed, place):
+        rim = jnp.where(used, turned(packed, -16 * place), 0.0)
         return jnp.concatenate([main, rim], axis=1)
 
     row = lax.broadcasted_iota(jnp.int32, (ROWS, 2 * COLS), 0)
@@ -255,11 +351,11 @@
         a = bh + (dx(bu) + dy(bw))
         return a, bu - rotation * bw + dx(a), bw + rotation * bu + dy(a)
 
-    state = tuple(wide(inc[v], inc_low[v], inc_high[v]) for v in range(3))
+    state = tuple(wide(parts[v], parts[3], v) for v in range(3))
     forcing = []
     for t in range(3):
-        w_t = wide(fields[t], f_low[t], f_high[t])
-        v_t = wide(fields[3 + t], f_low[3 + t], f_high[3 + t])
+        w_t = wide(sums[t], sums[6], t)
+        v_t = wide(sums[3 + t], sums[6], 3 + t)
         forcing.append(w_t * state[0] - v_t)
         if t < 2:
             state = forward(*state)
@@ -278,16 +374,16 @@
     by_row(flat, sent)
 
 
-def assimilate(inc, inc_low, inc_high, fields, f_low, f_high, ensemble):
+def assimilate(arrived, ensemble):
     return call(
         window,
         [
             jax.ShapeDtypeStruct((ROWS, SLOTS, COLS), BF16),
             jax.ShapeDtypeStruct((3, ROWS, COLS), F32),
         ],
-        [VMEM((MEM * ROWS, COLS), F32)],
-        7,
-    )(inc, inc_low, inc_high, fields, f_low, f_high, ensemble)
+        [VMEM((MEM * ROWS, COLS), F32), VMEM((7, ROWS, COLS), F32)],
+        2,
+    )(arrived, ensemble)
 
 
 def add_alpha(alpha, arrived, out, flat):
@@ -331,19 +427,18 @@
 ):
     first_row = lax.axis_index("grp") * TILE_ROWS
     rows = swap(to_send(alpha), SP)
-    tiles = tile_fields(obs_cell, obs_step, innovation, obs_weight, static_std, control)
+    tiles, edges = tile_fields(
+        obs_cell, obs_step, innovation, obs_weight, static_std, control, ensemble
+    )
+    from_low, from_high = neighbours(edges)
     weights = wave_weights(loc_spectrum)
-    localized = swap(localize(rows, weights), SP)
-    fields = all_rows(swap(tiles, "grp"))
-    f_low, f_high = neighbours(fields[:6])
-    summed = swap(partial_sums(ensemble, localized), "grp")
-    inc = increments(summed, fields)
-    inc_low, inc_high = neighbours(inc)
-    sent, adjoint = assimilate(inc, inc_low, inc_high, fields, f_low, f_high, ensemble)
+    localized = swap(localize(rows, weights, True), SP)
+    summed = swap(partial_sums(ensemble, localized, from_low, from_high, tiles), "grp")
+    sent, adjoint = assimilate(summed, ensemble)
     weighted = swap(sent, SP)
     mine = lax.dynamic_slice_in_dim(adjoint, first_row, TILE_ROWS, axis=1)
     grad_control = control + static_std * mine
-    filtered = swap(localize(weighted, weights), SP)
+    filtered = swap(localize(weighted, weights, False), SP)
     return finish(alpha, filtered), grad_control
 
 

time: 108 us -> 87.9 us (0.81)
  waiting for transfers between devices: 42.8 us -> 22.3 us
  blocking collectives: 19.2 us -> 35.6 us
  starting transfers between devices: 34.8 us -> 19.9 us
    all_to_all x5 -> x3, waiting for transfers between devices: 39.3 us -> 18.6 us  [swap(): return lax.all_to_all(x, axis, split_axis=0, concat_axis=0, tiled=True)]
    all_to_all x1 -> x2, blocking collectives: 19.2 us -> 35.6 us  [swap(): return lax.all_to_all(x, axis, split_axis=0, concat_axis=0, tiled=True)]
    all_to_all x5 -> x3, starting transfers between devices: 29.7 us -> 18.2 us  [swap(): return lax.all_to_all(x, axis, split_axis=0, concat_axis=0, tiled=True)]
    ppermute x4 -> x2, starting transfers between devices: 5.11 us -> 1.69 us  [neighbours(): return (lax.ppermute(x, SP, ahead), lax.ppermute(x, SP, back))]
    pallas_call x6 -> x4, Pallas kernels: 4.66 us -> 3.67 us  [the longest x2 2.93 us: localize(): call(functools.partial(filter_body, rims), jax.ShapeDtypeStruct((BLOCKS,...]
    ppermute x4 -> x2, waiting for transfers between devices: 3.51 us -> 3.72 us  [neighbours(): return (lax.ppermute(x, SP, ahead), lax.ppermute(x, SP, back))]
  transfers between devices with their start and end apart: 9 -> 5, of which waited for: 7 -> 5; matrix products, arithmetic and copies ran while one was open for 1% -> 1% of each run, Pallas kernels for 2% -> 1%
where the time goes in v2:
time: 87.9 us; the launch traced here: 87.4 us
  blocking collectives  35.6 us (41%)
  waiting for transfers between devices  22.3 us (25%)
  starting transfers between devices  19.9 us (23%)
  Pallas kernels  5.89 us (7%)
  local copies, waits for them, and re-layouts  1.89 us (2%)
  other arithmetic  0.91 us (1%)
    all_to_all x2, blocking collectives, swap(): return lax.all_to_all(x, axis, split_axis=0, concat_axis=0, tiled=True)  35.6 us
    all_to_all x3, waiting for transfers between devices, swap(): return lax.all_to_all(x, axis, split_axis=0, concat_axis=0, tiled=True)  18.6 us
    all_to_all x3, starting transfers between devices, swap(): return lax.all_to_all(x, axis, split_axis=0, concat_axis=0, tiled=True)  18.2 us
    ppermute x2, waiting for transfers between devices, neighbours(): return (lax.ppermute(x, SP, ahead), lax.ppermute(x, SP, back))  3.72 us
    pallas_call x2, Pallas kernels, localize(): call(functools.partial(filter_body, rims), jax.ShapeDtypeStruct((BLOCKS,...  2.93 us
  transfers between devices with their start and end apart: 5, of which 5 were waited for; matrix products, arithmetic and copies ran while one was open for 1% of the time, Pallas kernels for 1%

profile of v2, /device:TPU:1, one launch (start us, length us, event | category | flops | bytes accessed | tf_op | source)
XLA Modules:
  0.0 87.4 jit_solution(16773712470109353920)
XLA Ops:
  0.6 0.0 copy-start.1
  0.6 0.9 %copy-done.1 = f32[10,32,128]{2,1,0:T(8,128)S(1)} copy-done((f32[10,32,128]{2,1,0:T(8,128)S(1)}, f32[10,32,128]{2,1,0:T(8,128)}, u32[]{:S(2)}) %copy-start.1) | copy-done | bytes 163864
  1.5 0.8 shard_map.194
  2.3 0.0 copy-start.14
  2.3 0.0 copy-start.6
  2.3 10.2 %all-to-all-start = ((bf16[32,16,128]{2,1,0:T(8,128)(2,1)}), bf16[32,16,128]{2,1,0:T(8,128)(2,1)S(1)}, u32[]{:S(2)}, u32[]{:S(2)}) async-start(bf16[32,16,128]{2,1,0:T(8,128)(2,1)} %shard_map.194), calls=%async_computation | async-start | bytes 262144 | tf_op jit(solution)/shard_map/all_to_all | solution.py:416
  12.5 0.0 copy-done.14
  12.5 0.1 slice_multiply_fusion
  12.6 0.0 copy-start.7
  12.6 0.1 pad_maximum_fusion.1
  12.6 0.1 reshape.27
  12.7 0.0 copy-start.5
  12.7 0.1 copy.21
  12.8 0.0 copy-start.3
  12.8 0.0 copy-start.4
  12.8 0.1 reshape.26
  12.9 0.1 copy.22
  13.0 0.1 maximum_bitcast_fusion
  13.0 0.1 pad_maximum_fusion.weights
  13.1 7.9 %all-to-all-done.rows = bf16[32,16,128]{2,1,0:T(8,128)(2,1)S(1)} async-done(((bf16[32,16,128]{2,1,0:T(8,128)(2,1)}), bf16[32,16,128]{2,1,0:T(8,128)(2,1)S(1)}, u32[]{:S(2)}, u32[]{:S(2)}) %all-to-all-start) | async-done | bytes 131104 | tf_op jit(solution)/shard_map/all_to_all | solution.py:416
  21.0 0.0 copy-done.6
  21.0 0.0 copy-done.7
  21.0 0.0 copy-done.5
  21.0 0.0 copy-done.3
  21.0 0.0 copy-done.4
  21.0 0.0 copy-start.12
  21.1 0.0 copy-start.13
  21.1 1.6 %shard_map.195 = bf16[32,16,128]{2,1,0:T(8,128)(2,1)} custom-call(bf16[32,16,128]{2,1,0:T(8,128)(2,1)S(1)} %all-to-all-done.rows, bf16[256,128]{1,0:T(8,128)(2,1)S(1)} %copy-done.3, bf16[256,128]{1,0:T(8,128)(2,1)S(1)} %copy-done.4, bf16[128,256]{1,0:T(8,128)(2,1)S(1)} %copy-done.5, bf16[128,256]{1,0:T(8,128)(2,1)S(1)} %copy-done.6, ...), custom_call_target="tpu_custom_call" | custom-call | tf_op jit(solution)/shard_map/pallas_call | solution.py:166
  22.6 0.0 copy-start
  22.6 0.0 copy-start.9
  22.6 0.0 copy-start.10
  22.6 0.0 copy-start.11
  22.6 4.0 %all-to-all-start.1 = ((bf16[32,16,128]{2,1,0:T(8,128)(2,1)}), bf16[32,16,128]{2,1,0:T(8,128)(2,1)S(1)}, u32[]{:S(2)}, u32[]{:S(2)}) async-start(bf16[32,16,128]{2,1,0:T(8,128)(2,1)} %shard_map.195), calls=%async_computation.1 | async-start | bytes 262144 | tf_op jit(solution)/shard_map/all_to_all | solution.py:416
  26.7 0.0 copy-start.8
  26.7 0.0 copy-done.12
  26.7 0.0 copy-done.13
  26.7 0.0 copy-done
  26.7 0.0 copy-done.9
  26.7 0.0 copy-done.10
  26.8 0.0 copy-done.11
  26.8 0.6 copy-done.8
  27.4 0.5 shard_map.196
  27.9 1.7 %collective-permute-start = (bf16[144,128]{1,0:T(8,128)(2,1)S(1)}, bf16[144,128]{1,0:T(8,128)(2,1)S(1)}, u32[]{:S(2)}, u32[]{:S(2)}) collective-permute-start(bf16[144,128]{1,0:T(8,128)(2,1)S(1)} %get-tuple-element.6), channel_id=1, source_target_pairs={{0,1},{1,2},{2,3},{3,4},{4,5},{5,6},{6,7},{7,8},{8,9},{9,10},{10,1... | collective-permute-start | bytes 110600 | tf_op jit(solution)/shard_map/ppermute | solution.py:422
  29.6 0.0 collective-permute-start.1
  29.6 1.1 %collective-permute-done.from_low = bf16[144,128]{1,0:T(8,128)(2,1)S(1)} collective-permute-done((bf16[144,128]{1,0:T(8,128)(2,1)S(1)}, bf16[144,128]{1,0:T(8,128)(2,1)S(1)}, u32[]{:S(2)}, u32[]{:S(2)}) %collective-permute-start) | collective-permute-done | bytes 36896 | tf_op jit(solution)/shard_map/ppermute | solution.py:422
  30.6 2.7 %collective-permute-done.1.from_high = bf16[144,128]{1,0:T(8,128)(2,1)S(1)} collective-permute-done((bf16[144,128]{1,0:T(8,128)(2,1)S(1)}, bf16[144,128]{1,0:T(8,128)(2,1)S(1)}, u32[]{:S(2)}, u32[]{:S(2)}) %collective-permute-start.1) | collective-permute-done | bytes 36896 | tf_op jit(solution)/shard_map/ppermute | solution.py:422
  33.3 2.7 %all-to-all-done.1.arrived = bf16[32,16,128]{2,1,0:T(8,128)(2,1)S(1)} async-done(((bf16[32,16,128]{2,1,0:T(8,128)(2,1)}), bf16[32,16,128]{2,1,0:T(8,128)(2,1)S(1)}, u32[]{:S(2)}, u32[]{:S(2)}) %all-to-all-start.1) | async-done | bytes 131104 | tf_op jit(solution)/shard_map/all_to_all | solution.py:416
  35.9 0.3 shard_map.197
  36.2 19.3 %all_to_all.25.arrived = bf16[8,160,128]{2,1,0:T(8,128)(2,1)S(1)} all-to-all(bf16[8,160,128]{2,1,0:T(8,128)(2,1)S(1)} %shard_map.197), channel_id=1, replica_groups=mesh['grp'=8,'sp_0'=4,'sp_1'=4,'sp_2'=2] {'grp'}, dimensions={0} | all-to-all | bytes 655360 | tf_op jit(solution)/shard_map/all_to_all | solution.py:416
  55.5 0.7 shard_map.198
  56.3 16.3 %all_to_all.26.rows = bf16[32,16,128]{2,1,0:T(8,128)(2,1)S(1)} all-to-all(bf16[32,16,128]{2,1,0:T(8,128)(2,1)S(1)} %get-tuple-element.8), channel_id=1, replica_groups=mesh['grp'=8,'sp_0'=4,'sp_1'=4,'sp_2'=2] {'sp_0','sp_1','sp_2'}, dimensions={0} | all-to-all | bytes 262144 | tf_op jit(solution)/shard_map/all_to_all | solution.py:416
  72.6 1.4 %shard_map.199 = bf16[32,16,128]{2,1,0:T(8,128)(2,1)} custom-call(bf16[32,16,128]{2,1,0:T(8,128)(2,1)S(1)} %all_to_all.26.rows, bf16[256,128]{1,0:T(8,128)(2,1)S(1)} %copy-done.3, bf16[256,128]{1,0:T(8,128)(2,1)S(1)} %copy-done.4, bf16[128,256]{1,0:T(8,128)(2,1)S(1)} %copy-done.5, bf16[128,256]{1,0:T(8,128)(2,1)S(1)} %copy-done.6, ...), custom_call_target="tpu_custom_call" | custom-call | tf_op jit(solution)/shard_map/pallas_call | solution.py:166
  73.9 0.0 copy-start.2
  73.9 4.0 %all-to-all-start.4 = ((bf16[32,16,128]{2,1,0:T(8,128)(2,1)}), bf16[32,16,128]{2,1,0:T(8,128)(2,1)S(1)}, u32[]{:S(2)}, u32[]{:S(2)}) async-start(bf16[32,16,128]{2,1,0:T(8,128)(2,1)} %shard_map.199), calls=%async_computation.4 | async-start | bytes 262144 | tf_op jit(solution)/shard_map/all_to_all | solution.py:416
  78.0 0.6 multiply_add_fusion
  78.6 8.0 %all-to-all-done.4.arrived = bf16[32,16,128]{2,1,0:T(8,128)(2,1)S(1)} async-done(((bf16[32,16,128]{2,1,0:T(8,128)(2,1)}), bf16[32,16,128]{2,1,0:T(8,128)(2,1)S(1)}, u32[]{:S(2)}, u32[]{:S(2)}) %all-to-all-start.4) | async-done | bytes 131104 | tf_op jit(solution)/shard_map/all_to_all | solution.py:416
  86.6 0.0 copy-done.2
  86.6 0.7 shard_map.200
  (2 shorter events, 0.0 us)
Async XLA Ops:
  0.6 0.9 %copy-start.1 = (f32[10,32,128]{2,1,0:T(8,128)S(1)}, f32[10,32,128]{2,1,0:T(8,128)}, u32[]{:S(2)}) copy-start(f32[10,32,128]{2,1,0:T(8,128)} %alpha.1) | copy-start | bytes 491524
  2.3 10.2 %copy-start.14 = (f32[1024]{0:T(1024)S(1)}, f32[1024]{0:T(1024)}, u32[]{:S(2)}) copy-start(f32[1024]{0:T(1024)} %param.23) | copy-start | bytes 12292
  2.3 18.7 %copy-start.6 = (bf16[128,256]{1,0:T(8,128)(2,1)S(1)}, bf16[128,256]{1,0:T(8,128)(2,1)}, u32[]{:S(2)}) copy-start(bf16[128,256]{1,0:T(8,128)(2,1)} %constant.31.clone.low_t) | copy-start | bytes 196612
  2.3 18.7 %all-to-all-start = ((bf16[32,16,128]{2,1,0:T(8,128)(2,1)}), bf16[32,16,128]{2,1,0:T(8,128)(2,1)S(1)}, u32[]{:S(2)}, u32[]{:S(2)}) async-start(bf16[32,16,128]{2,1,0:T(8,128)(2,1)} %shard_map.194), calls=%async_computation | async-start | bytes 262144 | tf_op jit(solution)/shard_map/all_to_all | solution.py:416
  12.6 8.5 %copy-start.7 = (f32[2,32,128]{2,1,0:T(8,128)S(1)}, f32[2,32,128]{2,1,0:T(8,128)}, u32[]{:S(2)}) copy-start(f32[2,32,128]{2,1,0:T(8,128)} %constant.32.clone.twiddle) | copy-start | bytes 98308
  12.7 8.3 %copy-start.5 = (bf16[128,256]{1,0:T(8,128)(2,1)S(1)}, bf16[128,256]{1,0:T(8,128)(2,1)}, u32[]{:S(2)}) copy-start(bf16[128,256]{1,0:T(8,128)(2,1)} %constant.30.clone.high_t) | copy-start | bytes 196612
  12.8 8.2 %copy-start.3 = (bf16[256,128]{1,0:T(8,128)(2,1)S(1)}, bf16[256,128]{1,0:T(8,128)(2,1)}, u32[]{:S(2)}) copy-start(bf16[256,128]{1,0:T(8,128)(2,1)} %constant.28.clone.high) | copy-start | bytes 196612
  12.8 8.2 %copy-start.4 = (bf16[256,128]{1,0:T(8,128)(2,1)S(1)}, bf16[256,128]{1,0:T(8,128)(2,1)}, u32[]{:S(2)}) copy-start(bf16[256,128]{1,0:T(8,128)(2,1)} %constant.29.clone.low) | copy-start | bytes 196612
  21.0 5.7 %copy-start.12 = (f32[1024]{0:T(1024)S(1)}, f32[1024]{0:T(1024)}, u32[]{:S(2)}) copy-start(f32[1024]{0:T(1024)} %param.26) | copy-start | bytes 12292
  21.1 5.7 %copy-start.13 = (f32[1024]{0:T(1024)S(1)}, f32[1024]{0:T(1024)}, u32[]{:S(2)}) copy-start(f32[1024]{0:T(1024)} %param.27) | copy-start | bytes 12292
  22.6 4.1 %copy-start = (bf16[10,3,32,128]{3,2,1,0:T(8,128)(2,1)S(1)}, bf16[10,3,32,128]{3,2,1,0:T(8,128)(2,1)}, u32[]{:S(2)}) copy-start(bf16[10,3,32,128]{3,2,1,0:T(8,128)(2,1)} %ensemble.5) | copy-start | bytes 737284
  22.6 4.1 %copy-start.9 = (f32[3,4,128]{2,1,0:T(4,128)S(1)}, f32[3,4,128]{2,1,0:T(4,128)}, u32[]{:S(2)}) copy-start(f32[3,4,128]{2,1,0:T(4,128)} %control.1) | copy-start | bytes 18436
  22.6 4.1 %copy-start.10 = (s32[1024]{0:T(1024)S(1)}, s32[1024]{0:T(1024)}, u32[]{:S(2)}) copy-start(s32[1024]{0:T(1024)} %param.24) | copy-start | bytes 12292
  22.6 4.1 %copy-start.11 = (s32[1024]{0:T(1024)S(1)}, s32[1024]{0:T(1024)}, u32[]{:S(2)}) copy-start(s32[1024]{0:T(1024)} %param.25) | copy-start | bytes 12292
  22.6 13.3 %all-to-all-start.1 = ((bf16[32,16,128]{2,1,0:T(8,128)(2,1)}), bf16[32,16,128]{2,1,0:T(8,128)(2,1)S(1)}, u32[]{:S(2)}, u32[]{:S(2)}) async-start(bf16[32,16,128]{2,1,0:T(8,128)(2,1)} %shard_map.195), calls=%async_computation.1 | async-start | bytes 262144 | tf_op jit(solution)/shard_map/all_to_all | solution.py:416
  26.7 0.7 copy-start.8
  27.9 2.8 %collective-permute-start = (bf16[144,128]{1,0:T(8,128)(2,1)S(1)}, bf16[144,128]{1,0:T(8,128)(2,1)S(1)}, u32[]{:S(2)}, u32[]{:S(2)}) collective-permute-start(bf16[144,128]{1,0:T(8,128)(2,1)S(1)} %get-tuple-element.6), channel_id=1, source_target_pairs={{0,1},{1,2},{2,3},{3,4},{4,5},{5,6},{6,7},{7,8},{8,9},{9,10},{10,1... | collective-permute-start | bytes 110600 | tf_op jit(solution)/shard_map/ppermute | solution.py:422
  29.6 3.7 %collective-permute-start.1 = (bf16[144,128]{1,0:T(8,128)(2,1)S(1)}, bf16[144,128]{1,0:T(8,128)(2,1)S(1)}, u32[]{:S(2)}, u32[]{:S(2)}) collective-permute-start(bf16[144,128]{1,0:T(8,128)(2,1)S(1)} %get-tuple-element.6), channel_id=1, source_target_pairs={{1,0},{2,1},{3,2},{4,3},{5,4},{6,5},{7,6},{8,7},{9,8},{10,9},{11,1... | collective-permute-start | bytes 110600 | tf_op jit(solution)/shard_map/ppermute | solution.py:422
  73.9 12.7 %copy-start.2 = (f32[10,32,128]{2,1,0:T(8,128)S(1)}, f32[10,32,128]{2,1,0:T(8,128)}, u32[]{:S(2)}) copy-start(f32[10,32,128]{2,1,0:T(8,128)} %alpha.1) | copy-start | bytes 491524
  73.9 12.7 %all-to-all-start.4 = ((bf16[32,16,128]{2,1,0:T(8,128)(2,1)}), bf16[32,16,128]{2,1,0:T(8,128)(2,1)S(1)}, u32[]{:S(2)}, u32[]{:S(2)}) async-start(bf16[32,16,128]{2,1,0:T(8,128)(2,1)} %shard_map.199), calls=%async_computation.4 | async-start | bytes 262144 | tf_op jit(solution)/shard_map/all_to_all | solution.py:416

commit v3 on v2

--- a/solution.py
+++ b/solution.py
@@ -113,7 +113,31 @@
     return x if by == 0 else pltpu.roll(x, by, 1)
 
 
-def filter_body(rims, rows, high, low, high_t, low_t, twiddle, weights, out, wide, spec, flat):
+def pack_slots(field, count):
+    slot = slot_of((count, COLS))
+    first = jnp.zeros((count, COLS), F32)
+    for m in range(SLOT_COUNT):
+        first = jnp.where(slot == m, turned(field(m), 16 * m), first)
+    return first
+
+
+def pack_extra(field, count):
+    slot = slot_of((count, COLS))
+    extra = jnp.zeros((count, COLS), F32)
+    for v in range(3):
+        for i in range(EXTRA):
+            q = EXTRA * v + i
+            extra = jnp.where(slot == q, turned(field(SLOT_COUNT + i, v), 16 * q), extra)
+    return extra
+
+
+def filter_body(rims, *refs):
+    rows, high, low, high_t, low_t, twiddle, weights = refs[:7]
+    if rims:
+        edges, out, wide, spec, flat, arrived = refs[7:]
+    else:
+        out, wide, spec = refs[7:]
+
     def load(p):
         x = rows[p].astype(F32)
         return x[:8], x[8:]
@@ -137,42 +161,45 @@
         for p, (yr, yi) in enumerate(blocks):
             out[p] = jnp.concatenate([yr, yi], axis=0).astype(BF16)
         return
+    arrived[...] = rows[...].astype(F32).reshape(BLOCKS * SLOTS, COLS)
     for p, (yr, yi) in enumerate(blocks):
-        for place in {p + 1, 0 if p == BLOCKS - 1 else p + 1, BLOCKS + 1 if p == 0 else p + 1}:
-            flat[SLOTS * place : SLOTS * place + 8, :] = yr
-            flat[SLOTS * place + 8 : SLOTS * place + 16, :] = yi
+        flat[SLOTS * p : SLOTS * p + 8, :] = yr
+        flat[SLOTS * p + 8 : SLOTS * p + 16, :] = yi
+
+    def every(source, place):
+        return source[pl.ds(place, BLOCKS, stride=SLOTS), :]
+
+    first = pack_slots(lambda m: every(flat, m), BLOCKS)
+    extra = pack_extra(lambda m, v: every(flat, m), BLOCKS)
+    extra = extra * every(arrived, MEM + 3)
     slot = slot_of((BLOCKS, COLS))
     right = (lax.broadcasted_iota(jnp.int32, (BLOCKS, COLS), 1) & 15) < RIM
-    first = jnp.zeros((BLOCKS, COLS), F32)
-    second = jnp.zeros((BLOCKS, COLS), F32)
-    for m in range(MEM):
-        before = flat[pl.ds(m, BLOCKS, stride=SLOTS), :]
-        after = flat[pl.ds(m + 2 * SLOTS, BLOCKS, stride=SLOTS), :]
-        if m < SLOT_COUNT:
-            rim = jnp.where(right, turned(after, 16 * m), turned(before, 16 * m))
-            first = jnp.where(slot == m, rim, first)
-        else:
-            for v in range(3):
-                q = EXTRA * v + m - SLOT_COUNT
-                rim = jnp.where(right, turned(after, 16 * q), turned(before, 16 * q))
-                second = jnp.where(slot == q, rim, second)
-    flat[pl.ds(SLOTS + MEM, BLOCKS, stride=SLOTS), :] = first
-    flat[pl.ds(SLOTS + MEM + 1, BLOCKS, stride=SLOTS), :] = second
+    side = jnp.zeros((BLOCKS, COLS), F32)
+    for v in range(3):
+        t = first * every(arrived, MEM + v)
+        t = t + jnp.where(jnp.right_shift(slot, 1) == v, extra, 0.0)
+        for by in (64, 32, 16):
+            t = t + turned(t, by)
+        side = jnp.where(slot == v, t, side)
+    side = jnp.where(right, pltpu.roll(side, BLOCKS - 1, 0), pltpu.roll(side, 1, 0))
+    flat[pl.ds(MEM, BLOCKS, stride=SLOTS), :] = side
+    own_edges = edges[:5, :]
     for p in range(BLOCKS):
-        out[p] = flat[SLOTS * (p + 1) : SLOTS * (p + 2), :].astype(BF16)
-
-
-def localize(rows, weights, rims):
+        flat[SLOTS * p + MEM + 1 : SLOTS * p + SLOTS, :] = own_edges
+        out[p] = flat[SLOTS * p : SLOTS * p + SLOTS, :].astype(BF16)
+
+
+def localize(rows, weights, edges=None):
+    rims = edges is not None
+    scratch = [VMEM((8 * BLOCKS, 2 * COLS), F32), VMEM((8 * BLOCKS, COLS), F32)]
+    if rims:
+        scratch += [VMEM((SLOTS * BLOCKS, COLS), F32)] * 2
     return call(
         functools.partial(filter_body, rims),
         jax.ShapeDtypeStruct((BLOCKS, SLOTS, COLS), BF16),
-        [
-            VMEM((8 * BLOCKS, 2 * COLS), F32),
-            VMEM((8 * BLOCKS, COLS), F32),
-            VMEM((SLOTS * (BLOCKS + 2), COLS), F32),
-        ],
-        7,
-    )(rows, *tables(), weights)
+        scratch,
+        8 if rims else 7,
+    )(rows, *tables(), weights, *([edges] if rims else []))
 
 
 def by_row(flat, out):
@@ -182,14 +209,33 @@
         out[y] = x.astype(BF16)
 
 
-def to_send(alpha):
-    return call(by_row, jax.ShapeDtypeStruct((ROWS, SLOTS, COLS), BF16))(
-        alpha.reshape(MEM * ROWS, COLS)
-    )
-
-
-def contract(ensemble, arrived, from_low, from_high, tiles, out, flat):
+def send_body(alpha, ensemble, out, flat):
+    for m in range(MEM):
+        flat[pl.ds(m, ROWS, stride=SLOTS), :] = alpha[m]
+    for v in range(3):
+        flat[pl.ds(MEM + v, ROWS, stride=SLOTS), :] = pack_slots(
+            lambda m: ensemble[m, v].astype(F32), ROWS
+        )
+    flat[pl.ds(MEM + 3, ROWS, stride=SLOTS), :] = pack_extra(
+        lambda m, v: ensemble[m, v].astype(F32), ROWS
+    )
+    for place in range(MEM + 4, SLOTS):
+        flat[pl.ds(place, ROWS, stride=SLOTS), :] = jnp.zeros((ROWS, COLS), F32)
+    out[...] = flat[...].reshape(ROWS, SLOTS, COLS).astype(BF16)
+
+
+def to_send(alpha, ensemble):
+    return call(
+        send_body,
+        jax.ShapeDtypeStruct((ROWS, SLOTS, COLS), BF16),
+        [VMEM((ROWS * SLOTS, COLS), F32)],
+        2,
+    )(alpha, ensemble)
+
+
+def contract(ensemble, arrived, tiles, out, flat):
     own = lax.axis_index("grp")
+    column = lax.axis_index(SP)
     unspread = math.sqrt(MEM * GROUPS - 1)
     flat[...] = arrived[...].astype(F32).reshape(ROWS * SLOTS, COLS)
     totals = [jnp.zeros((ROWS, COLS), F32)] * 3
@@ -197,33 +243,19 @@
         field = flat[pl.ds(m, ROWS, stride=SLOTS), :]
         for v in range(3):
             totals[v] = totals[v] + ensemble[m, v].astype(F32) * field
-    right = (lax.broadcasted_iota(jnp.int32, (16, COLS), 1) & 15) < RIM
-
-    def rim(at, count):
-        return jnp.concatenate(
-            [
-                jnp.where(
-                    right,
-                    from_high[at + i : at + i + 16, :].astype(F32),
-                    from_low[at + i : at + i + 16, :].astype(F32),
-                )
-                for i in range(0, count, 16)
-            ],
-            axis=0,
-        )
-
-    slot = slot_of((ROWS, COLS))
-    first = flat[pl.ds(MEM, ROWS, stride=SLOTS), :]
-    second = flat[pl.ds(MEM + 1, ROWS, stride=SLOTS), :]
-    extra = rim(3 * ROWS, ROWS) * second
-    side = jnp.zeros((ROWS, COLS), F32)
-    for v in range(3):
-        t = rim(ROWS * v, ROWS) * first
-        t = t + jnp.where(jnp.right_shift(slot, 1) == v, extra, 0.0)
-        for by in (64, 32, 16):
-            t = t + turned(t, by)
-        side = jnp.where(slot == v, t, side)
-    obs_rim = rim(4 * ROWS, 16)
+    side = flat[pl.ds(MEM, ROWS, stride=SLOTS), :]
+    right = (lax.broadcasted_iota(jnp.int32, (SLOTS, COLS), 1) & 15) < RIM
+    after = arrived[(column + 1) & (BLOCKS - 1)].astype(F32)
+    before = arrived[(column + BLOCKS - 1) & (BLOCKS - 1)].astype(F32)
+    rim = jnp.where(right, after, before)
+    obs_rim = rim[MEM + 1 : MEM + 5]
+    last = rim[MEM + 5 : MEM + 6]
+    slot = slot_of((TILE_ROWS, COLS))
+    static_rim = jnp.where(
+        slot == 2,
+        jnp.concatenate([turned(last, 16 * (2 - r)) for r in range(TILE_ROWS)], axis=0),
+        turned(obs_rim, 32),
+    )
     mine = jnp.right_shift(lax.broadcasted_iota(jnp.int32, (ROWS, COLS), 0), 2) == own
 
     def on_own_rows(tile):
@@ -233,25 +265,25 @@
         (totals[v] + on_own_rows(tiles[24 + 4 * v : 28 + 4 * v, :])).astype(BF16)
         for v in range(3)
     ]
-    parts.append((side + on_own_rows(obs_rim[4:8])).astype(BF16))
+    parts.append((side + on_own_rows(static_rim)).astype(BF16))
     parts.append(
-        jnp.concatenate([tiles[:24, :], obs_rim[:4], jnp.zeros((4, COLS), F32)], axis=0).astype(BF16)
+        jnp.concatenate([tiles[:24, :], obs_rim, jnp.zeros((4, COLS), F32)], axis=0).astype(BF16)
     )
     for i, part in enumerate(parts):
         for g in range(GROUPS):
             out[g, ROWS * i : ROWS * i + ROWS, :] = part
 
 
-def partial_sums(ensemble, arrived, from_low, from_high, tiles):
+def partial_sums(ensemble, arrived, tiles):
     return call(
         contract,
         jax.ShapeDtypeStruct((GROUPS, 5 * ROWS, COLS), BF16),
         [VMEM((ROWS * SLOTS, COLS), F32)],
-        5,
-    )(ensemble, arrived, from_low, from_high, tiles)
-
-
-def observe(cell, step, innovation, weight, std, control, ensemble, tiles, edges):
+        3,
+    )(ensemble, arrived, tiles)
+
+
+def observe(cell, step, innovation, weight, std, control, tiles, edges):
     where_row = jnp.right_shift(cell[...], 12) & (TILE_ROWS - 1)
     key = step[...] * TILE_ROWS + where_row
     column = cell[...] & (COLS - 1)
@@ -275,42 +307,31 @@
     tiles[:24, :] = total
     for v in range(3):
         tiles[24 + 4 * v : 28 + 4 * v, :] = static[v]
-    slot = slot_of((ROWS, COLS))
-    extra = jnp.zeros((ROWS, COLS), F32)
-    for v in range(3):
-        packed = jnp.zeros((ROWS, COLS), F32)
-        for m in range(SLOT_COUNT):
-            packed = jnp.where(slot == m, turned(ensemble[m, v].astype(F32), 16 * m), packed)
-        edges[ROWS * v : ROWS * v + ROWS, :] = packed.astype(BF16)
-        for m in range(SLOT_COUNT, MEM):
-            q = EXTRA * v + m - SLOT_COUNT
-            extra = jnp.where(slot == q, turned(ensemble[m, v].astype(F32), 16 * q), extra)
-    edges[3 * ROWS : 4 * ROWS, :] = extra.astype(BF16)
     slot = slot_of((TILE_ROWS, COLS))
     sums = jnp.zeros((TILE_ROWS, COLS), F32)
     for f in range(6):
         sums = jnp.where(slot == f, turned(total[4 * f : 4 * f + 4], 16 * f), sums)
-    product_rim = jnp.zeros((TILE_ROWS, COLS), F32)
-    for v in range(3):
-        product_rim = jnp.where(slot == v, turned(static[v], 16 * v), product_rim)
-    pad = jnp.zeros((8, COLS), F32)
-    edges[4 * ROWS :, :] = jnp.concatenate([sums, product_rim, pad], axis=0).astype(BF16)
-
-
-def tile_fields(cell, step, innovation, weight, std, control, ensemble):
+    for v in range(2):
+        sums = jnp.where(slot == 6 + v, turned(static[v], 16 * (6 + v)), sums)
+    slot = slot_of((1, COLS))
+    last = jnp.zeros((1, COLS), F32)
+    for r in range(TILE_ROWS):
+        last = jnp.where(slot == r, turned(static[2][r : r + 1], 16 * r), last)
+    edges[...] = jnp.concatenate([sums, last, jnp.zeros((3, COLS), F32)], axis=0)
+
+
+def tile_fields(cell, step, innovation, weight, std, control):
     flat = [a.reshape(1, -1) for a in (cell, step, innovation, weight)]
     return call(
         observe,
-        [
-            jax.ShapeDtypeStruct((36, COLS), F32),
-            jax.ShapeDtypeStruct((4 * ROWS + 16, COLS), BF16),
-        ],
+        [jax.ShapeDtypeStruct((36, COLS), F32), jax.ShapeDtypeStruct((8, COLS), F32)],
         (),
-        7,
-    )(*flat, std, control, ensemble)
-
-
-def window(arrived, ensemble, sent, adj, flat, sums):
+        6,
+    )(*flat, std, control)
+
+
+def window(arrived, ensemble, sent, tile, flat, sums):
+    own = lax.axis_index("grp")
     spread = 1.0 / math.sqrt(MEM * GROUPS - 1)
     parts = []
     for i in range(4):
@@ -365,7 +386,10 @@
     bh = bh + forcing[0]
     fin = [x[:, :COLS] for x in (bh, bu, bw)]
     for v in range(3):
-        adj[v] = fin[v]
+        mine = fin[v][:TILE_ROWS]
+        for g in range(1, GROUPS):
+            mine = jnp.where(own == g, fin[v][TILE_ROWS * g : TILE_ROWS * g + TILE_ROWS], mine)
+        tile[v] = mine
     for m in range(MEM):
         total = ensemble[m, 0].astype(F32) * fin[0]
         for v in range(1, 3):
@@ -379,27 +403,32 @@
         window,
         [
             jax.ShapeDtypeStruct((ROWS, SLOTS, COLS), BF16),
-            jax.ShapeDtypeStruct((3, ROWS, COLS), F32),
+            jax.ShapeDtypeStruct((3, TILE_ROWS, COLS), F32),
         ],
         [VMEM((MEM * ROWS, COLS), F32), VMEM((7, ROWS, COLS), F32)],
         2,
     )(arrived, ensemble)
 
 
-def add_alpha(alpha, arrived, out, flat):
+def add_alpha(alpha, arrived, tile, std, control, out, grad, flat):
     spread = 1.0 / math.sqrt(MEM * GROUPS - 1)
+    for v in range(3):
+        grad[v] = control[v] + std[v] * tile[v]
     flat[...] = arrived[...].astype(F32).reshape(ROWS * SLOTS, COLS)
     for m in range(MEM):
         out[m] = alpha[m] + spread * flat[pl.ds(m, ROWS, stride=SLOTS), :]
 
 
-def finish(alpha, arrived):
+def finish(alpha, arrived, tile, std, control):
     return call(
         add_alpha,
-        jax.ShapeDtypeStruct((MEM, ROWS, COLS), F32),
+        [
+            jax.ShapeDtypeStruct((MEM, ROWS, COLS), F32),
+            jax.ShapeDtypeStruct((3, TILE_ROWS, COLS), F32),
+        ],
         [VMEM((ROWS * SLOTS, COLS), F32)],
-        2,
-    )(alpha, arrived)
+        5,
+    )(alpha, arrived, tile, std, control)
 
 
 def wave_weights(loc_spectrum):
@@ -416,30 +445,19 @@
     return lax.all_to_all(x, axis, split_axis=0, concat_axis=0, tiled=True)
 
 
-def neighbours(x):
-    ahead = [(i, (i + 1) % BLOCKS) for i in range(BLOCKS)]
-    back = [(t, s) for s, t in ahead]
-    return lax.ppermute(x, SP, ahead), lax.ppermute(x, SP, back)
-
-
 def per_device(
     alpha, ensemble, static_std, control, loc_spectrum, obs_cell, obs_step, innovation, obs_weight
 ):
-    first_row = lax.axis_index("grp") * TILE_ROWS
-    rows = swap(to_send(alpha), SP)
+    rows = swap(to_send(alpha, ensemble), SP)
     tiles, edges = tile_fields(
-        obs_cell, obs_step, innovation, obs_weight, static_std, control, ensemble
-    )
-    from_low, from_high = neighbours(edges)
+        obs_cell, obs_step, innovation, obs_weight, static_std, control
+    )
     weights = wave_weights(loc_spectrum)
-    localized = swap(localize(rows, weights, True), SP)
-    summed = swap(partial_sums(ensemble, localized, from_low, from_high, tiles), "grp")
-    sent, adjoint = assimilate(summed, ensemble)
-    weighted = swap(sent, SP)
-    mine = lax.dynamic_slice_in_dim(adjoint, first_row, TILE_ROWS, axis=1)
-    grad_control = control + static_std * mine
-    filtered = swap(localize(weighted, weights, False), SP)
-    return finish(alpha, filtered), grad_control
+    localized = swap(localize(rows, weights, edges), SP)
+    summed = swap(partial_sums(ensemble, localized, tiles), "grp")
+    sent, tile = assimilate(summed, ensemble)
+    filtered = swap(localize(swap(sent, SP), weights), SP)
+    return finish(alpha, filtered, tile, static_std, control)
 
 
 def solution(mesh):

time: 87.9 us -> 86 us (0.978)
  blocking collectives: 35.6 us -> 60.1 us
  waiting for transfers between devices: 22.3 us -> 7.12 us
  starting transfers between devices: 19.9 us -> 10.2 us
  Pallas kernels: 5.89 us -> 4.64 us
    all_to_all x2 -> x4, blocking collectives: 35.6 us -> 60.1 us  [swap(): return lax.all_to_all(x, axis, split_axis=0, concat_axis=0, tiled=True)]
    all_to_all x3 -> x1, waiting for transfers between devices: 18.6 us -> 7.12 us  [swap(): return lax.all_to_all(x, axis, split_axis=0, concat_axis=0, tiled=True)]
    all_to_all x3 -> x1, starting transfers between devices: 18.2 us -> 10.2 us  [swap(): return lax.all_to_all(x, axis, split_axis=0, concat_axis=0, tiled=True)]
    ppermute x2 -> x0, waiting for transfers between devices: 3.72 us -> none  [neighbours(): return (lax.ppermute(x, SP, ahead), lax.ppermute(x, SP, back))]
    ppermute x2 -> x0, starting transfers between devices: 1.69 us -> none  [neighbours(): return (lax.ppermute(x, SP, ahead), lax.ppermute(x, SP, back))]
    pallas_call x2, Pallas kernels: 2.93 us -> 1.79 us  [localize(): call(functools.partial(filter_body, rims), jax.ShapeDtypeStruct((BLOCKS,...]
    unnamed x30 -> x32, local copies, waits for them, and re-layouts: 1.59 us -> 2.17 us
  transfers between devices with their start and end apart: 5 -> 1, of which waited for: 5 -> 1; matrix products, arithmetic and copies ran while one was open for 1% -> 1% of each run, Pallas kernels for 1% -> 1%
where the time goes in v3:
time: 86 us; the launch traced here: 85.6 us
  blocking collectives  60.1 us (70%)
  starting transfers between devices  10.2 us (12%)
  waiting for transfers between devices  7.12 us (8%)
  Pallas kernels  4.64 us (5%)
  local copies, waits for them, and re-layouts  2.46 us (3%)
    all_to_all x4, blocking collectives, swap(): return lax.all_to_all(x, axis, split_axis=0, concat_axis=0, tiled=True)  60.1 us
    all_to_all x1, starting transfers between devices, swap(): return lax.all_to_all(x, axis, split_axis=0, concat_axis=0, tiled=True)  10.2 us
    all_to_all x1, waiting for transfers between devices, swap(): return lax.all_to_all(x, axis, split_axis=0, concat_axis=0, tiled=True)  7.12 us
    unnamed x32, local copies, waits for them, and re-layouts  2.17 us
    pallas_call x2, Pallas kernels, localize(): call(functools.partial(filter_body, rims), jax.ShapeDtypeStruct((BLOCKS,...  1.79 us
  transfers between devices with their start and end apart: 1, of which 1 were waited for; matrix products, arithmetic and copies ran while one was open for 1% of the time, Pallas kernels for 1%

profile of v3, /device:TPU:1, one launch (start us, length us, event | category | flops | bytes accessed | tf_op | source)
XLA Modules:
  0.0 85.6 jit_solution(10256263419042330126)
XLA Ops:
  0.6 0.0 copy-start
  0.6 0.9 %copy-done = bf16[10,3,32,128]{3,2,1,0:T(8,128)(2,1)S(1)} copy-done((bf16[10,3,32,128]{3,2,1,0:T(8,128)(2,1)S(1)}, bf16[10,3,32,128]{3,2,1,0:T(8,128)(2,1)}, u32[]{:S(2)}) %copy-start) | copy-done | bytes 245784
  1.6 0.0 copy-start.2
  1.6 0.9 %copy-done.2 = f32[10,32,128]{2,1,0:T(8,128)S(1)} copy-done((f32[10,32,128]{2,1,0:T(8,128)S(1)}, f32[10,32,128]{2,1,0:T(8,128)}, u32[]{:S(2)}) %copy-start.2) | copy-done | bytes 163864
  2.5 0.8 shard_map.194
  3.3 0.0 copy-start.15
  3.3 0.0 copy-start.11
  3.3 0.0 copy-start.12
  3.3 0.0 copy-start.13
  3.3 0.0 copy-start.14
  3.3 0.0 copy-start.8
  3.3 10.2 %all-to-all-start = ((bf16[32,16,128]{2,1,0:T(8,128)(2,1)}), bf16[32,16,128]{2,1,0:T(8,128)(2,1)S(1)}, u32[]{:S(2)}, u32[]{:S(2)}) async-start(bf16[32,16,128]{2,1,0:T(8,128)(2,1)} %shard_map.194), calls=%async_computation | async-start | bytes 262144 | tf_op jit(solution)/shard_map/all_to_all | solution.py:445
  13.5 0.0 copy-done.15
  13.5 0.1 slice_multiply_fusion
  13.6 0.0 copy-start.9
  13.6 0.0 copy-start.10
  13.6 0.0 copy-start.7
  13.6 0.1 pad_maximum_fusion.1
  13.7 0.1 reshape.22
  13.8 0.1 copy.22
  13.8 0.0 copy-start.6
  13.8 0.1 reshape.23
  13.9 0.1 copy.21
  14.0 0.0 copy-start.5
  14.0 0.0 copy-start.4
  14.0 0.0 copy-done.11
  14.0 0.0 copy-done.12
  14.0 0.0 copy-done.13
  14.0 0.0 copy-done.14
  14.0 0.2 copy-done.9
  14.3 0.0 copy-done.10
  14.3 0.5 shard_map.195
  14.8 0.1 maximum_bitcast_fusion
  14.9 0.1 pad_maximum_fusion.refs_6_
  14.9 7.1 %all-to-all-done.refs_0_ = bf16[32,16,128]{2,1,0:T(8,128)(2,1)S(1)} async-done(((bf16[32,16,128]{2,1,0:T(8,128)(2,1)}), bf16[32,16,128]{2,1,0:T(8,128)(2,1)S(1)}, u32[]{:S(2)}, u32[]{:S(2)}) %all-to-all-start) | async-done | bytes 131104 | tf_op jit(solution)/shard_map/all_to_all | solution.py:445
  22.1 0.0 copy-done.8
  22.1 0.0 copy-done.7
  22.1 0.0 copy-done.6
  22.1 0.0 copy-done.5
  22.1 0.0 copy-done.4
  22.1 1.1 %shard_map.196 = bf16[32,16,128]{2,1,0:T(8,128)(2,1)S(1)} custom-call(bf16[32,16,128]{2,1,0:T(8,128)(2,1)S(1)} %all-to-all-done.refs_0_, bf16[256,128]{1,0:T(8,128)(2,1)S(1)} %copy-done.7, bf16[256,128]{1,0:T(8,128)(2,1)S(1)} %copy-done.6, bf16[128,256]{1,0:T(8,128)(2,1)S(1)} %copy-done.5, bf16[128,256]{1,0:T(8,128)(2,1)S(1)} %copy-done.4, ...), custom_call_target="tpu_custom_call" | custom-call | tf_op jit(solution)/shard_map/pallas_call | solution.py:197
  23.2 0.0 copy-start.1
  23.2 12.3 %all_to_all.25.arrived = bf16[32,16,128]{2,1,0:T(8,128)(2,1)S(1)} all-to-all(bf16[32,16,128]{2,1,0:T(8,128)(2,1)S(1)} %shard_map.196), channel_id=1, replica_groups=mesh['grp'=8,'sp_0'=4,'sp_1'=4,'sp_2'=2] {'sp_0','sp_1','sp_2'}, dimensions={0} | all-to-all | bytes 262144 | tf_op jit(solution)/shard_map/all_to_all | solution.py:445
  35.4 0.0 copy-done.1
  35.4 0.1 shard_map.197
  35.6 19.4 %all_to_all.26.arrived = bf16[8,160,128]{2,1,0:T(8,128)(2,1)S(1)} all-to-all(bf16[8,160,128]{2,1,0:T(8,128)(2,1)S(1)} %shard_map.197), channel_id=1, replica_groups=mesh['grp'=8,'sp_0'=4,'sp_1'=4,'sp_2'=2] {'grp'}, dimensions={0} | all-to-all | bytes 655360 | tf_op jit(solution)/shard_map/all_to_all | solution.py:445
  54.9 0.7 shard_map.198
  55.6 16.2 %all_to_all.27.refs_0_ = bf16[32,16,128]{2,1,0:T(8,128)(2,1)S(1)} all-to-all(bf16[32,16,128]{2,1,0:T(8,128)(2,1)S(1)} %get-tuple-element.8), channel_id=1, replica_groups=mesh['grp'=8,'sp_0'=4,'sp_1'=4,'sp_2'=2] {'sp_0','sp_1','sp_2'}, dimensions={0} | all-to-all | bytes 262144 | tf_op jit(solution)/shard_map/all_to_all | solution.py:445
  71.8 0.7 shard_map.199
  72.5 0.0 copy-start.3
  72.6 12.3 %all_to_all.28.arrived = bf16[32,16,128]{2,1,0:T(8,128)(2,1)S(1)} all-to-all(bf16[32,16,128]{2,1,0:T(8,128)(2,1)S(1)} %shard_map.199), channel_id=1, replica_groups=mesh['grp'=8,'sp_0'=4,'sp_1'=4,'sp_2'=2] {'sp_0','sp_1','sp_2'}, dimensions={0} | all-to-all | bytes 262144 | tf_op jit(solution)/shard_map/all_to_all | solution.py:445
  84.8 0.0 copy-done.3
  84.8 0.8 shard_map.200
  (2 shorter events, 0.0 us)
Async XLA Ops:
  0.6 0.9 %copy-start = (bf16[10,3,32,128]{3,2,1,0:T(8,128)(2,1)S(1)}, bf16[10,3,32,128]{3,2,1,0:T(8,128)(2,1)}, u32[]{:S(2)}) copy-start(bf16[10,3,32,128]{3,2,1,0:T(8,128)(2,1)} %ensemble.5) | copy-start | bytes 737284
  1.6 0.9 %copy-start.2 = (f32[10,32,128]{2,1,0:T(8,128)S(1)}, f32[10,32,128]{2,1,0:T(8,128)}, u32[]{:S(2)}) copy-start(f32[10,32,128]{2,1,0:T(8,128)} %alpha.3) | copy-start | bytes 491524
  3.3 10.2 %copy-start.15 = (f32[1024]{0:T(1024)S(1)}, f32[1024]{0:T(1024)}, u32[]{:S(2)}) copy-start(f32[1024]{0:T(1024)} %param.23) | copy-start | bytes 12292
  3.3 10.7 %copy-start.11 = (s32[1024]{0:T(1024)S(1)}, s32[1024]{0:T(1024)}, u32[]{:S(2)}) copy-start(s32[1024]{0:T(1024)} %param.24) | copy-start | bytes 12292
  3.3 10.7 %copy-start.12 = (s32[1024]{0:T(1024)S(1)}, s32[1024]{0:T(1024)}, u32[]{:S(2)}) copy-start(s32[1024]{0:T(1024)} %param.25) | copy-start | bytes 12292
  3.3 10.7 %copy-start.13 = (f32[1024]{0:T(1024)S(1)}, f32[1024]{0:T(1024)}, u32[]{:S(2)}) copy-start(f32[1024]{0:T(1024)} %param.26) | copy-start | bytes 12292
  3.3 10.7 %copy-start.14 = (f32[1024]{0:T(1024)S(1)}, f32[1024]{0:T(1024)}, u32[]{:S(2)}) copy-start(f32[1024]{0:T(1024)} %param.27) | copy-start | bytes 12292
  3.3 18.7 %copy-start.8 = (f32[2,32,128]{2,1,0:T(8,128)S(1)}, f32[2,32,128]{2,1,0:T(8,128)}, u32[]{:S(2)}) copy-start(f32[2,32,128]{2,1,0:T(8,128)} %constant.21.clone.refs_5_) | copy-start | bytes 98308
  3.3 18.7 %all-to-all-start = ((bf16[32,16,128]{2,1,0:T(8,128)(2,1)}), bf16[32,16,128]{2,1,0:T(8,128)(2,1)S(1)}, u32[]{:S(2)}, u32[]{:S(2)}) async-start(bf16[32,16,128]{2,1,0:T(8,128)(2,1)} %shard_map.194), calls=%async_computation | async-start | bytes 262144 | tf_op jit(solution)/shard_map/all_to_all | solution.py:445
  13.6 0.7 copy-start.9
  13.6 0.7 copy-start.10
  13.6 8.5 %copy-start.7 = (bf16[256,128]{1,0:T(8,128)(2,1)S(1)}, bf16[256,128]{1,0:T(8,128)(2,1)}, u32[]{:S(2)}) copy-start(bf16[256,128]{1,0:T(8,128)(2,1)} %constant.7.clone.refs_1_) | copy-start | bytes 196612
  13.8 8.2 %copy-start.6 = (bf16[256,128]{1,0:T(8,128)(2,1)S(1)}, bf16[256,128]{1,0:T(8,128)(2,1)}, u32[]{:S(2)}) copy-start(bf16[256,128]{1,0:T(8,128)(2,1)} %constant.18.clone.refs_2_) | copy-start | bytes 196612
  14.0 8.1 %copy-start.5 = (bf16[128,256]{1,0:T(8,128)(2,1)S(1)}, bf16[128,256]{1,0:T(8,128)(2,1)}, u32[]{:S(2)}) copy-start(bf16[128,256]{1,0:T(8,128)(2,1)} %constant.19.clone.refs_3_) | copy-start | bytes 196612
  14.0 8.1 %copy-start.4 = (bf16[128,256]{1,0:T(8,128)(2,1)S(1)}, bf16[128,256]{1,0:T(8,128)(2,1)}, u32[]{:S(2)}) copy-start(bf16[128,256]{1,0:T(8,128)(2,1)} %constant.20.clone.refs_4_) | copy-start | bytes 196612
  23.2 12.3 %copy-start.1 = (bf16[10,3,32,128]{3,2,1,0:T(8,128)(2,1)S(1)}, bf16[10,3,32,128]{3,2,1,0:T(8,128)(2,1)}, u32[]{:S(2)}) copy-start(bf16[10,3,32,128]{3,2,1,0:T(8,128)(2,1)} %ensemble.5) | copy-start | bytes 737284
  72.5 12.3 %copy-start.3 = (f32[10,32,128]{2,1,0:T(8,128)S(1)}, f32[10,32,128]{2,1,0:T(8,128)}, u32[]{:S(2)}) copy-start(f32[10,32,128]{2,1,0:T(8,128)} %alpha.3) | copy-start | bytes 491524

commit v4 on v3

--- a/solution.py
+++ b/solution.py
@@ -7,11 +7,9 @@
 from jax import lax
 from jax.experimental import pallas as pl
 from jax.experimental.pallas import tpu as pltpu
-from jax.sharding import Mesh
 from jax.sharding import PartitionSpec as P
 
-GRP_SP = ("grp", "sp_0", "sp_1", "sp_2")
-SP = ("sp_0", "sp_1", "sp_2")
+SP = "sp"
 
 MEM = 10
 SLOTS = 16
@@ -27,6 +25,19 @@
 SLOT_COUNT = COLS // 16
 EXTRA = MEM - SLOT_COUNT
 COURANT = 0.4
+
+HEADS = (21, 21, 6, 21, 21)
+
+
+def places(count, head):
+    place = list(range(count))
+    place[0], place[head] = head, 0
+    return place
+
+
+FIRST, SECOND, THIRD, FOURTH, FIFTH = (
+    places(GROUPS if i == 2 else BLOCKS, head) for i, head in enumerate(HEADS)
+)
 
 F32 = jnp.float32
 BF16 = jnp.bfloat16
@@ -131,7 +142,7 @@
     return extra
 
 
-def filter_body(rims, *refs):
+def filter_body(rims, come, go, *refs):
     rows, high, low, high_t, low_t, twiddle, weights = refs[:7]
     if rims:
         edges, out, wide, spec, flat, arrived = refs[7:]
@@ -139,7 +150,9 @@
         out, wide, spec = refs[7:]
 
     def load(p):
-        x = rows[p].astype(F32)
+        x = rows[come[p]].astype(F32)
+        if rims:
+            arrived[8 * p : 8 * p + 8, :] = x[8:]
         return x[:8], x[8:]
 
     for b, (ur, ui) in enumerate(fft(load, 0, 1, BLOCKS, -1)):
@@ -159,9 +172,8 @@
     blocks = fft(load_back, 0, 1, BLOCKS, 1)
     if not rims:
         for p, (yr, yi) in enumerate(blocks):
-            out[p] = jnp.concatenate([yr, yi], axis=0).astype(BF16)
+            out[go[p]] = jnp.concatenate([yr, yi], axis=0).astype(BF16)
         return
-    arrived[...] = rows[...].astype(F32).reshape(BLOCKS * SLOTS, COLS)
     for p, (yr, yi) in enumerate(blocks):
         flat[SLOTS * p : SLOTS * p + 8, :] = yr
         flat[SLOTS * p + 8 : SLOTS * p + 16, :] = yi
@@ -169,14 +181,17 @@
     def every(source, place):
         return source[pl.ds(place, BLOCKS, stride=SLOTS), :]
 
+    def edge(i):
+        return arrived[pl.ds(MEM - 8 + i, BLOCKS, stride=8), :]
+
     first = pack_slots(lambda m: every(flat, m), BLOCKS)
     extra = pack_extra(lambda m, v: every(flat, m), BLOCKS)
-    extra = extra * every(arrived, MEM + 3)
+    extra = extra * edge(3)
     slot = slot_of((BLOCKS, COLS))
     right = (lax.broadcasted_iota(jnp.int32, (BLOCKS, COLS), 1) & 15) < RIM
     side = jnp.zeros((BLOCKS, COLS), F32)
     for v in range(3):
-        t = first * every(arrived, MEM + v)
+        t = first * edge(v)
         t = t + jnp.where(jnp.right_shift(slot, 1) == v, extra, 0.0)
         for by in (64, 32, 16):
             t = t + turned(t, by)
@@ -186,58 +201,162 @@
     own_edges = edges[:5, :]
     for p in range(BLOCKS):
         flat[SLOTS * p + MEM + 1 : SLOTS * p + SLOTS, :] = own_edges
-        out[p] = flat[SLOTS * p : SLOTS * p + SLOTS, :].astype(BF16)
-
-
-def localize(rows, weights, edges=None):
+        out[go[p]] = flat[SLOTS * p : SLOTS * p + SLOTS, :].astype(BF16)
+
+
+def localize(rows, weights, come, go, edges=None):
     rims = edges is not None
     scratch = [VMEM((8 * BLOCKS, 2 * COLS), F32), VMEM((8 * BLOCKS, COLS), F32)]
     if rims:
-        scratch += [VMEM((SLOTS * BLOCKS, COLS), F32)] * 2
+        scratch += [VMEM((SLOTS * BLOCKS, COLS), F32), VMEM((8 * BLOCKS, COLS), F32)]
     return call(
-        functools.partial(filter_body, rims),
+        functools.partial(filter_body, rims, come, go),
         jax.ShapeDtypeStruct((BLOCKS, SLOTS, COLS), BF16),
         scratch,
         8 if rims else 7,
     )(rows, *tables(), weights, *([edges] if rims else []))
 
 
-def by_row(flat, out):
-    for y in range(ROWS):
+def by_row(flat, out, order):
+    for y, place in enumerate(order):
         x = flat[pl.ds(y, MEM, stride=ROWS), :]
         x = jnp.concatenate([x, jnp.zeros((SLOTS - MEM, COLS), F32)], axis=0)
-        out[y] = x.astype(BF16)
-
-
-def send_body(alpha, ensemble, out, flat):
-    for m in range(MEM):
-        flat[pl.ds(m, ROWS, stride=SLOTS), :] = alpha[m]
+        out[place] = x.astype(BF16)
+
+
+def pack_weights(loc, out, square, sheet):
+    x = loc[...]
+    for r in range(4):
+        sheet[pl.ds(r, 8, stride=4), :] = turned(x, -BLOCKS * r)
+    up = sheet[...]
+    lane = lax.broadcasted_iota(jnp.int32, (BLOCKS, COLS), 1)
+    row = lax.broadcasted_iota(jnp.int32, (BLOCKS, COLS), 0)
+    next_row = jnp.where(row < BLOCKS - 1, pltpu.roll(up, BLOCKS - 1, 0), 0.0)
+    down = jnp.where(lane == BLOCKS - 1, turned(next_row, BLOCKS - 1), turned(up, -1))
+    both = jnp.concatenate([up, down, jnp.zeros((2 * BLOCKS, COLS), F32)], axis=0)
+    square[...] = both.T
+    for b in range(BLOCKS):
+        sheet[b : b + 1, :] = square[BLOCKS - 1 - b : BLOCKS - b, :]
+    h = jnp.where(lane < BLOCKS, square[:BLOCKS, :], jnp.where(lane < 2 * BLOCKS, sheet[...], 0.0))
+    h = jnp.where(jnp.logical_and(row == 0, lane == 0), h, 0.5 * h)
+    out[...] = h + turned(h, 2 * BLOCKS)
+
+
+PIECE = 2
+SMALL = 7
+
+
+def first_body(
+    alpha, ensemble, loc, cell, step, innovation, weight, std, control,
+    out, tiles, edges, weights,
+    alpha_v, ens_v, loc_v, cell_v, step_v, innovation_v, weight_v, std_v, control_v,
+    flat, square, sheet, small_sem, alpha_sem, ens_sem,
+):
+    small = [
+        pltpu.make_async_copy(a, b, small_sem.at[i])
+        for i, (a, b) in enumerate(
+            (
+                (cell, cell_v),
+                (step, step_v),
+                (innovation, innovation_v),
+                (weight, weight_v),
+                (std, std_v),
+                (control, control_v),
+                (loc, loc_v),
+            )
+        )
+    ]
+    count = MEM // PIECE
+
+    def pieces(source, target, sem):
+        return [
+            pltpu.make_async_copy(
+                source.at[pl.ds(PIECE * i, PIECE)], target.at[pl.ds(PIECE * i, PIECE)], sem.at[i]
+            )
+            for i in range(count)
+        ]
+
+    from_alpha = pieces(alpha, alpha_v, alpha_sem)
+    from_ensemble = pieces(ensemble, ens_v, ens_sem)
+    for copy in small + from_alpha + from_ensemble:
+        copy.start()
+    for copy in small:
+        copy.wait()
+    observe(cell_v, step_v, innovation_v, weight_v, std_v, control_v, tiles, edges)
+    pack_weights(loc_v, weights, square, sheet)
+    for place in range(MEM + 4, SLOTS):
+        flat[pl.ds(place, ROWS, stride=SLOTS), :] = jnp.zeros((ROWS, COLS), F32)
+    for i, copy in enumerate(from_alpha):
+        copy.wait()
+        for m in range(PIECE * i, PIECE * i + PIECE):
+            flat[pl.ds(m, ROWS, stride=SLOTS), :] = alpha_v[m]
+    for copy in from_ensemble:
+        copy.wait()
     for v in range(3):
         flat[pl.ds(MEM + v, ROWS, stride=SLOTS), :] = pack_slots(
-            lambda m: ensemble[m, v].astype(F32), ROWS
+            lambda m: ens_v[m, v].astype(F32), ROWS
         )
     flat[pl.ds(MEM + 3, ROWS, stride=SLOTS), :] = pack_extra(
-        lambda m, v: ensemble[m, v].astype(F32), ROWS
-    )
-    for place in range(MEM + 4, SLOTS):
-        flat[pl.ds(place, ROWS, stride=SLOTS), :] = jnp.zeros((ROWS, COLS), F32)
-    out[...] = flat[...].reshape(ROWS, SLOTS, COLS).astype(BF16)
-
-
-def to_send(alpha, ensemble):
-    return call(
-        send_body,
-        jax.ShapeDtypeStruct((ROWS, SLOTS, COLS), BF16),
-        [VMEM((ROWS * SLOTS, COLS), F32)],
-        2,
-    )(alpha, ensemble)
+        lambda m, v: ens_v[m, v].astype(F32), ROWS
+    )
+    for y, place in enumerate(FIRST):
+        out[place] = flat[SLOTS * y : SLOTS * y + SLOTS, :].astype(BF16)
+
+
+def first_step(alpha, ensemble, loc, cell, step, innovation, weight, std, control):
+    far = pl.BlockSpec(memory_space=pltpu.HBM)
+    near = pl.BlockSpec(memory_space=VMEM)
+    line = (1, cell.shape[0])
+    sems = pltpu.SemaphoreType.DMA
+    return pl.pallas_call(
+        first_body,
+        out_shape=[
+            jax.ShapeDtypeStruct((ROWS, SLOTS, COLS), BF16),
+            jax.ShapeDtypeStruct((36, COLS), F32),
+            jax.ShapeDtypeStruct((8, COLS), F32),
+            jax.ShapeDtypeStruct((BLOCKS, COLS), F32),
+        ],
+        in_specs=[far] * 9,
+        out_specs=[near] * 4,
+        scratch_shapes=[
+            VMEM(alpha.shape, F32),
+            VMEM(ensemble.shape, BF16),
+            VMEM((8, COLS), F32),
+            VMEM(line, jnp.int32),
+            VMEM(line, jnp.int32),
+            VMEM(line, F32),
+            VMEM(line, F32),
+            VMEM(std.shape, F32),
+            VMEM(control.shape, F32),
+            VMEM((ROWS * SLOTS, COLS), F32),
+            VMEM((COLS, COLS), F32),
+            VMEM((BLOCKS, COLS), F32),
+            sems((SMALL,)),
+            sems((MEM // PIECE,)),
+            sems((MEM // PIECE,)),
+        ],
+        compiler_params=pltpu.CompilerParams(vmem_limit_bytes=32 << 20),
+    )(
+        *[
+            pltpu.with_memory_space_constraint(a, pltpu.HBM)
+            for a in (
+                alpha,
+                ensemble,
+                loc.reshape(8, COLS),
+                *[a.reshape(line) for a in (cell, step, innovation, weight)],
+                std,
+                control,
+            )
+        ]
+    )
 
 
 def contract(ensemble, arrived, tiles, out, flat):
     own = lax.axis_index("grp")
     column = lax.axis_index(SP)
     unspread = math.sqrt(MEM * GROUPS - 1)
-    flat[...] = arrived[...].astype(F32).reshape(ROWS * SLOTS, COLS)
+    for y, place in enumerate(SECOND):
+        flat[SLOTS * y : SLOTS * y + SLOTS, :] = arrived[place].astype(F32)
     totals = [jnp.zeros((ROWS, COLS), F32)] * 3
     for m in range(MEM):
         field = flat[pl.ds(m, ROWS, stride=SLOTS), :]
@@ -245,8 +364,12 @@
             totals[v] = totals[v] + ensemble[m, v].astype(F32) * field
     side = flat[pl.ds(MEM, ROWS, stride=SLOTS), :]
     right = (lax.broadcasted_iota(jnp.int32, (SLOTS, COLS), 1) & 15) < RIM
-    after = arrived[(column + 1) & (BLOCKS - 1)].astype(F32)
-    before = arrived[(column + BLOCKS - 1) & (BLOCKS - 1)].astype(F32)
+
+    def block(y):
+        return flat[pl.ds(pl.multiple_of(SLOTS * (y & (BLOCKS - 1)), SLOTS), SLOTS), :]
+
+    after = block(column + 1)
+    before = block(column + BLOCKS - 1)
     rim = jnp.where(right, after, before)
     obs_rim = rim[MEM + 1 : MEM + 5]
     last = rim[MEM + 5 : MEM + 6]
@@ -320,16 +443,6 @@
     edges[...] = jnp.concatenate([sums, last, jnp.zeros((3, COLS), F32)], axis=0)
 
 
-def tile_fields(cell, step, innovation, weight, std, control):
-    flat = [a.reshape(1, -1) for a in (cell, step, innovation, weight)]
-    return call(
-        observe,
-        [jax.ShapeDtypeStruct((36, COLS), F32), jax.ShapeDtypeStruct((8, COLS), F32)],
-        (),
-        6,
-    )(*flat, std, control)
-
-
 def window(arrived, ensemble, sent, tile, flat, sums):
     own = lax.axis_index("grp")
     spread = 1.0 / math.sqrt(MEM * GROUPS - 1)
@@ -340,7 +453,7 @@
             total = total + arrived[g, ROWS * i : ROWS * i + ROWS, :].astype(F32)
         parts.append(spread * total)
     for g in range(GROUPS):
-        x = arrived[g, 4 * ROWS : 5 * ROWS, :].astype(F32)
+        x = arrived[THIRD[g], 4 * ROWS : 5 * ROWS, :].astype(F32)
         for f in range(7):
             sums[f, TILE_ROWS * g : TILE_ROWS * g + TILE_ROWS, :] = x[4 * f : 4 * f + 4]
     lane = lax.broadcasted_iota(jnp.int32, (ROWS, COLS), 1)
@@ -395,7 +508,7 @@
         for v in range(1, 3):
             total = total + ensemble[m, v].astype(F32) * fin[v]
         flat[ROWS * m : ROWS * m + ROWS, :] = total
-    by_row(flat, sent)
+    by_row(flat, sent, FOURTH)
 
 
 def assimilate(arrived, ensemble):
@@ -414,7 +527,8 @@
     spread = 1.0 / math.sqrt(MEM * GROUPS - 1)
     for v in range(3):
         grad[v] = control[v] + std[v] * tile[v]
-    flat[...] = arrived[...].astype(F32).reshape(ROWS * SLOTS, COLS)
+    for y, place in enumerate(FIFTH):
+        flat[SLOTS * y : SLOTS * y + SLOTS, :] = arrived[place].astype(F32)
     for m in range(MEM):
         out[m] = alpha[m] + spread * flat[pl.ds(m, ROWS, stride=SLOTS), :]
 
@@ -431,51 +545,42 @@
     )(alpha, arrived, tile, std, control)
 
 
-def wave_weights(loc_spectrum):
-    side = KEEP // BLOCKS
-    first = jnp.arange(KEEP) == 0
-    up = jnp.where(first, loc_spectrum, 0.5 * loc_spectrum).reshape(side, BLOCKS)
-    after = jnp.concatenate([0.5 * loc_spectrum[1:], jnp.zeros((1,), F32)])
-    down = after.reshape(side, BLOCKS)[:, ::-1]
-    both = jnp.concatenate([up, down], axis=0).T
-    return jnp.concatenate([both, both], axis=1)
-
-
-def swap(x, axis):
-    return lax.all_to_all(x, axis, split_axis=0, concat_axis=0, tiled=True)
+def swap(x, axis, order):
+    return lax.all_to_all(
+        x, axis, split_axis=0, concat_axis=0, tiled=True, axis_index_groups=[order]
+    )
 
 
 def per_device(
     alpha, ensemble, static_std, control, loc_spectrum, obs_cell, obs_step, innovation, obs_weight
 ):
-    rows = swap(to_send(alpha, ensemble), SP)
-    tiles, edges = tile_fields(
-        obs_cell, obs_step, innovation, obs_weight, static_std, control
-    )
-    weights = wave_weights(loc_spectrum)
-    localized = swap(localize(rows, weights, edges), SP)
-    summed = swap(partial_sums(ensemble, localized, tiles), "grp")
+    sent, tiles, edges, weights = first_step(
+        alpha, ensemble, loc_spectrum, obs_cell, obs_step, innovation, obs_weight, static_std, control
+    )
+    rows = swap(sent, SP, FIRST)
+    localized = swap(localize(rows, weights, FIRST, SECOND, edges), SP, SECOND)
+    summed = swap(partial_sums(ensemble, localized, tiles), "grp", THIRD)
     sent, tile = assimilate(summed, ensemble)
-    filtered = swap(localize(swap(sent, SP), weights), SP)
+    filtered = swap(localize(swap(sent, SP, FOURTH), weights, FOURTH, FIFTH), SP, FIFTH)
     return finish(alpha, filtered, tile, static_std, control)
 
 
 def solution(mesh):
-    torus = Mesh(mesh.devices.reshape(mesh.shape["grp"], 4, 4, 2), GRP_SP)
+    both = P(("grp", SP))
     placed = (
         P("grp", None, SP),
         P("grp", None, None, SP),
         P(None, "grp", SP),
         P(None, "grp", SP),
         P(),
-        P(GRP_SP),
-        P(GRP_SP),
-        P(GRP_SP),
-        P(GRP_SP),
+        both,
+        both,
+        both,
+        both,
     )
     return jax.shard_map(
         per_device,
-        mesh=torus,
+        mesh=mesh,
         in_specs=placed,
         out_specs=(P("grp", None, SP), P(None, "grp", SP)),
         check_vma=False,

time: 86 us -> 71.9 us (0.84)
  starting transfers between devices: 10.2 us -> 0 us
  waiting for transfers between devices: 7.12 us -> 0 us
  blocking collectives: 60.1 us -> 65.5 us
  local copies, waits for them, and re-layouts: 2.46 us -> 0.06 us
    all_to_all x1 -> x0, starting transfers between devices: 10.2 us -> none  [swap(): return lax.all_to_all(x, axis, split_axis=0, concat_axis=0, tiled=True)]
    all_to_all x1 -> x0, waiting for transfers between devices: 7.12 us -> none  [swap(): return lax.all_to_all(x, axis, split_axis=0, concat_axis=0, tiled=True)]
    all_to_all x4 -> x5, blocking collectives: 60.1 us -> 65.5 us  [swap(): lax.all_to_all(x, axis, split_axis=0, concat_axis=0, tiled=True, axis_ind...]
    unnamed x32 -> x18, local copies, waits for them, and re-layouts: 2.17 us -> 0.06 us
    pallas_call x4 -> x3, Pallas kernels: 3.05 us -> 3.62 us  [the longest x1 1.82 us: first_step(): pl.pallas_call(first_body, out_shape=[jax.ShapeDtypeStruct((ROWS, SLOTS,...]
  transfers between devices with their start and end apart: 1 -> 0, of which waited for: 1 -> 0; matrix products, arithmetic and copies ran while one was open for 1% -> 0% of each run, Pallas kernels for 1% -> 0%
where the time goes in v4:
time: 71.9 us; the launch traced here: 71.5 us
  blocking collectives  65.5 us (91%)
  Pallas kernels  5.2 us (7%)
  between operations  0.77 us (1%)
    all_to_all x5, blocking collectives, swap(): lax.all_to_all(x, axis, split_axis=0, concat_axis=0, tiled=True, axis_ind...  65.5 us
    pallas_call x1, Pallas kernels, first_step(): pl.pallas_call(first_body, out_shape=[jax.ShapeDtypeStruct((ROWS, SLOTS,...  1.82 us
    pallas_call x2, Pallas kernels, localize(): call(functools.partial(filter_body, rims, come, go), jax.ShapeDtypeStruct...  1.8 us

profile of v4, /device:TPU:1, one launch (start us, length us, event | category | flops | bytes accessed | tf_op | source)
XLA Modules:
  0.0 71.5 jit_solution(1629435288155684287)
XLA Ops:
  0.6 0.0 copy-start.6
  0.6 1.8 %shard_map.194 = (bf16[32,16,128]{2,1,0:T(8,128)(2,1)S(1)}, f32[36,128]{1,0:T(8,128)S(1)}, f32[8,128]{1,0:T(8,128)S(1)}, f32[32,128]{1,0:T(8,128)S(1)}) custom-call(f32[10,32,128]{2,1,0:T(8,128)} %alpha.3, bf16[10,3,32,128]{3,2,1,0:T(8,128)(2,1)} %ensemble.5, f32[8,128]{1,0:T(8,128)} %bitcast.5, s32[1,1024]{1,0:T(1,128)} %bitcast.6, s32[1,1024]{1,0:T(1,128)} %bitcast.7, ...), custom_call_target="tpu_custom_call" | custom-call | tf_op jit(solution)/shard_map/pallas_call | solution.py:311
  2.5 0.0 copy-start.2
  2.5 0.0 copy-start.3
  2.5 0.0 copy-start.4
  2.5 0.0 copy-start.5
  2.5 14.9 %all_to_all.25.refs_0_ = bf16[32,16,128]{2,1,0:T(8,128)(2,1)S(1)} all-to-all(bf16[32,16,128]{2,1,0:T(8,128)(2,1)S(1)} %get-tuple-element.8), channel_id=1, replica_groups={{21,1,2,3,4,5,6,7,8,9,10,11,12,13,14,15,16,17,18,19,20,0,22,23,24,25,26..., dimensions={0} | all-to-all | bytes 262144 | tf_op jit(solution)/shard_map/all_to_all | solution.py:549
  17.4 0.0 copy-done.6
  17.4 0.0 copy-done.2
  17.4 0.0 copy-done.3
  17.4 0.0 copy-done.4
  17.5 0.0 copy-done.5
  17.5 1.1 %shard_map.195 = bf16[32,16,128]{2,1,0:T(8,128)(2,1)S(1)} custom-call(bf16[32,16,128]{2,1,0:T(8,128)(2,1)S(1)} %all_to_all.25.refs_0_, bf16[256,128]{1,0:T(8,128)(2,1)S(1)} %copy-done.5, bf16[256,128]{1,0:T(8,128)(2,1)S(1)} %copy-done.4, bf16[128,256]{1,0:T(8,128)(2,1)S(1)} %copy-done.3, bf16[128,256]{1,0:T(8,128)(2,1)S(1)} %copy-done.2, ...), custom_call_target="tpu_custom_call" | custom-call | tf_op jit(solution)/shard_map/pallas_call | solution.py:212
  18.6 0.0 copy-start
  18.6 11.0 %all_to_all.26.arrived = bf16[32,16,128]{2,1,0:T(8,128)(2,1)S(1)} all-to-all(bf16[32,16,128]{2,1,0:T(8,128)(2,1)S(1)} %shard_map.195), channel_id=1, replica_groups={{21,1,2,3,4,5,6,7,8,9,10,11,12,13,14,15,16,17,18,19,20,0,22,23,24,25,26..., dimensions={0} | all-to-all | bytes 262144 | tf_op jit(solution)/shard_map/all_to_all | solution.py:549
  29.6 0.0 copy-done
  29.6 0.1 shard_map.196
  29.7 14.3 %all_to_all.27.arrived = bf16[8,160,128]{2,1,0:T(8,128)(2,1)S(1)} all-to-all(bf16[8,160,128]{2,1,0:T(8,128)(2,1)S(1)} %shard_map.196), channel_id=1, replica_groups={{192,32,64,96,128,160,0,224},{193,33,65,97,129,161,1,225},{194,34,66,98..., dimensions={0} | all-to-all | bytes 655360 | tf_op jit(solution)/shard_map/all_to_all | solution.py:549
  44.0 0.7 shard_map.197
  44.7 14.2 %all_to_all.28.refs_0_ = bf16[32,16,128]{2,1,0:T(8,128)(2,1)S(1)} all-to-all(bf16[32,16,128]{2,1,0:T(8,128)(2,1)S(1)} %get-tuple-element.12), channel_id=1, replica_groups={{21,1,2,3,4,5,6,7,8,9,10,11,12,13,14,15,16,17,18,19,20,0,22,23,24,25,26..., dimensions={0} | all-to-all | bytes 262144 | tf_op jit(solution)/shard_map/all_to_all | solution.py:549
  59.0 0.7 %shard_map.198 = bf16[32,16,128]{2,1,0:T(8,128)(2,1)S(1)} custom-call(bf16[32,16,128]{2,1,0:T(8,128)(2,1)S(1)} %all_to_all.28.refs_0_, bf16[256,128]{1,0:T(8,128)(2,1)S(1)} %copy-done.5, bf16[256,128]{1,0:T(8,128)(2,1)S(1)} %copy-done.4, bf16[128,256]{1,0:T(8,128)(2,1)S(1)} %copy-done.3, bf16[128,256]{1,0:T(8,128)(2,1)S(1)} %copy-done.2, ...), custom_call_target="tpu_custom_call" | custom-call | tf_op jit(solution)/shard_map/pallas_call | solution.py:212
  59.7 0.0 copy-start.1
  59.7 0.0 copy-start.7
  59.7 0.0 copy-start.8
  59.7 11.0 %all_to_all.29.arrived = bf16[32,16,128]{2,1,0:T(8,128)(2,1)S(1)} all-to-all(bf16[32,16,128]{2,1,0:T(8,128)(2,1)S(1)} %shard_map.198), channel_id=1, replica_groups={{21,1,2,3,4,5,6,7,8,9,10,11,12,13,14,15,16,17,18,19,20,0,22,23,24,25,26..., dimensions={0} | all-to-all | bytes 262144 | tf_op jit(solution)/shard_map/all_to_all | solution.py:549
  70.8 0.0 copy-done.1
  70.8 0.0 copy-done.7
  70.8 0.0 copy-done.8
  70.8 0.8 %shard_map.199 = (f32[10,32,128]{2,1,0:T(8,128)}, f32[3,4,128]{2,1,0:T(4,128)}) custom-call(f32[10,32,128]{2,1,0:T(8,128)S(1)} %copy-done.1, bf16[32,16,128]{2,1,0:T(8,128)(2,1)S(1)} %all_to_all.29.arrived, f32[3,4,128]{2,1,0:T(4,128)S(1)} %get-tuple-element.13.tile, f32[3,4,128]{2,1,0:T(4,128)S(1)} %copy-done.7, f32[3,4,128]{2,1,0:T(4,128)S(1)} %copy-done.8), custom_call_target="tpu_custom_call" | custom-call | tf_op jit(solution)/shard_map/pallas_call | solution.py:537
Async XLA Ops:
  0.6 16.8 %copy-start.6 = (f32[2,32,128]{2,1,0:T(8,128)S(1)}, f32[2,32,128]{2,1,0:T(8,128)}, u32[]{:S(2)}) copy-start(f32[2,32,128]{2,1,0:T(8,128)} %constant.14.clone.refs_5_) | copy-start | bytes 98308
  2.5 15.0 %copy-start.2 = (bf16[128,256]{1,0:T(8,128)(2,1)S(1)}, bf16[128,256]{1,0:T(8,128)(2,1)}, u32[]{:S(2)}) copy-start(bf16[128,256]{1,0:T(8,128)(2,1)} %constant.13.clone.refs_4_) | copy-start | bytes 196612
  2.5 15.0 %copy-start.3 = (bf16[128,256]{1,0:T(8,128)(2,1)S(1)}, bf16[128,256]{1,0:T(8,128)(2,1)}, u32[]{:S(2)}) copy-start(bf16[128,256]{1,0:T(8,128)(2,1)} %constant.12.clone.refs_3_) | copy-start | bytes 196612
  2.5 15.0 %copy-start.4 = (bf16[256,128]{1,0:T(8,128)(2,1)S(1)}, bf16[256,128]{1,0:T(8,128)(2,1)}, u32[]{:S(2)}) copy-start(bf16[256,128]{1,0:T(8,128)(2,1)} %constant.11.clone.refs_2_) | copy-start | bytes 196612
  2.5 14.9 %copy-start.5 = (bf16[256,128]{1,0:T(8,128)(2,1)S(1)}, bf16[256,128]{1,0:T(8,128)(2,1)}, u32[]{:S(2)}) copy-start(bf16[256,128]{1,0:T(8,128)(2,1)} %constant.10.clone.refs_1_) | copy-start | bytes 196612
  18.6 11.1 %copy-start = (bf16[10,3,32,128]{3,2,1,0:T(8,128)(2,1)S(1)}, bf16[10,3,32,128]{3,2,1,0:T(8,128)(2,1)}, u32[]{:S(2)}) copy-start(bf16[10,3,32,128]{3,2,1,0:T(8,128)(2,1)} %ensemble.5) | copy-start | bytes 737284
  59.7 11.1 %copy-start.1 = (f32[10,32,128]{2,1,0:T(8,128)S(1)}, f32[10,32,128]{2,1,0:T(8,128)}, u32[]{:S(2)}) copy-start(f32[10,32,128]{2,1,0:T(8,128)} %alpha.3) | copy-start | bytes 491524
  59.7 11.1 %copy-start.7 = (f32[3,4,128]{2,1,0:T(4,128)S(1)}, f32[3,4,128]{2,1,0:T(4,128)}, u32[]{:S(2)}) copy-start(f32[3,4,128]{2,1,0:T(4,128)} %std.3) | copy-start | bytes 18436
  59.7 11.1 %copy-start.8 = (f32[3,4,128]{2,1,0:T(4,128)S(1)}, f32[3,4,128]{2,1,0:T(4,128)}, u32[]{:S(2)}) copy-start(f32[3,4,128]{2,1,0:T(4,128)} %control.3) | copy-start | bytes 18436

commit v5 on v4

--- a/solution.py
+++ b/solution.py
@@ -25,8 +25,10 @@
 SLOT_COUNT = COLS // 16
 EXTRA = MEM - SLOT_COUNT
 COURANT = 0.4
-
-HEADS = (21, 21, 6, 21, 21)
+SUMMED = 3 * ROWS + 16
+LOAD = SUMMED + 32
+
+HEADS = (21, 21, 2, 21, 21)
 
 
 def places(count, head):
@@ -36,7 +38,7 @@
 
 
 FIRST, SECOND, THIRD, FOURTH, FIFTH = (
-    places(GROUPS if i == 2 else BLOCKS, head) for i, head in enumerate(HEADS)
+    places(GROUPS // 2 if i == 2 else BLOCKS, head) for i, head in enumerate(HEADS)
 )
 
 F32 = jnp.float32
@@ -388,22 +390,41 @@
         (totals[v] + on_own_rows(tiles[24 + 4 * v : 28 + 4 * v, :])).astype(BF16)
         for v in range(3)
     ]
-    parts.append((side + on_own_rows(static_rim)).astype(BF16))
+    side = side + on_own_rows(static_rim)
+    side = jnp.where(slot_of((16, COLS)) < 4, side[:16], turned(side[16:], COLS // 2))
+    parts.append(side.astype(BF16))
     parts.append(
         jnp.concatenate([tiles[:24, :], obs_rim, jnp.zeros((4, COLS), F32)], axis=0).astype(BF16)
     )
-    for i, part in enumerate(parts):
-        for g in range(GROUPS):
-            out[g, ROWS * i : ROWS * i + ROWS, :] = part
+    payload = jnp.concatenate(parts, axis=0)
+    out[...] = payload
 
 
 def partial_sums(ensemble, arrived, tiles):
     return call(
         contract,
-        jax.ShapeDtypeStruct((GROUPS, 5 * ROWS, COLS), BF16),
+        jax.ShapeDtypeStruct((LOAD, COLS), BF16),
         [VMEM((ROWS * SLOTS, COLS), F32)],
         3,
     )(ensemble, arrived, tiles)
+
+
+def add_pair(own, other, out):
+    low = lax.axis_index("grp") < GROUPS // 2
+    x = own[...].astype(F32)
+    y = other[...].astype(F32)
+    a, b = x[SUMMED:], y[SUMMED:]
+    payload = jnp.concatenate(
+        [x[:SUMMED] + y[:SUMMED], jnp.where(low, a, b), jnp.where(low, b, a)], axis=0
+    ).astype(BF16)
+    for g in range(GROUPS // 2):
+        out[g] = payload
+
+
+def pair_sums(own, other):
+    return call(
+        add_pair, jax.ShapeDtypeStruct((GROUPS // 2, LOAD + 32, COLS), BF16), (), 2
+    )(own, other)
 
 
 def observe(cell, step, innovation, weight, std, control, tiles, edges):
@@ -446,14 +467,15 @@
 def window(arrived, ensemble, sent, tile, flat, sums):
     own = lax.axis_index("grp")
     spread = 1.0 / math.sqrt(MEM * GROUPS - 1)
-    parts = []
-    for i in range(4):
-        total = arrived[0, ROWS * i : ROWS * i + ROWS, :].astype(F32)
-        for g in range(1, GROUPS):
-            total = total + arrived[g, ROWS * i : ROWS * i + ROWS, :].astype(F32)
-        parts.append(spread * total)
+    total = arrived[0, :SUMMED, :].astype(F32)
+    for g in range(1, GROUPS // 2):
+        total = total + arrived[g, :SUMMED, :].astype(F32)
+    total = spread * total
+    parts = [total[ROWS * v : ROWS * v + ROWS] for v in range(3)]
+    side = total[3 * ROWS :]
+    parts.append(jnp.concatenate([side, turned(side, COLS // 2)], axis=0))
     for g in range(GROUPS):
-        x = arrived[THIRD[g], 4 * ROWS : 5 * ROWS, :].astype(F32)
+        x = arrived[THIRD[g % 4], SUMMED + 32 * (g // 4) : LOAD + 32 * (g // 4), :].astype(F32)
         for f in range(7):
             sums[f, TILE_ROWS * g : TILE_ROWS * g + TILE_ROWS, :] = x[4 * f : 4 * f + 4]
     lane = lax.broadcasted_iota(jnp.int32, (ROWS, COLS), 1)
@@ -547,7 +569,7 @@
 
 def swap(x, axis, order):
     return lax.all_to_all(
-        x, axis, split_axis=0, concat_axis=0, tiled=True, axis_index_groups=[order]
+        x, axis, split_axis=0, concat_axis=0, tiled=True, axis_index_groups=[order] if axis == SP else [order, [i + GROUPS // 2 for i in order]]
     )
 
 
@@ -559,7 +581,9 @@
     )
     rows = swap(sent, SP, FIRST)
     localized = swap(localize(rows, weights, FIRST, SECOND, edges), SP, SECOND)
-    summed = swap(partial_sums(ensemble, localized, tiles), "grp", THIRD)
+    own = partial_sums(ensemble, localized, tiles)
+    other = lax.ppermute(own, "grp", [(i, (i + GROUPS // 2) % GROUPS) for i in range(GROUPS)])
+    summed = swap(pair_sums(own, other), "grp", THIRD)
     sent, tile = assimilate(summed, ensemble)
     filtered = swap(localize(swap(sent, SP, FOURTH), weights, FOURTH, FIFTH), SP, FIFTH)
     return finish(alpha, filtered, tile, static_std, control)

time: 71.9 us -> 71 us (0.987)
  blocking collectives: 65.5 us -> 57.6 us
  starting transfers between devices: 0 us -> 4.73 us
  waiting for transfers between devices: 0 us -> 2.17 us
    all_to_all x5, blocking collectives: 65.5 us -> 57.6 us  [swap(): lax.all_to_all(x, axis, split_axis=0, concat_axis=0, tiled=True, axis_ind...]
    ppermute x0 -> x1, starting transfers between devices: none -> 4.73 us  [per_device(): lax.ppermute(own, 'grp', [(i, (i + GROUPS // 2) % GROUPS) for i in range(...]
    ppermute x0 -> x1, waiting for transfers between devices: none -> 2.17 us  [per_device(): lax.ppermute(own, 'grp', [(i, (i + GROUPS // 2) % GROUPS) for i in range(...]
  transfers between devices with their start and end apart: 0 -> 1, of which waited for: 0 -> 1; matrix products, arithmetic and copies ran while one was open for 0% -> 0% of each run, Pallas kernels for 0% -> 0%
where the time goes in v5:
time: 71 us; the launch traced here: 70.6 us
  blocking collectives  57.6 us (81%)
  Pallas kernels  5.31 us (7%)
  starting transfers between devices  4.73 us (7%)
  waiting for transfers between devices  2.17 us (3%)
  between operations  0.77 us (1%)
    all_to_all x5, blocking collectives, swap(): lax.all_to_all(x, axis, split_axis=0, concat_axis=0, tiled=True, axis_ind...  57.6 us
    ppermute x1, starting transfers between devices, per_device(): lax.ppermute(own, 'grp', [(i, (i + GROUPS // 2) % GROUPS) for i in range(...  4.73 us
    ppermute x1, waiting for transfers between devices, per_device(): lax.ppermute(own, 'grp', [(i, (i + GROUPS // 2) % GROUPS) for i in range(...  2.17 us
    pallas_call x1, Pallas kernels, first_step(): pl.pallas_call(first_body, out_shape=[jax.ShapeDtypeStruct((ROWS, SLOTS,...  1.82 us
    pallas_call x2, Pallas kernels, localize(): call(functools.partial(filter_body, rims, come, go), jax.ShapeDtypeStruct...  1.8 us
  transfers between devices with their start and end apart: 1, of which 1 were waited for; matrix products, arithmetic and copies ran while one was open for 0% of the time, Pallas kernels for 0%

profile of v5, /device:TPU:1, one launch (start us, length us, event | category | flops | bytes accessed | tf_op | source)
XLA Modules:
  0.0 70.6 jit_solution(5530642702843002116)
XLA Ops:
  0.6 0.0 copy-start.6
  0.6 1.8 %shard_map.194 = (bf16[32,16,128]{2,1,0:T(8,128)(2,1)S(1)}, f32[36,128]{1,0:T(8,128)S(1)}, f32[8,128]{1,0:T(8,128)S(1)}, f32[32,128]{1,0:T(8,128)S(1)}) custom-call(f32[10,32,128]{2,1,0:T(8,128)} %alpha.3, bf16[10,3,32,128]{3,2,1,0:T(8,128)(2,1)} %ensemble.5, f32[8,128]{1,0:T(8,128)} %bitcast.5, s32[1,1024]{1,0:T(1,128)} %bitcast.6, s32[1,1024]{1,0:T(1,128)} %bitcast.7, ...), custom_call_target="tpu_custom_call" | custom-call | tf_op jit(solution)/shard_map/pallas_call | solution.py:313
  2.5 0.0 copy-start.2
  2.5 0.0 copy-start.3
  2.5 0.0 copy-start.4
  2.5 0.0 copy-start.5
  2.5 14.9 %all_to_all.25.refs_0_ = bf16[32,16,128]{2,1,0:T(8,128)(2,1)S(1)} all-to-all(bf16[32,16,128]{2,1,0:T(8,128)(2,1)S(1)} %get-tuple-element.8), channel_id=1, replica_groups={{21,1,2,3,4,5,6,7,8,9,10,11,12,13,14,15,16,17,18,19,20,0,22,23,24,25,26..., dimensions={0} | all-to-all | bytes 262144 | tf_op jit(solution)/shard_map/all_to_all | solution.py:571
  17.4 0.0 copy-done.6
  17.4 0.0 copy-done.2
  17.4 0.0 copy-done.3
  17.4 0.0 copy-done.4
  17.5 0.0 copy-done.5
  17.5 1.1 %shard_map.195 = bf16[32,16,128]{2,1,0:T(8,128)(2,1)S(1)} custom-call(bf16[32,16,128]{2,1,0:T(8,128)(2,1)S(1)} %all_to_all.25.refs_0_, bf16[256,128]{1,0:T(8,128)(2,1)S(1)} %copy-done.5, bf16[256,128]{1,0:T(8,128)(2,1)S(1)} %copy-done.4, bf16[128,256]{1,0:T(8,128)(2,1)S(1)} %copy-done.3, bf16[128,256]{1,0:T(8,128)(2,1)S(1)} %copy-done.2, ...), custom_call_target="tpu_custom_call" | custom-call | tf_op jit(solution)/shard_map/pallas_call | solution.py:214
  18.6 0.0 copy-start
  18.6 11.0 %all_to_all.26.arrived = bf16[32,16,128]{2,1,0:T(8,128)(2,1)S(1)} all-to-all(bf16[32,16,128]{2,1,0:T(8,128)(2,1)S(1)} %shard_map.195), channel_id=1, replica_groups={{21,1,2,3,4,5,6,7,8,9,10,11,12,13,14,15,16,17,18,19,20,0,22,23,24,25,26..., dimensions={0} | all-to-all | bytes 262144 | tf_op jit(solution)/shard_map/all_to_all | solution.py:571
  29.6 0.0 copy-done
  29.6 0.2 shard_map.196.own
  29.8 4.7 %collective-permute-start = (bf16[144,128]{1,0:T(8,128)(2,1)S(1)}, bf16[144,128]{1,0:T(8,128)(2,1)S(1)}, u32[]{:S(2)}, u32[]{:S(2)}) collective-permute-start(bf16[144,128]{1,0:T(8,128)(2,1)S(1)} %shard_map.196.own), channel_id=1, source_target_pairs={{0,128},{32,160},{64,192},{96,224},{128,0},{160,32},{192,64},{224,... | collective-permute-start | bytes 110600 | tf_op jit(solution)/shard_map/ppermute | solution.py:585
  34.5 2.2 %collective-permute-done.other = bf16[144,128]{1,0:T(8,128)(2,1)S(1)} collective-permute-done((bf16[144,128]{1,0:T(8,128)(2,1)S(1)}, bf16[144,128]{1,0:T(8,128)(2,1)S(1)}, u32[]{:S(2)}, u32[]{:S(2)}) %collective-permute-start) | collective-permute-done | bytes 36896 | tf_op jit(solution)/shard_map/ppermute | solution.py:585
  36.7 7.7 %all_to_all.27.arrived = bf16[4,176,128]{2,1,0:T(8,128)(2,1)S(1)} all-to-all(bf16[4,176,128]{2,1,0:T(8,128)(2,1)S(1)} %shard_map.197), channel_id=1, replica_groups={{64,32,0,96},{192,160,128,224},{65,33,1,97},{193,161,129,225},{66,34,2,..., dimensions={0} | all-to-all | bytes 360448 | tf_op jit(solution)/shard_map/all_to_all | solution.py:571
  44.4 0.7 %shard_map.198 = (bf16[32,16,128]{2,1,0:T(8,128)(2,1)S(1)}, f32[3,4,128]{2,1,0:T(4,128)S(1)}) custom-call(bf16[4,176,128]{2,1,0:T(8,128)(2,1)S(1)} %all_to_all.27.arrived, bf16[10,3,32,128]{3,2,1,0:T(8,128)(2,1)S(1)} %copy-done), custom_call_target="tpu_custom_call" | custom-call | tf_op jit(solution)/shard_map/pallas_call | solution.py:537
  45.2 12.9 %all_to_all.28.refs_0_ = bf16[32,16,128]{2,1,0:T(8,128)(2,1)S(1)} all-to-all(bf16[32,16,128]{2,1,0:T(8,128)(2,1)S(1)} %get-tuple-element.12), channel_id=1, replica_groups={{21,1,2,3,4,5,6,7,8,9,10,11,12,13,14,15,16,17,18,19,20,0,22,23,24,25,26..., dimensions={0} | all-to-all | bytes 262144 | tf_op jit(solution)/shard_map/all_to_all | solution.py:571
  58.1 0.7 %shard_map.199 = bf16[32,16,128]{2,1,0:T(8,128)(2,1)S(1)} custom-call(bf16[32,16,128]{2,1,0:T(8,128)(2,1)S(1)} %all_to_all.28.refs_0_, bf16[256,128]{1,0:T(8,128)(2,1)S(1)} %copy-done.5, bf16[256,128]{1,0:T(8,128)(2,1)S(1)} %copy-done.4, bf16[128,256]{1,0:T(8,128)(2,1)S(1)} %copy-done.3, bf16[128,256]{1,0:T(8,128)(2,1)S(1)} %copy-done.2, ...), custom_call_target="tpu_custom_call" | custom-call | tf_op jit(solution)/shard_map/pallas_call | solution.py:214
  58.8 0.0 copy-start.1
  58.8 0.0 copy-start.7
  58.8 0.0 copy-start.8
  58.8 11.0 %all_to_all.29.arrived = bf16[32,16,128]{2,1,0:T(8,128)(2,1)S(1)} all-to-all(bf16[32,16,128]{2,1,0:T(8,128)(2,1)S(1)} %shard_map.199), channel_id=1, replica_groups={{21,1,2,3,4,5,6,7,8,9,10,11,12,13,14,15,16,17,18,19,20,0,22,23,24,25,26..., dimensions={0} | all-to-all | bytes 262144 | tf_op jit(solution)/shard_map/all_to_all | solution.py:571
  69.9 0.0 copy-done.1
  69.9 0.0 copy-done.7
  69.9 0.0 copy-done.8
  69.9 0.8 %shard_map.200 = (f32[10,32,128]{2,1,0:T(8,128)}, f32[3,4,128]{2,1,0:T(4,128)}) custom-call(f32[10,32,128]{2,1,0:T(8,128)S(1)} %copy-done.1, bf16[32,16,128]{2,1,0:T(8,128)(2,1)S(1)} %all_to_all.29.arrived, f32[3,4,128]{2,1,0:T(4,128)S(1)} %get-tuple-element.13.tile, f32[3,4,128]{2,1,0:T(4,128)S(1)} %copy-done.7, f32[3,4,128]{2,1,0:T(4,128)S(1)} %copy-done.8), custom_call_target="tpu_custom_call" | custom-call | tf_op jit(solution)/shard_map/pallas_call | solution.py:559
  (1 shorter events, 0.0 us)
Async XLA Ops:
  0.6 16.8 %copy-start.6 = (f32[2,32,128]{2,1,0:T(8,128)S(1)}, f32[2,32,128]{2,1,0:T(8,128)}, u32[]{:S(2)}) copy-start(f32[2,32,128]{2,1,0:T(8,128)} %constant.14.clone.refs_5_) | copy-start | bytes 98308
  2.5 15.0 %copy-start.2 = (bf16[128,256]{1,0:T(8,128)(2,1)S(1)}, bf16[128,256]{1,0:T(8,128)(2,1)}, u32[]{:S(2)}) copy-start(bf16[128,256]{1,0:T(8,128)(2,1)} %constant.13.clone.refs_4_) | copy-start | bytes 196612
  2.5 15.0 %copy-start.3 = (bf16[128,256]{1,0:T(8,128)(2,1)S(1)}, bf16[128,256]{1,0:T(8,128)(2,1)}, u32[]{:S(2)}) copy-start(bf16[128,256]{1,0:T(8,128)(2,1)} %constant.12.clone.refs_3_) | copy-start | bytes 196612
  2.5 15.0 %copy-start.4 = (bf16[256,128]{1,0:T(8,128)(2,1)S(1)}, bf16[256,128]{1,0:T(8,128)(2,1)}, u32[]{:S(2)}) copy-start(bf16[256,128]{1,0:T(8,128)(2,1)} %constant.11.clone.refs_2_) | copy-start | bytes 196612
  2.5 14.9 %copy-start.5 = (bf16[256,128]{1,0:T(8,128)(2,1)S(1)}, bf16[256,128]{1,0:T(8,128)(2,1)}, u32[]{:S(2)}) copy-start(bf16[256,128]{1,0:T(8,128)(2,1)} %constant.10.clone.refs_1_) | copy-start | bytes 196612
  18.6 11.1 %copy-start = (bf16[10,3,32,128]{3,2,1,0:T(8,128)(2,1)S(1)}, bf16[10,3,32,128]{3,2,1,0:T(8,128)(2,1)}, u32[]{:S(2)}) copy-start(bf16[10,3,32,128]{3,2,1,0:T(8,128)(2,1)} %ensemble.5) | copy-start | bytes 737284
  29.8 6.9 %collective-permute-start = (bf16[144,128]{1,0:T(8,128)(2,1)S(1)}, bf16[144,128]{1,0:T(8,128)(2,1)S(1)}, u32[]{:S(2)}, u32[]{:S(2)}) collective-permute-start(bf16[144,128]{1,0:T(8,128)(2,1)S(1)} %shard_map.196.own), channel_id=1, source_target_pairs={{0,128},{32,160},{64,192},{96,224},{128,0},{160,32},{192,64},{224,... | collective-permute-start | bytes 110600 | tf_op jit(solution)/shard_map/ppermute | solution.py:585
  58.8 11.1 %copy-start.1 = (f32[10,32,128]{2,1,0:T(8,128)S(1)}, f32[10,32,128]{2,1,0:T(8,128)}, u32[]{:S(2)}) copy-start(f32[10,32,128]{2,1,0:T(8,128)} %alpha.3) | copy-start | bytes 491524
  58.8 11.1 %copy-start.7 = (f32[3,4,128]{2,1,0:T(4,128)S(1)}, f32[3,4,128]{2,1,0:T(4,128)}, u32[]{:S(2)}) copy-start(f32[3,4,128]{2,1,0:T(4,128)} %std.3) | copy-start | bytes 18436
  58.8 11.1 %copy-start.8 = (f32[3,4,128]{2,1,0:T(4,128)S(1)}, f32[3,4,128]{2,1,0:T(4,128)}, u32[]{:S(2)}) copy-start(f32[3,4,128]{2,1,0:T(4,128)} %control.3) | copy-start | bytes 18436

commit v6 on v5

--- a/solution.py
+++ b/solution.py
@@ -111,9 +111,9 @@
     xh = x.astype(BF16)
     xl = (x - xh.astype(F32)).astype(BF16)
     h = high[...]
-    total = jnp.dot(xl, h, preferred_element_type=F32)
-    total = total + jnp.dot(xh, low[...], preferred_element_type=F32)
-    return total + jnp.dot(xh, h, preferred_element_type=F32)
+    n = x.shape[0]
+    both = jnp.dot(jnp.concatenate([xl, xh], axis=0), h, preferred_element_type=F32)
+    return both[:n] + jnp.dot(xh, low[...], preferred_element_type=F32) + both[n:]
 
 
 def slot_of(shape):
@@ -244,7 +244,7 @@
     out[...] = h + turned(h, 2 * BLOCKS)
 
 
-PIECE = 2
+PIECE = 10
 SMALL = 7
 
 
@@ -442,11 +442,13 @@
     mid = rest.astype(BF16)
     low = (rest - mid.astype(F32)).astype(BF16)
     hot = (lax.broadcasted_iota(jnp.int32, (COLS, count), 0) == column).astype(F32).astype(BF16)
-    total = jnp.zeros((2 * n, COLS), F32)
-    for piece in (low, mid, high):
-        total = total + lax.dot_general(
-            piece, hot, (((1,), (1,)), ((), ())), preferred_element_type=F32
-        )
+    pieces = lax.dot_general(
+        jnp.concatenate([low.astype(F32), mid.astype(F32), high.astype(F32)], axis=0).astype(BF16),
+        hot,
+        (((1,), (1,)), ((), ())),
+        preferred_element_type=F32,
+    )
+    total = pieces[: 2 * n] + pieces[2 * n : 4 * n] + pieces[4 * n :]
     static = [std[v] * control[v] for v in range(3)]
     tiles[:24, :] = total
     for v in range(3):

time: 71 us -> 70.5 us (level)
  no operation moved by 1% of the time
where the time goes in v6:
time: 70.5 us; the launch traced here: 70.2 us
  blocking collectives  57.6 us (82%)
  Pallas kernels  4.89 us (7%)
  starting transfers between devices  4.74 us (7%)
  waiting for transfers between devices  2.16 us (3%)
  between operations  0.77 us (1%)
    all_to_all x5, blocking collectives, swap(): lax.all_to_all(x, axis, split_axis=0, concat_axis=0, tiled=True, axis_ind...  57.6 us
    ppermute x1, starting transfers between devices, per_device(): lax.ppermute(own, 'grp', [(i, (i + GROUPS // 2) % GROUPS) for i in range(...  4.74 us
    ppermute x1, waiting for transfers between devices, per_device(): lax.ppermute(own, 'grp', [(i, (i + GROUPS // 2) % GROUPS) for i in range(...  2.16 us
    pallas_call x2, Pallas kernels, localize(): call(functools.partial(filter_body, rims, come, go), jax.ShapeDtypeStruct...  1.71 us
    pallas_call x1, Pallas kernels, first_step(): pl.pallas_call(first_body, out_shape=[jax.ShapeDtypeStruct((ROWS, SLOTS,...  1.47 us
  transfers between devices with their start and end apart: 1, of which 1 were waited for; matrix products, arithmetic and copies ran while one was open for 0% of the time, Pallas kernels for 0%

profile of v6, /device:TPU:1, one launch (start us, length us, event | category | flops | bytes accessed | tf_op | source)
XLA Modules:
  0.0 70.2 jit_solution(3132608948020198648)
XLA Ops:
  0.6 0.0 copy-start.6
  0.6 1.5 %shard_map.194 = (bf16[32,16,128]{2,1,0:T(8,128)(2,1)S(1)}, f32[36,128]{1,0:T(8,128)S(1)}, f32[8,128]{1,0:T(8,128)S(1)}, f32[32,128]{1,0:T(8,128)S(1)}) custom-call(f32[10,32,128]{2,1,0:T(8,128)} %alpha.3, bf16[10,3,32,128]{3,2,1,0:T(8,128)(2,1)} %ensemble.5, f32[8,128]{1,0:T(8,128)} %bitcast.5, s32[1,1024]{1,0:T(1,128)} %bitcast.6, s32[1,1024]{1,0:T(1,128)} %bitcast.7, ...), custom_call_target="tpu_custom_call" | custom-call | tf_op jit(solution)/shard_map/pallas_call | solution.py:313
  2.1 0.0 copy-start.2
  2.1 0.0 copy-start.3
  2.2 0.0 copy-start.4
  2.2 0.0 copy-start.5
  2.2 14.9 %all_to_all.25.refs_0_ = bf16[32,16,128]{2,1,0:T(8,128)(2,1)S(1)} all-to-all(bf16[32,16,128]{2,1,0:T(8,128)(2,1)S(1)} %get-tuple-element.8), channel_id=1, replica_groups={{21,1,2,3,4,5,6,7,8,9,10,11,12,13,14,15,16,17,18,19,20,0,22,23,24,25,26..., dimensions={0} | all-to-all | bytes 262144 | tf_op jit(solution)/shard_map/all_to_all | solution.py:573
  17.1 0.0 copy-done.6
  17.1 0.0 copy-done.2
  17.1 0.0 copy-done.3
  17.1 0.0 copy-done.4
  17.1 0.0 copy-done.5
  17.1 1.0 %shard_map.195 = bf16[32,16,128]{2,1,0:T(8,128)(2,1)S(1)} custom-call(bf16[32,16,128]{2,1,0:T(8,128)(2,1)S(1)} %all_to_all.25.refs_0_, bf16[256,128]{1,0:T(8,128)(2,1)S(1)} %copy-done.5, bf16[256,128]{1,0:T(8,128)(2,1)S(1)} %copy-done.4, bf16[128,256]{1,0:T(8,128)(2,1)S(1)} %copy-done.3, bf16[128,256]{1,0:T(8,128)(2,1)S(1)} %copy-done.2, ...), custom_call_target="tpu_custom_call" | custom-call | tf_op jit(solution)/shard_map/pallas_call | solution.py:214
  18.2 0.0 copy-start
  18.2 11.0 %all_to_all.26.arrived = bf16[32,16,128]{2,1,0:T(8,128)(2,1)S(1)} all-to-all(bf16[32,16,128]{2,1,0:T(8,128)(2,1)S(1)} %shard_map.195), channel_id=1, replica_groups={{21,1,2,3,4,5,6,7,8,9,10,11,12,13,14,15,16,17,18,19,20,0,22,23,24,25,26..., dimensions={0} | all-to-all | bytes 262144 | tf_op jit(solution)/shard_map/all_to_all | solution.py:573
  29.2 0.0 copy-done
  29.2 0.2 shard_map.196.own
  29.4 4.7 %collective-permute-start = (bf16[144,128]{1,0:T(8,128)(2,1)S(1)}, bf16[144,128]{1,0:T(8,128)(2,1)S(1)}, u32[]{:S(2)}, u32[]{:S(2)}) collective-permute-start(bf16[144,128]{1,0:T(8,128)(2,1)S(1)} %shard_map.196.own), channel_id=1, source_target_pairs={{0,128},{32,160},{64,192},{96,224},{128,0},{160,32},{192,64},{224,... | collective-permute-start | bytes 110600 | tf_op jit(solution)/shard_map/ppermute | solution.py:587
  34.1 2.2 %collective-permute-done.other = bf16[144,128]{1,0:T(8,128)(2,1)S(1)} collective-permute-done((bf16[144,128]{1,0:T(8,128)(2,1)S(1)}, bf16[144,128]{1,0:T(8,128)(2,1)S(1)}, u32[]{:S(2)}, u32[]{:S(2)}) %collective-permute-start) | collective-permute-done | bytes 36896 | tf_op jit(solution)/shard_map/ppermute | solution.py:587
  36.3 7.7 %all_to_all.27.arrived = bf16[4,176,128]{2,1,0:T(8,128)(2,1)S(1)} all-to-all(bf16[4,176,128]{2,1,0:T(8,128)(2,1)S(1)} %shard_map.197), channel_id=1, replica_groups={{64,32,0,96},{192,160,128,224},{65,33,1,97},{193,161,129,225},{66,34,2,..., dimensions={0} | all-to-all | bytes 360448 | tf_op jit(solution)/shard_map/all_to_all | solution.py:573
  44.0 0.7 %shard_map.198 = (bf16[32,16,128]{2,1,0:T(8,128)(2,1)S(1)}, f32[3,4,128]{2,1,0:T(4,128)S(1)}) custom-call(bf16[4,176,128]{2,1,0:T(8,128)(2,1)S(1)} %all_to_all.27.arrived, bf16[10,3,32,128]{3,2,1,0:T(8,128)(2,1)S(1)} %copy-done), custom_call_target="tpu_custom_call" | custom-call | tf_op jit(solution)/shard_map/pallas_call | solution.py:539
  44.8 12.9 %all_to_all.28.refs_0_ = bf16[32,16,128]{2,1,0:T(8,128)(2,1)S(1)} all-to-all(bf16[32,16,128]{2,1,0:T(8,128)(2,1)S(1)} %get-tuple-element.12), channel_id=1, replica_groups={{21,1,2,3,4,5,6,7,8,9,10,11,12,13,14,15,16,17,18,19,20,0,22,23,24,25,26..., dimensions={0} | all-to-all | bytes 262144 | tf_op jit(solution)/shard_map/all_to_all | solution.py:573
  57.7 0.7 shard_map.199
  58.4 0.0 copy-start.1
  58.4 0.0 copy-start.7
  58.4 0.0 copy-start.8
  58.4 11.0 %all_to_all.29.arrived = bf16[32,16,128]{2,1,0:T(8,128)(2,1)S(1)} all-to-all(bf16[32,16,128]{2,1,0:T(8,128)(2,1)S(1)} %shard_map.199), channel_id=1, replica_groups={{21,1,2,3,4,5,6,7,8,9,10,11,12,13,14,15,16,17,18,19,20,0,22,23,24,25,26..., dimensions={0} | all-to-all | bytes 262144 | tf_op jit(solution)/shard_map/all_to_all | solution.py:573
  69.4 0.0 copy-done.1
  69.4 0.0 copy-done.7
  69.5 0.0 copy-done.8
  69.5 0.8 %shard_map.200 = (f32[10,32,128]{2,1,0:T(8,128)}, f32[3,4,128]{2,1,0:T(4,128)}) custom-call(f32[10,32,128]{2,1,0:T(8,128)S(1)} %copy-done.1, bf16[32,16,128]{2,1,0:T(8,128)(2,1)S(1)} %all_to_all.29.arrived, f32[3,4,128]{2,1,0:T(4,128)S(1)} %get-tuple-element.13.tile, f32[3,4,128]{2,1,0:T(4,128)S(1)} %copy-done.7, f32[3,4,128]{2,1,0:T(4,128)S(1)} %copy-done.8), custom_call_target="tpu_custom_call" | custom-call | tf_op jit(solution)/shard_map/pallas_call | solution.py:561
  (1 shorter events, 0.0 us)
Async XLA Ops:
  0.6 16.5 %copy-start.6 = (f32[2,32,128]{2,1,0:T(8,128)S(1)}, f32[2,32,128]{2,1,0:T(8,128)}, u32[]{:S(2)}) copy-start(f32[2,32,128]{2,1,0:T(8,128)} %constant.14.clone.refs_5_) | copy-start | bytes 98308
  2.1 15.0 %copy-start.2 = (bf16[128,256]{1,0:T(8,128)(2,1)S(1)}, bf16[128,256]{1,0:T(8,128)(2,1)}, u32[]{:S(2)}) copy-start(bf16[128,256]{1,0:T(8,128)(2,1)} %constant.13.clone.refs_4_) | copy-start | bytes 196612
  2.1 15.0 %copy-start.3 = (bf16[128,256]{1,0:T(8,128)(2,1)S(1)}, bf16[128,256]{1,0:T(8,128)(2,1)}, u32[]{:S(2)}) copy-start(bf16[128,256]{1,0:T(8,128)(2,1)} %constant.12.clone.refs_3_) | copy-start | bytes 196612
  2.2 14.9 %copy-start.4 = (bf16[256,128]{1,0:T(8,128)(2,1)S(1)}, bf16[256,128]{1,0:T(8,128)(2,1)}, u32[]{:S(2)}) copy-start(bf16[256,128]{1,0:T(8,128)(2,1)} %constant.11.clone.refs_2_) | copy-start | bytes 196612
  2.2 14.9 %copy-start.5 = (bf16[256,128]{1,0:T(8,128)(2,1)S(1)}, bf16[256,128]{1,0:T(8,128)(2,1)}, u32[]{:S(2)}) copy-start(bf16[256,128]{1,0:T(8,128)(2,1)} %constant.10.clone.refs_1_) | copy-start | bytes 196612
  18.2 11.1 %copy-start = (bf16[10,3,32,128]{3,2,1,0:T(8,128)(2,1)S(1)}, bf16[10,3,32,128]{3,2,1,0:T(8,128)(2,1)}, u32[]{:S(2)}) copy-start(bf16[10,3,32,128]{3,2,1,0:T(8,128)(2,1)} %ensemble.5) | copy-start | bytes 737284
  29.4 6.9 %collective-permute-start = (bf16[144,128]{1,0:T(8,128)(2,1)S(1)}, bf16[144,128]{1,0:T(8,128)(2,1)S(1)}, u32[]{:S(2)}, u32[]{:S(2)}) collective-permute-start(bf16[144,128]{1,0:T(8,128)(2,1)S(1)} %shard_map.196.own), channel_id=1, source_target_pairs={{0,128},{32,160},{64,192},{96,224},{128,0},{160,32},{192,64},{224,... | collective-permute-start | bytes 110600 | tf_op jit(solution)/shard_map/ppermute | solution.py:587
  58.4 11.1 %copy-start.1 = (f32[10,32,128]{2,1,0:T(8,128)S(1)}, f32[10,32,128]{2,1,0:T(8,128)}, u32[]{:S(2)}) copy-start(f32[10,32,128]{2,1,0:T(8,128)} %alpha.3) | copy-start | bytes 491524
  58.4 11.1 %copy-start.7 = (f32[3,4,128]{2,1,0:T(4,128)S(1)}, f32[3,4,128]{2,1,0:T(4,128)}, u32[]{:S(2)}) copy-start(f32[3,4,128]{2,1,0:T(4,128)} %std.3) | copy-start | bytes 18436
  58.4 11.1 %copy-start.8 = (f32[3,4,128]{2,1,0:T(4,128)S(1)}, f32[3,4,128]{2,1,0:T(4,128)}, u32[]{:S(2)}) copy-start(f32[3,4,128]{2,1,0:T(4,128)} %control.3) | copy-start | bytes 18436

commit v7 on v6

--- a/solution.py
+++ b/solution.py
@@ -199,11 +199,14 @@
             t = t + turned(t, by)
         side = jnp.where(slot == v, t, side)
     side = jnp.where(right, pltpu.roll(side, BLOCKS - 1, 0), pltpu.roll(side, 1, 0))
-    flat[pl.ds(MEM, BLOCKS, stride=SLOTS), :] = side
-    own_edges = edges[:5, :]
+    spec[:BLOCKS, :] = side
+    sub = lax.broadcasted_iota(jnp.int32, (8, COLS), 0)
+    own_edges = pltpu.roll(edges[...], MEM - 8 + 1, 0)
     for p in range(BLOCKS):
-        flat[SLOTS * p + MEM + 1 : SLOTS * p + SLOTS, :] = own_edges
-        out[go[p]] = flat[SLOTS * p : SLOTS * p + SLOTS, :].astype(BF16)
+        late = flat[SLOTS * p + 8 : SLOTS * p + SLOTS, :]
+        late = jnp.where(sub < MEM - 8, late, own_edges)
+        late = jnp.where(sub == MEM - 8, spec[p : p + 1, :], late)
+        out[go[p]] = jnp.concatenate([flat[SLOTS * p : SLOTS * p + 8, :], late], axis=0).astype(BF16)
 
 
 def localize(rows, weights, come, go, edges=None):

time: 70.5 us -> 70.5 us (level)
  no operation moved by 1% of the time
where the time goes in v7:
time: 70.5 us; the launch traced here: 70.2 us
  blocking collectives  57.6 us (82%)
  Pallas kernels  4.88 us (7%)
  starting transfers between devices  4.74 us (7%)
  waiting for transfers between devices  2.16 us (3%)
  between operations  0.77 us (1%)
    all_to_all x5, blocking collectives, swap(): lax.all_to_all(x, axis, split_axis=0, concat_axis=0, tiled=True, axis_ind...  57.6 us
    ppermute x1, starting transfers between devices, per_device(): lax.ppermute(own, 'grp', [(i, (i + GROUPS // 2) % GROUPS) for i in range(...  4.74 us
    ppermute x1, waiting for transfers between devices, per_device(): lax.ppermute(own, 'grp', [(i, (i + GROUPS // 2) % GROUPS) for i in range(...  2.16 us
    pallas_call x2, Pallas kernels, localize(): call(functools.partial(filter_body, rims, come, go), jax.ShapeDtypeStruct...  1.71 us
    pallas_call x1, Pallas kernels, first_step(): pl.pallas_call(first_body, out_shape=[jax.ShapeDtypeStruct((ROWS, SLOTS,...  1.47 us
  transfers between devices with their start and end apart: 1, of which 1 were waited for; matrix products, arithmetic and copies ran while one was open for 0% of the time, Pallas kernels for 0%

profile of v7, /device:TPU:1, one launch (start us, length us, event | category | flops | bytes accessed | tf_op | source)
XLA Modules:
  0.0 70.2 jit_solution(1707539618662832805)
XLA Ops:
  0.6 0.0 copy-start.6
  0.6 1.5 %shard_map.194 = (bf16[32,16,128]{2,1,0:T(8,128)(2,1)S(1)}, f32[36,128]{1,0:T(8,128)S(1)}, f32[8,128]{1,0:T(8,128)S(1)}, f32[32,128]{1,0:T(8,128)S(1)}) custom-call(f32[10,32,128]{2,1,0:T(8,128)} %alpha.3, bf16[10,3,32,128]{3,2,1,0:T(8,128)(2,1)} %ensemble.5, f32[8,128]{1,0:T(8,128)} %bitcast.5, s32[1,1024]{1,0:T(1,128)} %bitcast.6, s32[1,1024]{1,0:T(1,128)} %bitcast.7, ...), custom_call_target="tpu_custom_call" | custom-call | tf_op jit(solution)/shard_map/pallas_call | solution.py:316
  2.1 0.0 copy-start.2
  2.1 0.0 copy-start.3
  2.2 0.0 copy-start.4
  2.2 0.0 copy-start.5
  2.2 14.9 %all_to_all.25.refs_0_ = bf16[32,16,128]{2,1,0:T(8,128)(2,1)S(1)} all-to-all(bf16[32,16,128]{2,1,0:T(8,128)(2,1)S(1)} %get-tuple-element.8), channel_id=1, replica_groups={{21,1,2,3,4,5,6,7,8,9,10,11,12,13,14,15,16,17,18,19,20,0,22,23,24,25,26..., dimensions={0} | all-to-all | bytes 262144 | tf_op jit(solution)/shard_map/all_to_all | solution.py:576
  17.1 0.0 copy-done.6
  17.1 0.0 copy-done.2
  17.1 0.0 copy-done.3
  17.1 0.0 copy-done.4
  17.1 0.0 copy-done.5
  17.1 1.0 %shard_map.195 = bf16[32,16,128]{2,1,0:T(8,128)(2,1)S(1)} custom-call(bf16[32,16,128]{2,1,0:T(8,128)(2,1)S(1)} %all_to_all.25.refs_0_, bf16[256,128]{1,0:T(8,128)(2,1)S(1)} %copy-done.5, bf16[256,128]{1,0:T(8,128)(2,1)S(1)} %copy-done.4, bf16[128,256]{1,0:T(8,128)(2,1)S(1)} %copy-done.3, bf16[128,256]{1,0:T(8,128)(2,1)S(1)} %copy-done.2, ...), custom_call_target="tpu_custom_call" | custom-call | tf_op jit(solution)/shard_map/pallas_call | solution.py:217
  18.2 0.0 copy-start
  18.2 11.0 %all_to_all.26.arrived = bf16[32,16,128]{2,1,0:T(8,128)(2,1)S(1)} all-to-all(bf16[32,16,128]{2,1,0:T(8,128)(2,1)S(1)} %shard_map.195), channel_id=1, replica_groups={{21,1,2,3,4,5,6,7,8,9,10,11,12,13,14,15,16,17,18,19,20,0,22,23,24,25,26..., dimensions={0} | all-to-all | bytes 262144 | tf_op jit(solution)/shard_map/all_to_all | solution.py:576
  29.2 0.0 copy-done
  29.2 0.2 shard_map.196.own
  29.4 4.7 %collective-permute-start = (bf16[144,128]{1,0:T(8,128)(2,1)S(1)}, bf16[144,128]{1,0:T(8,128)(2,1)S(1)}, u32[]{:S(2)}, u32[]{:S(2)}) collective-permute-start(bf16[144,128]{1,0:T(8,128)(2,1)S(1)} %shard_map.196.own), channel_id=1, source_target_pairs={{0,128},{32,160},{64,192},{96,224},{128,0},{160,32},{192,64},{224,... | collective-permute-start | bytes 110600 | tf_op jit(solution)/shard_map/ppermute | solution.py:590
  34.1 2.2 %collective-permute-done.other = bf16[144,128]{1,0:T(8,128)(2,1)S(1)} collective-permute-done((bf16[144,128]{1,0:T(8,128)(2,1)S(1)}, bf16[144,128]{1,0:T(8,128)(2,1)S(1)}, u32[]{:S(2)}, u32[]{:S(2)}) %collective-permute-start) | collective-permute-done | bytes 36896 | tf_op jit(solution)/shard_map/ppermute | solution.py:590
  36.3 7.7 %all_to_all.27.arrived = bf16[4,176,128]{2,1,0:T(8,128)(2,1)S(1)} all-to-all(bf16[4,176,128]{2,1,0:T(8,128)(2,1)S(1)} %shard_map.197), channel_id=1, replica_groups={{64,32,0,96},{192,160,128,224},{65,33,1,97},{193,161,129,225},{66,34,2,..., dimensions={0} | all-to-all | bytes 360448 | tf_op jit(solution)/shard_map/all_to_all | solution.py:576
  44.0 0.7 %shard_map.198 = (bf16[32,16,128]{2,1,0:T(8,128)(2,1)S(1)}, f32[3,4,128]{2,1,0:T(4,128)S(1)}) custom-call(bf16[4,176,128]{2,1,0:T(8,128)(2,1)S(1)} %all_to_all.27.arrived, bf16[10,3,32,128]{3,2,1,0:T(8,128)(2,1)S(1)} %copy-done), custom_call_target="tpu_custom_call" | custom-call | tf_op jit(solution)/shard_map/pallas_call | solution.py:542
  44.8 12.9 %all_to_all.28.refs_0_ = bf16[32,16,128]{2,1,0:T(8,128)(2,1)S(1)} all-to-all(bf16[32,16,128]{2,1,0:T(8,128)(2,1)S(1)} %get-tuple-element.12), channel_id=1, replica_groups={{21,1,2,3,4,5,6,7,8,9,10,11,12,13,14,15,16,17,18,19,20,0,22,23,24,25,26..., dimensions={0} | all-to-all | bytes 262144 | tf_op jit(solution)/shard_map/all_to_all | solution.py:576
  57.7 0.7 shard_map.199
  58.4 0.0 copy-start.1
  58.4 0.0 copy-start.7
  58.4 0.0 copy-start.8
  58.4 11.0 %all_to_all.29.arrived = bf16[32,16,128]{2,1,0:T(8,128)(2,1)S(1)} all-to-all(bf16[32,16,128]{2,1,0:T(8,128)(2,1)S(1)} %shard_map.199), channel_id=1, replica_groups={{21,1,2,3,4,5,6,7,8,9,10,11,12,13,14,15,16,17,18,19,20,0,22,23,24,25,26..., dimensions={0} | all-to-all | bytes 262144 | tf_op jit(solution)/shard_map/all_to_all | solution.py:576
  69.4 0.0 copy-done.1
  69.4 0.0 copy-done.7
  69.4 0.0 copy-done.8
  69.5 0.8 %shard_map.200 = (f32[10,32,128]{2,1,0:T(8,128)}, f32[3,4,128]{2,1,0:T(4,128)}) custom-call(f32[10,32,128]{2,1,0:T(8,128)S(1)} %copy-done.1, bf16[32,16,128]{2,1,0:T(8,128)(2,1)S(1)} %all_to_all.29.arrived, f32[3,4,128]{2,1,0:T(4,128)S(1)} %get-tuple-element.13.tile, f32[3,4,128]{2,1,0:T(4,128)S(1)} %copy-done.7, f32[3,4,128]{2,1,0:T(4,128)S(1)} %copy-done.8), custom_call_target="tpu_custom_call" | custom-call | tf_op jit(solution)/shard_map/pallas_call | solution.py:564
  (1 shorter events, 0.0 us)
Async XLA Ops:
  0.6 16.5 %copy-start.6 = (f32[2,32,128]{2,1,0:T(8,128)S(1)}, f32[2,32,128]{2,1,0:T(8,128)}, u32[]{:S(2)}) copy-start(f32[2,32,128]{2,1,0:T(8,128)} %constant.14.clone.refs_5_) | copy-start | bytes 98308
  2.1 15.0 %copy-start.2 = (bf16[128,256]{1,0:T(8,128)(2,1)S(1)}, bf16[128,256]{1,0:T(8,128)(2,1)}, u32[]{:S(2)}) copy-start(bf16[128,256]{1,0:T(8,128)(2,1)} %constant.13.clone.refs_4_) | copy-start | bytes 196612
  2.1 15.0 %copy-start.3 = (bf16[128,256]{1,0:T(8,128)(2,1)S(1)}, bf16[128,256]{1,0:T(8,128)(2,1)}, u32[]{:S(2)}) copy-start(bf16[128,256]{1,0:T(8,128)(2,1)} %constant.12.clone.refs_3_) | copy-start | bytes 196612
  2.2 14.9 %copy-start.4 = (bf16[256,128]{1,0:T(8,128)(2,1)S(1)}, bf16[256,128]{1,0:T(8,128)(2,1)}, u32[]{:S(2)}) copy-start(bf16[256,128]{1,0:T(8,128)(2,1)} %constant.11.clone.refs_2_) | copy-start | bytes 196612
  2.2 14.9 %copy-start.5 = (bf16[256,128]{1,0:T(8,128)(2,1)S(1)}, bf16[256,128]{1,0:T(8,128)(2,1)}, u32[]{:S(2)}) copy-start(bf16[256,128]{1,0:T(8,128)(2,1)} %constant.10.clone.refs_1_) | copy-start | bytes 196612
  18.2 11.1 %copy-start = (bf16[10,3,32,128]{3,2,1,0:T(8,128)(2,1)S(1)}, bf16[10,3,32,128]{3,2,1,0:T(8,128)(2,1)}, u32[]{:S(2)}) copy-start(bf16[10,3,32,128]{3,2,1,0:T(8,128)(2,1)} %ensemble.5) | copy-start | bytes 737284
  29.4 6.9 %collective-permute-start = (bf16[144,128]{1,0:T(8,128)(2,1)S(1)}, bf16[144,128]{1,0:T(8,128)(2,1)S(1)}, u32[]{:S(2)}, u32[]{:S(2)}) collective-permute-start(bf16[144,128]{1,0:T(8,128)(2,1)S(1)} %shard_map.196.own), channel_id=1, source_target_pairs={{0,128},{32,160},{64,192},{96,224},{128,0},{160,32},{192,64},{224,... | collective-permute-start | bytes 110600 | tf_op jit(solution)/shard_map/ppermute | solution.py:590
  58.4 11.1 %copy-start.1 = (f32[10,32,128]{2,1,0:T(8,128)S(1)}, f32[10,32,128]{2,1,0:T(8,128)}, u32[]{:S(2)}) copy-start(f32[10,32,128]{2,1,0:T(8,128)} %alpha.3) | copy-start | bytes 491524
  58.4 11.1 %copy-start.7 = (f32[3,4,128]{2,1,0:T(4,128)S(1)}, f32[3,4,128]{2,1,0:T(4,128)}, u32[]{:S(2)}) copy-start(f32[3,4,128]{2,1,0:T(4,128)} %std.3) | copy-start | bytes 18436
  58.4 11.1 %copy-start.8 = (f32[3,4,128]{2,1,0:T(4,128)S(1)}, f32[3,4,128]{2,1,0:T(4,128)}, u32[]{:S(2)}) copy-start(f32[3,4,128]{2,1,0:T(4,128)} %control.3) | copy-start | bytes 18436
